TPU v7x, 256 devices: a whole 4x4x8 slice. The times are simulated.
256 devices in a mesh: bin: 64 (over x, z_hi, y, core), dp: 4 (over z_lo).
Axes of the slice: x: 4, y: 4, z: 8 (z_hi: 2, z_lo: 4; z = z_hi * 4 + z_lo), core: 2. Of those that a mesh axis runs over, the one named last changes fastest.
Arguments:
- peak_bins: int32 [512, 128], P('dp'), may hold values from 0 to 196607
- peak_values: bfloat16 [512, 128], P('dp'), may hold values from 0.049804688 to 1
- enc_weight: bfloat16 [196608, 2048], P(('bin', 'dp')), may hold values from -0.5 to 0.5
- enc_bias: float32 [2048], replicated, may hold values from -3 to 3
- dec_weight: bfloat16 [2048, 196608], P(None, ('bin', 'dp')), may hold values from -0.0007324219 to 0.0007324219
Outputs:
- grad_enc: bfloat16 [196608, 2048], P(('bin', 'dp'))
- grad_dec: bfloat16 [2048, 196608], P(None, ('bin', 'dp'))
All inputs are finite; a program needn't handle non-finite values.
Results may differ from a plain program's by a relative error of at most 0.0057.
Values may be sent and summed in bfloat16 or wider, within the bound.
No kernel may reach another device: no remote copies, remote signals or barrier semaphores. Data moves between devices by JAX's collectives and lax.ppermute only.
A program may use at most 64 MiB of HBM per device.

v0:
```python
import jax
import jax.numpy as jnp
from jax import lax
from jax.sharding import PartitionSpec as P


def activation(values):
    return jax.nn.gelu(values, approximate=True)


def slope_times(pre, back):
    _, pullback = jax.vjp(activation, pre)
    return pullback(back)[0].astype(jnp.bfloat16)


def on_device(peak_bins, peak_values, enc_weight, enc_bias, dec_weight):
    bins_dev = enc_weight.shape[0]
    first_bin = (lax.axis_index("bin") * lax.axis_size("dp") + lax.axis_index("dp")) * bins_dev
    all_bins = lax.all_gather(peak_bins, "dp", axis=0, tiled=True)
    all_values = lax.all_gather(peak_values, "dp", axis=0, tiled=True)
    total_rows = all_bins.shape[0]
    local_bins = all_bins - first_bin
    inside = (local_bins >= 0) & (local_bins < bins_dev)
    row_ids = jnp.broadcast_to(jnp.arange(total_rows, dtype=jnp.int32)[:, None], all_bins.shape)
    dense = (
        jnp.zeros((total_rows, bins_dev), jnp.float32)
        .at[row_ids, jnp.where(inside, local_bins, 0)]
        .add(jnp.where(inside, all_values.astype(jnp.float32), 0.0))
        .astype(jnp.bfloat16)
    )
    partial_pre = jnp.dot(dense, enc_weight, preferred_element_type=jnp.float32)
    own_pre = (
        lax.psum(lax.psum_scatter(partial_pre, "dp", scatter_dimension=0, tiled=True), "bin")
        + enc_bias
    )
    hidden = lax.all_gather(activation(own_pre).astype(jnp.bfloat16), "dp", axis=0, tiled=True)
    recon = jnp.dot(hidden, dec_weight, preferred_element_type=jnp.float32)
    resid = (recon - dense.astype(jnp.float32)).astype(jnp.bfloat16)
    grad_dec = lax.dot_general(
        hidden, resid, (((0,), (0,)), ((), ())), preferred_element_type=jnp.float32
    ).astype(jnp.bfloat16)
    partial_back = lax.dot_general(
        resid, dec_weight, (((1,), (1,)), ((), ())), preferred_element_type=jnp.float32
    )
    own_back = lax.psum(
        lax.psum_scatter(partial_back, "dp", scatter_dimension=0, tiled=True), "bin"
    )
    dpre = lax.all_gather(slope_times(own_pre, own_back), "dp", axis=0, tiled=True)
    grad_enc = lax.dot_general(
        dense, dpre, (((0,), (0,)), ((), ())), preferred_element_type=jnp.float32
    ).astype(jnp.bfloat16)
    return (grad_enc, grad_dec)


def solution(mesh):
    placed = (P("dp", None), P("dp", None), P(("bin", "dp"), None), P(), P(None, ("bin", "dp")))
    return jax.shard_map(
        on_device,
        mesh=mesh,
        in_specs=placed,
        out_specs=(P(("bin", "dp"), None), P(None, ("bin", "dp"))),
        check_vma=False,
    )
```

profile of v0, /device:TPU:1, one launch (start us, length us, event | category | flops | bytes accessed | tf_op | source)
XLA Modules:
  0.0 2368.2 jit_solution(12340559209032257120)
XLA Ops:
  7.2 0.0 copy-start
  7.2 0.0 copy-start.3
  7.2 0.0 reduce-scatter.3.cloned.1.call-start
  7.2 13.3 all_gather.13
  20.5 11.3 all_gather.12
  31.8 0.1 fusion.12
  31.9 0.8 select_bitcast_fusion.1
  32.7 0.8 and_reduce_fusion
  33.5 0.0 copy-done.3
  33.5 0.1 multiply_reduce_fusion
  33.7 452.9 %scatter_custom_fusion = f32[393216]{0:T(1024)} fusion(s32[65536]{0:T(1024)S(1)} %select_bitcast_fusion, f32[65536]{0:T(1024)} %select_bitcast_fusion.1, f32[]{:T(128)} %constant.13.clone.1), kind=kCustom, calls=%fused_computation.17 | custom fusion | flops 65536 | bytes 1573376
  486.6 2.4 convert_element_type.32
  488.9 2.5 reshape.21
  491.4 5.9 fusion.13
  497.3 0.0 copy-start.2
  497.3 0.0 reduce-scatter.3.cloned.1.call-update
  497.3 0.0 all-reduce.3.cloned.1.call-start
  497.4 88.7 %reduce-scatter.3.cloned.1.call-done = f32[128,2048]{1,0:T(8,128)} async-done(((f32[512,2048]{1,0:T(8,128)}), f32[128,2048]{1,0:T(8,128)}) %reduce-scatter.3.cloned.1.call-update) | async-done | bytes 1048592 | tf_op jit(solution)/shard_map/reduce_scatter | solution.py:33
  586.1 0.0 all-reduce.3.cloned.1.call-update
  586.1 0.0 all-gather.3.cloned.1.call-start
  586.2 786.4 %all-reduce.3.cloned.1.call-done = f32[128,2048]{1,0:T(8,128)} async-done(((f32[128,2048]{1,0:T(8,128)}), f32[128,2048]{1,0:T(8,128)}) %all-reduce.3.cloned.1.call-update) | async-done | bytes 1048592 | tf_op jit(solution)/shard_map/psum | solution.py:33
  1372.6 0.0 copy-done.2
  1372.6 2.4 multiply_convert_fusion
  1375.0 0.0 all-gather.3.cloned.1.call-update
  1375.0 0.0 reduce-scatter.5.cloned.1.call-start
  1375.0 50.6 %all-gather.3.cloned.1.call-done = bf16[512,2048]{1,0:T(8,128)(2,1)} async-done(((bf16[128,2048]{1,0:T(8,128)(2,1)}), bf16[512,2048]{1,0:T(8,128)(2,1)}) %all-gather.3.cloned.1.call-update) | async-done | bytes 2097168 | tf_op jit(solution)/shard_map/all_gather | solution.py:36
  1425.7 0.0 copy-done
  1425.7 0.0 copy-start.1
  1425.7 3.5 fusion.14
  1429.1 0.0 copy-start.4
  1429.2 1.1 copy-done.4
  1430.3 0.0 copy-done.1
  1430.3 3.8 fusion
  1434.1 0.0 reduce-scatter.5.cloned.1.call-update
  1434.1 0.0 all-reduce.5.cloned.1.call-start
  1434.1 81.5 %reduce-scatter.5.cloned.1.call-done = f32[128,2048]{1,0:T(8,128)} async-done(((f32[512,2048]{1,0:T(8,128)}), f32[128,2048]{1,0:T(8,128)}) %reduce-scatter.5.cloned.1.call-update) | async-done | bytes 1048592 | tf_op jit(solution)/shard_map/reduce_scatter | solution.py:46
  1515.6 0.0 all-reduce.5.cloned.1.call-update
  1515.6 0.2 all-gather.5.cloned.1.call-start
  1515.9 786.4 %all-reduce.5.cloned.1.call-done = f32[128,2048]{1,0:T(8,128)} async-done(((f32[128,2048]{1,0:T(8,128)}), f32[128,2048]{1,0:T(8,128)}) %all-reduce.5.cloned.1.call-update) | async-done | bytes 1048592 | tf_op jit(solution)/shard_map/psum | solution.py:45
  2302.3 3.1 fusion.9
  2305.3 0.0 all-gather.5.cloned.1.call-update
  2305.4 5.8 convolution_convert_fusion
  2311.1 44.9 %all-gather.5.cloned.1.call-done = bf16[512,2048]{1,0:T(8,128)(2,1)} async-done(((bf16[128,2048]{1,0:T(8,128)(2,1)}), bf16[512,2048]{1,0:T(8,128)(2,1)}) %all-gather.5.cloned.1.call-update) | async-done | bytes 2097168 | tf_op jit(solution)/shard_map/all_gather | solution.py:48
  2356.1 5.3 convolution_convert_fusion.1
  (2 shorter events, 0.0 us)
Async XLA Ops:
  7.2 1418.5 %copy-start = (bf16[2048,768]{1,0:T(8,128)(2,1)S(1)}, bf16[2048,768]{1,0:T(8,128)(2,1)}, u32[]{:S(2)}) copy-start(bf16[2048,768]{1,0:T(8,128)(2,1)} %param.9) | copy-start | bytes 9437188
  7.2 26.3 %copy-start.3 = (s32[2]{0:T(128)S(1)}, s32[2]{0:T(128)}, u32[]{:S(2)}) copy-start(s32[2]{0:T(128)} %constant.34) | copy-start | bytes 28
  7.2 578.9 %reduce-scatter.3.cloned.1.call-start = ((), (), s32[]{:S(2)}) async-start(), calls=%async_computation.2 | async-start | bytes 5242880 | tf_op jit(solution)/shard_map/reduce_scatter | solution.py:33
  497.3 875.3 %copy-start.2 = (f32[2048]{0:T(1024)S(1)}, f32[2048]{0:T(1024)}, u32[]{:S(2)}) copy-start(f32[2048]{0:T(1024)} %param.8) | copy-start | bytes 24580
  497.3 875.3 %all-reduce.3.cloned.1.call-start = ((), (), s32[]{:S(2)}) async-start(), calls=%async_computation.3 | async-start | bytes 2097152 | tf_op jit(solution)/shard_map/psum | solution.py:33
  586.1 839.6 %all-gather.3.cloned.1.call-start = ((), (), s32[]{:S(2)}) async-start(), calls=%async_computation.4 | async-start | bytes 2621440 | tf_op jit(solution)/shard_map/all_gather | solution.py:36
  1375.0 140.6 %reduce-scatter.5.cloned.1.call-start = ((), (), s32[]{:S(2)}) async-start(), calls=%async_computation.5 | async-start | bytes 5242880 | tf_op jit(solution)/shard_map/reduce_scatter | solution.py:46
  1425.7 4.6 copy-start.1
  1429.1 1.1 copy-start.4
  1434.1 868.2 %all-reduce.5.cloned.1.call-start = ((), (), s32[]{:S(2)}) async-start(), calls=%async_computation.6 | async-start | bytes 2097152 | tf_op jit(solution)/shard_map/psum | solution.py:45
  1515.6 840.4 %all-gather.5.cloned.1.call-start = ((), (), s32[]{:S(2)}) async-start(), calls=%async_computation.7 | async-start | bytes 2621440 | tf_op jit(solution)/shard_map/all_gather | solution.py:48
Sparse Core Ops, SparseCore 0:
  497.4 88.6 reduce-scatter.2
  588.9 783.6 all-reduce.2
  1375.1 50.5 all-gather.2
  1434.2 81.3 reduce-scatter.4
  1518.3 783.9 all-reduce.4
  2305.5 50.5 all-gather.4
where the time goes:
time: 2370 us
  waiting for transfers between devices  1840 us (78%)
  other arithmetic  462 us (19%)
  blocking collectives  24.6 us (1%)
  matrix products  24.2 us (1%)
    psum x1, waiting for transfers between devices, on_device(): lax.psum(lax.psum_scatter(partial_pre, 'dp', scatter_dimension=0, tiled=T...  786 us
    psum x1, waiting for transfers between devices, on_device(): lax.psum(lax.psum_scatter(partial_back, 'dp', scatter_dimension=0, tiled=...  786 us
    unnamed x4, other arithmetic  454 us
    reduce_scatter x1, waiting for transfers between devices, on_device(): lax.psum_scatter(partial_pre, 'dp', scatter_dimension=0, tiled=True)  88.7 us
    reduce_scatter x1, waiting for transfers between devices, on_device(): lax.psum_scatter(partial_back, 'dp', scatter_dimension=0, tiled=True)  81.5 us
    all_gather x1, waiting for transfers between devices, on_device(): lax.all_gather(activation(own_pre).astype(jnp.bfloat16), 'dp', axis=0, ti...  50.6 us
  transfers between devices with their start and end apart: 6, of which 6 were waited for; matrix products, arithmetic and copies ran while one was open for 0% of the time, Pallas kernels for 0%

commit v1 on v0

v1 whole, which is shorter than its diff:
```python
import functools

import jax
import jax.numpy as jnp
from jax import lax
from jax.experimental import pallas as pl
from jax.experimental.pallas import tpu as pltpu
from jax.sharding import Mesh
from jax.sharding import PartitionSpec as P

SHAPE = (4, 2, 4, 2, 4)
NAMES = ("x", "zhi", "y", "core", "zlo")
PLANE = ("x", "y")
DEPTH = ("zhi", "zlo")
LANES = 128
BF16 = jnp.bfloat16
F32 = jnp.float32


def activation(values):
    return jax.nn.gelu(values, approximate=True)


def slope_times(pre, back):
    _, pullback = jax.vjp(activation, pre)
    return pullback(back)[0].astype(BF16)


def dense_kernel(place_ref, peaks_ref, out_ref, *, peaks):
    rows, width = out_ref.shape
    tiles = width // LANES
    first, shift = place_ref[0], place_ref[1]
    lane = lax.broadcasted_iota(jnp.int32, (LANES, 1), 0).astype(BF16)
    sub = lax.broadcasted_iota(jnp.int32, (8, 1), 0)

    def step(group, carry):
        row = pl.multiple_of(group * 16, 16)
        source = pl.multiple_of(lax.rem(row + shift, rows), 16)
        local = peaks_ref[pl.ds(source, 16), :peaks].astype(jnp.int32) - first
        values = peaks_ref[pl.ds(source, 16), peaks:]
        high = local >> 7
        low = (local & (LANES - 1)).astype(BF16)
        halves = []
        for half in (0, 8):
            picked = [
                jnp.where(high[half : half + 8] == tile, values[half : half + 8], 0.0)
                for tile in range(tiles)
            ]
            total = None
            for pair in range(0, 8, 2):
                left = jnp.concatenate(
                    [
                        jnp.concatenate([jnp.where(sub == s, one, 0.0) for one in picked], axis=0)
                        for s in (pair, pair + 1)
                    ],
                    axis=1,
                ).astype(BF16)
                right = jnp.concatenate(
                    [
                        jnp.where(low[half + s][None, :] == lane, 1.0, 0.0).astype(BF16)
                        for s in (pair, pair + 1)
                    ],
                    axis=1,
                )
                term = lax.dot_general(
                    left, right, (((1,), (1,)), ((), ())), preferred_element_type=F32
                )
                total = term if total is None else total + term
            halves.append(total)
        for tile in range(tiles):
            block = jnp.concatenate(
                [total[tile * 8 : tile * 8 + 8] for total in halves], axis=0
            )
            out_ref[pl.ds(row, 16), tile * LANES : (tile + 1) * LANES] = block.astype(BF16)
        return carry

    lax.fori_loop(0, rows // 16, step, 0, unroll=4)


def build_dense(place, packed, width):
    rows, lanes = packed.shape
    return pl.pallas_call(
        functools.partial(dense_kernel, peaks=lanes // 2),
        out_shape=jax.ShapeDtypeStruct((rows, width), BF16),
        in_specs=[
            pl.BlockSpec(memory_space=pltpu.SMEM),
            pl.BlockSpec(memory_space=pltpu.VMEM),
        ],
        out_specs=pl.BlockSpec(memory_space=pltpu.VMEM),
        compiler_params=pltpu.CompilerParams(vmem_limit_bytes=32 << 20),
        name="build_dense",
    )(place, packed)


def swap(values):
    return lax.ppermute(values, "core", [(0, 1), (1, 0)])


def exchange(values, axes):
    return lax.all_to_all(values, axes, 0, 0, tiled=True)


def gather(values, axes):
    count = lax.axis_size(axes)
    sent = jnp.broadcast_to(values[None], (count,) + values.shape)
    return exchange(sent, axes).reshape(-1, values.shape[-1])


def scatter_sum(own, other):
    hidden = own.shape[1]
    half = own + swap(other.astype(BF16)).astype(F32)
    plane = exchange(half.astype(BF16).reshape(16, -1, hidden), PLANE).astype(F32).sum(0)
    depth = exchange(plane.reshape(8, -1, hidden), DEPTH)
    return depth.sum(0)


def gather_rows(values):
    own = gather(gather(values, DEPTH), PLANE)
    return own, swap(own)


def on_device(peak_bins, peak_values, enc_weight, enc_bias, dec_weight):
    width = enc_weight.shape[0]
    position = lax.axis_index("x")
    for name in NAMES[1:]:
        position = position * lax.axis_size(name) + lax.axis_index(name)
    packed = gather(
        jnp.concatenate([peak_bins.astype(F32), peak_values.astype(F32)], axis=1), "zlo"
    )
    rows = packed.shape[0]
    part = rows // 2
    place = jnp.stack([position * width, lax.axis_index("core") * part]).astype(jnp.int32)
    dense = build_dense(place, packed, width)
    dense_own, dense_other = dense[:part], dense[part:]

    def encode(block):
        return jnp.dot(block, enc_weight, preferred_element_type=F32)

    def residual(block, hidden):
        recon = jnp.dot(hidden, dec_weight, preferred_element_type=F32)
        return (recon - block.astype(F32)).astype(BF16)

    def decode_back(resid):
        return lax.dot_general(
            resid, dec_weight, (((1,), (1,)), ((), ())), preferred_element_type=F32
        )

    def weight_grad(left, right):
        return lax.dot_general(
            left, right, (((0,), (0,)), ((), ())), preferred_element_type=F32
        ).astype(BF16)

    pre = scatter_sum(encode(dense_own), encode(dense_other)) + enc_bias
    hidden_own, hidden_other = gather_rows(activation(pre).astype(BF16))
    resid_own = residual(dense_own, hidden_own)
    resid_other = residual(dense_other, hidden_other)
    back = scatter_sum(decode_back(resid_own), decode_back(resid_other))
    grad_dec = weight_grad(
        jnp.concatenate([hidden_own, hidden_other]), jnp.concatenate([resid_own, resid_other])
    )
    dpre = jnp.concatenate(gather_rows(slope_times(pre, back)))
    grad_enc = weight_grad(dense, dpre)
    return (grad_enc, grad_dec)


def solution(mesh):
    fine = Mesh(mesh.devices.reshape(SHAPE), NAMES)
    bins = ("x", "zhi", "y", "core", "zlo")
    placed = (P("zlo", None), P("zlo", None), P(bins, None), P(), P(None, bins))
    return jax.shard_map(
        on_device,
        mesh=fine,
        in_specs=placed,
        out_specs=(P(bins, None), P(None, bins)),
        check_vma=False,
    )
```

time: 2370 us -> 190 us (0.08)
  waiting for transfers between devices: 1840 us -> 19.9 us
  other arithmetic: 462 us -> 2.33 us
  blocking collectives: 24.6 us -> 117 us
    psum x2 -> x0, waiting for transfers between devices: 1570 us -> none  [the longest x1 786 us: on_device(): lax.psum(lax.psum_scatter(partial_pre, 'dp', scatter_dimension=0, tiled=T...]
    unnamed x4 -> x0, other arithmetic: 454 us -> none
    reduce_scatter x2 -> x0, waiting for transfers between devices: 170 us -> none  [the longest x1 88.7 us: on_device(): lax.psum_scatter(partial_pre, 'dp', scatter_dimension=0, tiled=True)]
    all_to_all x0 -> x8, blocking collectives: none -> 117 us  [exchange(): return lax.all_to_all(values, axes, 0, 0, tiled=True)]
    all_gather x2 -> x0, waiting for transfers between devices: 95.6 us -> none  [the longest x1 50.6 us: on_device(): lax.all_gather(activation(own_pre).astype(jnp.bfloat16), 'dp', axis=0, ti...]
    all_gather x2 -> x0, blocking collectives: 24.6 us -> none  [the longest x1 13.3 us: on_device(): all_values = lax.all_gather(peak_values, 'dp', axis=0, tiled=True)]
  transfers between devices with their start and end apart: 6 -> 5, of which waited for: 6 -> 4; matrix products, arithmetic and copies ran while one was open for 0% -> 2% of each run, Pallas kernels for 0% -> 0%
where the time goes in v1:
time: 190 us; the launch traced here: 189 us
  blocking collectives  117 us (62%)
  starting transfers between devices  20 us (11%)
  waiting for transfers between devices  19.9 us (10%)
  matrix products  15.2 us (8%)
  Pallas kernels  10.3 us (5%)
  local copies, waits for them, and re-layouts  3.13 us (2%)
  other arithmetic  2.33 us (1%)
    all_to_all x8, blocking collectives, exchange(): return lax.all_to_all(values, axes, 0, 0, tiled=True)  117 us
    all_to_all x1, waiting for transfers between devices, exchange(): return lax.all_to_all(values, axes, 0, 0, tiled=True)  14 us
    ppermute x4, starting transfers between devices, swap(): return lax.ppermute(values, 'core', [(0, 1), (1, 0)])  13.6 us
    pallas_call x1, Pallas kernels, build_dense(): pl.pallas_call(functools.partial(dense_kernel, peaks=lanes // 2), out_sha...  10.3 us
    dot_general x2, matrix products, weight_grad(): lax.dot_general(left, right, (((0,), (0,)), ((), ())), preferred_element_...  7 us
    all_to_all x1, starting transfers between devices, exchange(): return lax.all_to_all(values, axes, 0, 0, tiled=True)  6.44 us
    ppermute x4, waiting for transfers between devices, swap(): return lax.ppermute(values, 'core', [(0, 1), (1, 0)])  5.84 us
    dot_general x2, matrix products, encode(): return jnp.dot(block, enc_weight, preferred_element_type=F32)  4.16 us
  transfers between devices with their start and end apart: 5, of which 4 were waited for; matrix products, arithmetic and copies ran while one was open for 2% of the time, Pallas kernels for 0%

profile of v1, /device:TPU:1, one launch (start us, length us, event | category | flops | bytes accessed | tf_op | source)
XLA Modules:
  0.0 189.1 jit_solution(2333315787322889383)
XLA Ops:
  0.6 0.0 copy-start
  0.6 1.0 convert_element_type.62
  1.6 0.8 convert_element_type.63
  2.4 0.8 broadcast_in_dim.14
  3.3 6.4 %all-to-all-start = ((f32[4,128,256]{2,1,0:T(8,128)}), f32[4,128,256]{2,1,0:T(8,128)}, u32[]{:S(2)}, u32[]{:S(2)}) async-start(f32[4,128,256]{2,1,0:T(8,128)} %broadcast_in_dim.14), calls=%async_computation | async-start | bytes 1048576 | tf_op jit(solution)/shard_map/all_to_all | solution.py:100
  9.7 0.1 pad_add_fusion.place_ref
  9.8 14.0 %all-to-all-done = f32[4,128,256]{2,1,0:T(8,128)} async-done(((f32[4,128,256]{2,1,0:T(8,128)}), f32[4,128,256]{2,1,0:T(8,128)}, u32[]{:S(2)}, u32[]{:S(2)}) %all-to-all-start) | async-done | bytes 524320 | tf_op jit(solution)/shard_map/all_to_all | solution.py:100
  23.8 10.3 %build_dense.1 = bf16[512,768]{1,0:T(8,128)(2,1)S(1)} custom-call(s32[2]{0:T(128)S(1)} %pad_add_fusion.place_ref, f32[512,256]{1,0:T(8,128)} %bitcast.2.peaks_ref), custom_call_target="tpu_custom_call" | custom-call | tf_op jit(solution)/shard_map/build_dense/pallas_call | solution.py:82
  34.1 0.0 copy-start.1
  34.1 3.2 %convolution_convert_fusion.3 = bf16[256,2048]{1,0:T(8,128)(2,1)S(1)} fusion(bf16[768,2048]{1,0:T(8,128)(2,1)} %param.7, bf16[512,768]{1,0:T(8,128)(2,1)S(1)} %build_dense.1), kind=kOutput, calls=%fused_computation.3 | convolution fusion | flops 805830656 | bytes 4587520 | tf_op jit(solution)/shard_map/dot_general | solution.py:137
  37.3 1.5 collective-permute-start
  38.8 2.3 %collective-permute-done = bf16[256,2048]{1,0:T(8,128)(2,1)S(1)} collective-permute-done((bf16[256,2048]{1,0:T(8,128)(2,1)S(1)}, bf16[256,2048]{1,0:T(8,128)(2,1)S(1)}, u32[]{:S(2)}, u32[]{:S(2)}) %collective-permute-start) | collective-permute-done | bytes 1048608 | tf_op jit(solution)/shard_map/ppermute | solution.py:96
  41.1 0.0 copy-done.7
  41.1 1.0 add_convert_fusion.1
  42.1 0.0 copy-start.6
  42.1 22.5 %all_to_all.45 = bf16[16,16,2048]{2,1,0:T(8,128)(2,1)S(1)} all-to-all(bf16[16,16,2048]{2,1,0:T(8,128)(2,1)S(1)} %bitcast.23), channel_id=1, replica_groups=mesh['x'=4,'zhi'=2,'y'=4,'core'=2,'zlo'=4] {'x','y'}, dimensions={0} | all-to-all | bytes 2097152 | tf_op jit(solution)/shard_map/all_to_all | solution.py:100
  64.7 0.1 convert_reduce_fusion.1
  64.8 0.1 reshape.88
  64.9 14.5 %all_to_all.46 = f32[8,2,2048]{2,1,0:T(2,128)S(1)} all-to-all(f32[8,2,2048]{2,1,0:T(2,128)S(1)} %reshape.88), channel_id=1, replica_groups=mesh['x'=4,'zhi'=2,'y'=4,'core'=2,'zlo'=4] {'zhi','zlo'}, dimensions={0} | all-to-all | bytes 262144 | tf_op jit(solution)/shard_map/all_to_all | solution.py:100
  79.6 9.6 %all_to_all.47 = bf16[8,2,2048]{2,1,0:T(2,128)(2,1)S(1)} all-to-all(bf16[8,2,2048]{2,1,0:T(2,128)(2,1)S(1)} %broadcast_in_dim.15), channel_id=1, replica_groups=mesh['x'=4,'zhi'=2,'y'=4,'core'=2,'zlo'=4] {'zhi','zlo'}, dimensions={0} | all-to-all | bytes 131072 | tf_op jit(solution)/shard_map/all_to_all | solution.py:100
  89.2 0.1 broadcast_in_dim.17
  89.3 15.2 %all_to_all.48 = bf16[16,16,2048]{2,1,0:T(8,128)(2,1)S(1)} all-to-all(bf16[16,16,2048]{2,1,0:T(8,128)(2,1)S(1)} %broadcast_in_dim.17), channel_id=1, replica_groups=mesh['x'=4,'zhi'=2,'y'=4,'core'=2,'zlo'=4] {'x','y'}, dimensions={0} | all-to-all | bytes 2097152 | tf_op jit(solution)/shard_map/all_to_all | solution.py:100
  104.6 6.4 %collective-permute-start.1 = (bf16[256,2048]{1,0:T(8,128)(2,1)S(1)}, bf16[256,2048]{1,0:T(8,128)(2,1)S(1)}, u32[]{:S(2)}, u32[]{:S(2)}) collective-permute-start(bf16[256,2048]{1,0:T(8,128)(2,1)S(1)} %bitcast.18), channel_id=1, source_target_pairs={{0,4},{4,0},{1,5},{5,1},{2,6},{6,2},{3,7},{7,3},{8,12},{12,8},{9,1... | collective-permute-start | bytes 3145736 | tf_op jit(solution)/shard_map/ppermute | solution.py:96
  110.9 2.3 %collective-permute-done.1 = bf16[256,2048]{1,0:T(8,128)(2,1)S(1)} collective-permute-done((bf16[256,2048]{1,0:T(8,128)(2,1)S(1)}, bf16[256,2048]{1,0:T(8,128)(2,1)S(1)}, u32[]{:S(2)}, u32[]{:S(2)}) %collective-permute-start.1) | collective-permute-done | bytes 1048608 | tf_op jit(solution)/shard_map/ppermute | solution.py:96
  113.2 1.0 copy-done.8
  114.2 1.0 fusion.7
  115.2 0.8 copy-done.12
  116.0 1.0 convolution_convert_fusion.2
  117.0 0.5 collective-permute-start.2
  117.5 1.0 fusion.6
  118.5 1.3 collective-permute-done.2
  119.7 1.0 add_convert_fusion
  120.8 18.9 %all_to_all.49 = bf16[16,16,2048]{2,1,0:T(8,128)(2,1)S(1)} all-to-all(bf16[16,16,2048]{2,1,0:T(8,128)(2,1)S(1)} %bitcast.24), channel_id=1, replica_groups=mesh['x'=4,'zhi'=2,'y'=4,'core'=2,'zlo'=4] {'x','y'}, dimensions={0} | all-to-all | bytes 2097152 | tf_op jit(solution)/shard_map/all_to_all | solution.py:100
  139.7 0.1 convert_reduce_fusion
  139.9 0.1 reshape.91
  140.0 10.4 %all_to_all.50 = f32[8,2,2048]{2,1,0:T(2,128)S(1)} all-to-all(f32[8,2,2048]{2,1,0:T(2,128)S(1)} %reshape.91), channel_id=1, replica_groups=mesh['x'=4,'zhi'=2,'y'=4,'core'=2,'zlo'=4] {'zhi','zlo'}, dimensions={0} | all-to-all | bytes 262144 | tf_op jit(solution)/shard_map/all_to_all | solution.py:100
  150.4 0.1 fusion.22
  150.5 9.6 %all_to_all.51 = bf16[8,2,2048]{2,1,0:T(2,128)(2,1)S(1)} all-to-all(bf16[8,2,2048]{2,1,0:T(2,128)(2,1)S(1)} %broadcast_in_dim.18), channel_id=1, replica_groups=mesh['x'=4,'zhi'=2,'y'=4,'core'=2,'zlo'=4] {'zhi','zlo'}, dimensions={0} | all-to-all | bytes 131072 | tf_op jit(solution)/shard_map/all_to_all | solution.py:100
  160.2 0.0 copy-start.5
  160.2 0.0 copy-start.9
  160.2 0.0 copy-start.11
  160.2 0.0 copy-start.13
  160.2 0.1 broadcast_in_dim.39
  160.3 16.5 %all_to_all.52 = bf16[16,16,2048]{2,1,0:T(8,128)(2,1)S(1)} all-to-all(bf16[16,16,2048]{2,1,0:T(8,128)(2,1)S(1)} %broadcast_in_dim.39), channel_id=1, replica_groups=mesh['x'=4,'zhi'=2,'y'=4,'core'=2,'zlo'=4] {'x','y'}, dimensions={0} | all-to-all | bytes 2097152 | tf_op jit(solution)/shard_map/all_to_all | solution.py:100
  176.9 5.2 %collective-permute-start.3 = (bf16[256,2048]{1,0:T(8,128)(2,1)S(1)}, bf16[256,2048]{1,0:T(8,128)(2,1)S(1)}, u32[]{:S(2)}, u32[]{:S(2)}) collective-permute-start(bf16[256,2048]{1,0:T(8,128)(2,1)S(1)} %bitcast.21), channel_id=1, source_target_pairs={{0,4},{4,0},{1,5},{5,1},{2,6},{6,2},{3,7},{7,3},{8,12},{12,8},{9,1... | collective-permute-start | bytes 3145736 | tf_op jit(solution)/shard_map/ppermute | solution.py:96
  182.1 3.5 %convolution_convert_fusion = bf16[2048,768]{1,0:T(8,128)(2,1)} fusion(bf16[256,2048]{1,0:T(8,128)(2,1)S(1)} %copy-done.9, bf16[256,2048]{1,0:T(8,128)(2,1)S(1)} %bitcast.20, bf16[256,768]{1,0:T(8,128)(2,1)S(1)} %copy-done.13, bf16[256,768]{1,0:T(8,128)(2,1)S(1)} %copy-done.11), kind=kOutput, calls=%fused_computation | convolution fusion | flops 1617952768 | bytes 6029312 | tf_op jit(solution)/shard_map/dot_general | solution.py:149
  185.6 0.0 collective-permute-done.3
  185.6 3.5 %convolution_convert_fusion.1 = bf16[768,2048]{1,0:T(8,128)(2,1)} fusion(bf16[512,768]{1,0:T(8,128)(2,1)S(1)} %copy-done.3, bf16[256,2048]{1,0:T(8,128)(2,1)S(1)} %collective-permute-done.3, bf16[256,2048]{1,0:T(8,128)(2,1)S(1)} %bitcast.22), kind=kOutput, calls=%fused_computation.1 | convolution fusion | flops 1616379904 | bytes 6029312 | tf_op jit(solution)/shard_map/dot_general | solution.py:149
  (26 shorter events, 0.3 us)
Async XLA Ops:
  0.6 113.6 %copy-start = (bf16[2048,768]{1,0:T(8,128)(2,1)S(1)}, bf16[2048,768]{1,0:T(8,128)(2,1)}, u32[]{:S(2)}) copy-start(bf16[2048,768]{1,0:T(8,128)(2,1)} %param.9) | copy-start | bytes 9437188
  3.3 20.5 %all-to-all-start = ((f32[4,128,256]{2,1,0:T(8,128)}), f32[4,128,256]{2,1,0:T(8,128)}, u32[]{:S(2)}, u32[]{:S(2)}) async-start(f32[4,128,256]{2,1,0:T(8,128)} %broadcast_in_dim.14), calls=%async_computation | async-start | bytes 1048576 | tf_op jit(solution)/shard_map/all_to_all | solution.py:100
  23.8 17.3 %copy-start.7 = (bf16[768,2048]{1,0:T(8,128)(2,1)S(1)}, bf16[768,2048]{1,0:T(8,128)(2,1)}, u32[]{:S(2)}) copy-start(bf16[768,2048]{1,0:T(8,128)(2,1)} %param.7) | copy-start | bytes 9437188
  34.1 8.0 %copy-start.1 = (bf16[512,768]{1,0:T(8,128)(2,1)}, bf16[512,768]{1,0:T(8,128)(2,1)S(1)}, u32[]{:S(2)}) copy-start(bf16[512,768]{1,0:T(8,128)(2,1)S(1)} %build_dense.1) | copy-start | bytes 2359300
  37.3 3.8 %collective-permute-start = (bf16[256,2048]{1,0:T(8,128)(2,1)S(1)}, bf16[256,2048]{1,0:T(8,128)(2,1)S(1)}, u32[]{:S(2)}, u32[]{:S(2)}) collective-permute-start(bf16[256,2048]{1,0:T(8,128)(2,1)S(1)} %convolution_convert_fusion.3), channel_id=1, source_target_pairs={{0,4},{4,0},{1,5},{5,1},{2,6},{6,2},{3,7},{7,3},{8,12},{12,8},{9,1... | collective-permute-start | bytes 3145736 | tf_op jit(solution)/shard_map/ppermute | solution.py:96
  42.1 37.3 %copy-start.6 = (f32[2048]{0:T(1024)S(1)}, f32[2048]{0:T(1024)}, u32[]{:S(2)}) copy-start(f32[2048]{0:T(1024)} %param.8) | copy-start | bytes 24580
  89.2 25.0 %copy-start.2 = (bf16[512,768]{1,0:T(8,128)(2,1)S(1)}, bf16[512,768]{1,0:T(8,128)(2,1)}, u32[]{:S(2)}) copy-start(bf16[512,768]{1,0:T(8,128)(2,1)} %copy-done.1) | copy-start | bytes 2359300
  104.6 12.9 %copy-start.4 = (bf16[16,16,2048]{2,1,0:T(8,128)(2,1)}, bf16[16,16,2048]{2,1,0:T(8,128)(2,1)S(1)}, u32[]{:S(2)}) copy-start(bf16[16,16,2048]{2,1,0:T(8,128)(2,1)S(1)} %all_to_all.48) | copy-start | bytes 3145732
  104.6 8.7 %collective-permute-start.1 = (bf16[256,2048]{1,0:T(8,128)(2,1)S(1)}, bf16[256,2048]{1,0:T(8,128)(2,1)S(1)}, u32[]{:S(2)}, u32[]{:S(2)}) collective-permute-start(bf16[256,2048]{1,0:T(8,128)(2,1)S(1)} %bitcast.18), channel_id=1, source_target_pairs={{0,4},{4,0},{1,5},{5,1},{2,6},{6,2},{3,7},{7,3},{8,12},{12,8},{9,1... | collective-permute-start | bytes 3145736 | tf_op jit(solution)/shard_map/ppermute | solution.py:96
  113.2 1.0 copy-start.8
  115.2 0.8 copy-start.12
  117.0 2.7 %collective-permute-start.2 = (bf16[256,2048]{1,0:T(8,128)(2,1)S(1)}, bf16[256,2048]{1,0:T(8,128)(2,1)S(1)}, u32[]{:S(2)}, u32[]{:S(2)}) collective-permute-start(bf16[256,2048]{1,0:T(8,128)(2,1)S(1)} %convolution_convert_fusion.2), channel_id=1, source_target_pairs={{0,4},{4,0},{1,5},{5,1},{2,6},{6,2},{3,7},{7,3},{8,12},{12,8},{9,1... | collective-permute-start | bytes 3145736 | tf_op jit(solution)/shard_map/ppermute | solution.py:96
  118.5 21.3 %copy-start.10 = (bf16[256,768]{1,0:T(8,128)(2,1)}, bf16[256,768]{1,0:T(8,128)(2,1)S(1)}, u32[]{:S(2)}) copy-start(bf16[256,768]{1,0:T(8,128)(2,1)S(1)} %fusion.6) | copy-start | bytes 1179652
  160.2 21.9 %copy-start.5 = (bf16[16,16,2048]{2,1,0:T(8,128)(2,1)S(1)}, bf16[16,16,2048]{2,1,0:T(8,128)(2,1)}, u32[]{:S(2)}) copy-start(bf16[16,16,2048]{2,1,0:T(8,128)(2,1)} %copy-done.4) | copy-start | bytes 3145732
  160.2 21.9 %copy-start.9 = (bf16[256,2048]{1,0:T(8,128)(2,1)S(1)}, bf16[256,2048]{1,0:T(8,128)(2,1)}, u32[]{:S(2)}) copy-start(bf16[256,2048]{1,0:T(8,128)(2,1)} %copy-done.8) | copy-start | bytes 3145732
  160.2 21.9 %copy-start.11 = (bf16[256,768]{1,0:T(8,128)(2,1)S(1)}, bf16[256,768]{1,0:T(8,128)(2,1)}, u32[]{:S(2)}) copy-start(bf16[256,768]{1,0:T(8,128)(2,1)} %copy-done.10) | copy-start | bytes 1179652
  160.2 21.9 %copy-start.13 = (bf16[256,768]{1,0:T(8,128)(2,1)S(1)}, bf16[256,768]{1,0:T(8,128)(2,1)}, u32[]{:S(2)}) copy-start(bf16[256,768]{1,0:T(8,128)(2,1)} %copy-done.12) | copy-start | bytes 1179652
  176.9 8.7 %copy-start.3 = (bf16[512,768]{1,0:T(8,128)(2,1)S(1)}, bf16[512,768]{1,0:T(8,128)(2,1)}, u32[]{:S(2)}) copy-start(bf16[512,768]{1,0:T(8,128)(2,1)} %copy-done.1) | copy-start | bytes 2359300
  176.9 8.7 %collective-permute-start.3 = (bf16[256,2048]{1,0:T(8,128)(2,1)S(1)}, bf16[256,2048]{1,0:T(8,128)(2,1)S(1)}, u32[]{:S(2)}, u32[]{:S(2)}) collective-permute-start(bf16[256,2048]{1,0:T(8,128)(2,1)S(1)} %bitcast.21), channel_id=1, source_target_pairs={{0,4},{4,0},{1,5},{5,1},{2,6},{6,2},{3,7},{7,3},{8,12},{12,8},{9,1... | collective-permute-start | bytes 3145736 | tf_op jit(solution)/shard_map/ppermute | solution.py:96

commit v2 on v0

v2 whole, which is shorter than its diff:
```python
import functools

import jax
import jax.numpy as jnp
from jax import lax
from jax.experimental import pallas as pl
from jax.experimental.pallas import tpu as pltpu
from jax.sharding import Mesh
from jax.sharding import PartitionSpec as P

SHAPE = (4, 2, 4, 2, 2, 2)
NAMES = ("x", "zhi", "y", "core", "zp", "zq")
NEAR = ("x", "y", "zq")
FAR = ("zhi", "zp")
SPECTRA_AXES = ("zp", "zq")
LANES = 128
STEP = 512
BF16 = jnp.bfloat16
F32 = jnp.float32


def activation(values):
    return jax.nn.gelu(values, approximate=True)


def slope_times(pre, back):
    _, pullback = jax.vjp(activation, pre)
    return pullback(back)[0].astype(BF16)


def pack_kernel(core_ref, bins_ref, values_ref, out_ref):
    rows, lanes = out_ref.shape
    peaks = lanes // 3
    first = pl.multiple_of(core_ref[0] * rows, rows)
    bins = bins_ref[pl.ds(first, rows), :]
    out_ref[:, :peaks] = ((bins >> 9) - 192).astype(F32).astype(BF16)
    out_ref[:, peaks : 2 * peaks] = ((bins & (STEP - 1)) - 256).astype(F32).astype(BF16)
    out_ref[:, 2 * peaks :] = values_ref[pl.ds(first, rows), :]


def pack_peaks(core, bins, values):
    rows, peaks = bins.shape
    vmem = pl.BlockSpec(memory_space=pltpu.VMEM)
    return pl.pallas_call(
        pack_kernel,
        out_shape=jax.ShapeDtypeStruct((rows // 2, 3 * peaks), BF16),
        in_specs=[pl.BlockSpec(memory_space=pltpu.SMEM), vmem, vmem],
        out_specs=vmem,
        compiler_params=pltpu.CompilerParams(vmem_limit_bytes=4 << 20),
        name="pack_peaks",
    )(core, bins, values)


def dense_rows(bins, values, firsts, tiles, consts):
    lane, upper, which = consts
    low = (bins & (LANES - 1)).astype(BF16)
    twice = jnp.concatenate([values, values], axis=0).astype(BF16)
    picked = []
    for first in firsts:
        local = bins - first
        inside = (local >= 0) & (local < tiles * LANES)
        high = jnp.where(inside, local >> 7, -9).astype(F32)
        high = jnp.concatenate([high, high], axis=0).astype(BF16) - upper
        for tile in range(0, tiles, 2):
            picked.append(jnp.where(high == tile, twice, jnp.zeros_like(twice)))
    left = jnp.concatenate(
        [
            jnp.concatenate(
                [jnp.where(which == row, one, jnp.zeros_like(one)) for one in picked], axis=0
            )
            for row in range(8)
        ],
        axis=1,
    )
    ones = jnp.ones((LANES, LANES), BF16)
    right = jnp.concatenate(
        [jnp.where(low[row][None, :] == lane, ones, jnp.zeros_like(ones)) for row in range(8)],
        axis=1,
    )
    return lax.dot_general(left, right, (((1,), (1,)), ((), ())), preferred_element_type=F32)


def dense_kernel(place_ref, *refs, groups):
    packed_refs, (own_ref, other_ref) = refs[:groups], refs[groups:]
    peaks = packed_refs[0].shape[1] // 3
    rows = packed_refs[0].shape[0]
    tiles = own_ref.shape[1] // LANES
    firsts = (place_ref[0], place_ref[1])
    lane = lax.broadcasted_iota(jnp.int32, (LANES, 1), 0).astype(BF16)
    row16 = lax.broadcasted_iota(jnp.int32, (16, LANES), 0)
    consts = (lane, (row16 >= 8).astype(jnp.int32).astype(BF16), (row16 & 7).astype(BF16))
    for back, packed_ref in enumerate(packed_refs):
        base = lax.rem(place_ref[2] + groups - back, groups) * rows

        def step(group, carry, packed_ref=packed_ref, base=base):
            row = pl.multiple_of(group * 16, 16)
            block = packed_ref[pl.ds(row, 16), :].astype(F32)
            bins = (block[:, :peaks].astype(jnp.int32) + 192) * STEP
            bins = bins + block[:, peaks : 2 * peaks].astype(jnp.int32) + 256
            values = block[:, 2 * peaks :]
            sums = [
                dense_rows(bins[h : h + 8], values[h : h + 8], firsts, tiles, consts)
                for h in (0, 8)
            ]
            target = pl.multiple_of(base + row, 16)
            for ref, skip in ((own_ref, 0), (other_ref, tiles)):
                for tile in range(tiles):
                    at = (skip + tile) * 8
                    ref[pl.ds(target, 16), tile * LANES : (tile + 1) * LANES] = jnp.concatenate(
                        [one[at : at + 8] for one in sums], axis=0
                    ).astype(BF16)
            return carry

        lax.fori_loop(0, rows // 16, step, 0, unroll=True)


def build_dense(place, blocks, width):
    rows = blocks[0].shape[0] * len(blocks)
    vmem = pl.BlockSpec(memory_space=pltpu.VMEM)
    return pl.pallas_call(
        functools.partial(dense_kernel, groups=len(blocks)),
        out_shape=(jax.ShapeDtypeStruct((rows, width), BF16),) * 2,
        in_specs=[pl.BlockSpec(memory_space=pltpu.SMEM)] + [vmem] * len(blocks),
        out_specs=(vmem, vmem),
        compiler_params=pltpu.CompilerParams(vmem_limit_bytes=8 << 20),
        name="build_dense",
    )(place, *blocks)


def sum_kernel(parts_ref, out_ref):
    count, _, columns = parts_ref.shape
    block = 4 * LANES
    for first in range(0, columns, block):
        at = slice(first, first + block)
        total = parts_ref[0, :, at].astype(F32)
        for part in range(1, count):
            total = total + parts_ref[part, :, at].astype(F32)
        out_ref[:, at] = total.astype(out_ref.dtype)


def sum_parts(parts):
    vmem = pl.BlockSpec(memory_space=pltpu.VMEM)
    return pl.pallas_call(
        sum_kernel,
        out_shape=jax.ShapeDtypeStruct(parts.shape[1:], BF16),
        in_specs=[vmem],
        out_specs=vmem,
        compiler_params=pltpu.CompilerParams(vmem_limit_bytes=4 << 20),
        name="sum_parts",
    )(parts)


def swap(values):
    return lax.ppermute(values, "core", [(0, 1), (1, 0)])


def from_others(values, axes):
    count = lax.axis_size(axes)
    return [
        lax.ppermute(values, axes, [(i, (i + step) % count) for i in range(count)])
        for step in range(1, count)
    ]


def near_exchange(values):
    return lax.all_to_all(values, NEAR, 0, 0, tiled=True)


def far_sum(sent):
    one, two, three = [block.astype(F32) for block in from_others(sent, FAR)]
    return (sent.astype(F32) + two) + (one + three)


def near_gather(values):
    count = lax.axis_size(NEAR)
    sent = jnp.broadcast_to(values[None], (count,) + values.shape)
    return near_exchange(sent).reshape(-1, values.shape[-1])


def on_device(peak_bins, peak_values, enc_weight, enc_bias, dec_weight):
    width, hidden_size = enc_weight.shape
    core = lax.axis_index("core")
    group = lax.axis_index(SPECTRA_AXES)
    position = lax.axis_index(NAMES)
    stride = lax.axis_size(SPECTRA_AXES)
    partner = position + (1 - 2 * core) * stride
    place = jnp.stack([position * width, partner * width, group]).astype(jnp.int32)
    packed = pack_peaks(core.reshape(1), peak_bins, peak_values)
    dense_own, dense_sent = build_dense(
        place, [packed] + from_others(packed, SPECTRA_AXES), width
    )
    dense_other = swap(dense_sent)

    def encode(block):
        return jnp.dot(block, enc_weight, preferred_element_type=F32)

    def residual(block, hidden):
        recon = jnp.dot(hidden, dec_weight, preferred_element_type=F32)
        return (recon - block.astype(F32)).astype(BF16)

    def decode_back(resid):
        return lax.dot_general(
            resid, dec_weight, (((1,), (1,)), ((), ())), preferred_element_type=F32
        )

    def rows_dot(left, right):
        return lax.dot_general(
            left, right, (((0,), (0,)), ((), ())), preferred_element_type=F32
        )

    def near_parts(own, other):
        half = own + swap(other.astype(BF16)).astype(F32)
        return near_exchange(half.astype(BF16).reshape(lax.axis_size(NEAR), -1, hidden_size))

    parts = near_parts(encode(dense_own), encode(dense_other))
    pre = far_sum(sum_parts(parts)) + enc_bias
    hidden_own = near_gather(activation(pre).astype(BF16))
    hidden_other = swap(hidden_own)
    resid_own = residual(dense_own, hidden_own)
    resid_other = residual(dense_other, hidden_other)
    parts = near_parts(decode_back(resid_own), decode_back(resid_other))
    grad_dec = rows_dot(
        jnp.concatenate([hidden_own, hidden_other]), jnp.concatenate([resid_own, resid_other])
    ).astype(BF16)
    parts, grad_dec = lax.optimization_barrier((parts, grad_dec))
    back = far_sum(sum_parts(parts))
    dpre_own = near_gather(slope_times(pre, back))
    dpre_other = swap(dpre_own)
    grad_enc = (rows_dot(dense_own, dpre_own) + rows_dot(dense_other, dpre_other)).astype(BF16)
    return (grad_enc, grad_dec)


def solution(mesh):
    fine = Mesh(mesh.devices.reshape(SHAPE), NAMES)
    placed = (
        P(SPECTRA_AXES, None),
        P(SPECTRA_AXES, None),
        P(NAMES, None),
        P(),
        P(None, NAMES),
    )
    return jax.shard_map(
        on_device,
        mesh=fine,
        in_specs=placed,
        out_specs=(P(NAMES, None), P(None, NAMES)),
        check_vma=False,
    )
```

time: 2370 us -> 161 us (0.07)
  waiting for transfers between devices: 1840 us -> 33.8 us
  other arithmetic: 462 us -> 1.02 us
  blocking collectives: 24.6 us -> 61.8 us
  starting transfers between devices: 0.42 us -> 31 us
    psum x2 -> x0, waiting for transfers between devices: 1570 us -> none  [the longest x1 786 us: on_device(): lax.psum(lax.psum_scatter(partial_pre, 'dp', scatter_dimension=0, tiled=T...]
    unnamed x4 -> x0, other arithmetic: 454 us -> none
    reduce_scatter x2 -> x0, waiting for transfers between devices: 170 us -> none  [the longest x1 88.7 us: on_device(): lax.psum_scatter(partial_pre, 'dp', scatter_dimension=0, tiled=True)]
    all_gather x2 -> x0, waiting for transfers between devices: 95.6 us -> none  [the longest x1 50.6 us: on_device(): lax.all_gather(activation(own_pre).astype(jnp.bfloat16), 'dp', axis=0, ti...]
    all_to_all x0 -> x3, blocking collectives: none -> 61.8 us  [near_exchange(): return lax.all_to_all(values, NEAR, 0, 0, tiled=True)]
    ppermute x0 -> x14, starting transfers between devices: none -> 26.4 us  [the longest x9 18.3 us: from_others(): lax.ppermute(values, axes, [(i, (i + step) % count) for i in range(count)])]
    all_gather x2 -> x0, blocking collectives: 24.6 us -> none  [the longest x1 13.3 us: on_device(): all_values = lax.all_gather(peak_values, 'dp', axis=0, tiled=True)]
  transfers between devices with their start and end apart: 6 -> 15, of which waited for: 6 -> 12; matrix products, arithmetic and copies ran while one was open for 0% -> 4% of each run, Pallas kernels for 0% -> 0%
where the time goes in v2:
time: 161 us
  blocking collectives  61.8 us (38%)
  waiting for transfers between devices  33.8 us (21%)
  starting transfers between devices  31 us (19%)
  matrix products  18.8 us (12%)
  local copies, waits for them, and re-layouts  8.62 us (5%)
  Pallas kernels  4.89 us (3%)
    all_to_all x3, blocking collectives, near_exchange(): return lax.all_to_all(values, NEAR, 0, 0, tiled=True)  61.8 us
    ppermute x9, starting transfers between devices, from_others(): lax.ppermute(values, axes, [(i, (i + step) % count) for i in range(count)])  18.3 us
    ppermute x9, waiting for transfers between devices, from_others(): lax.ppermute(values, axes, [(i, (i + step) % count) for i in range(count)])  12.9 us
    all_to_all x1, waiting for transfers between devices, near_exchange(): return lax.all_to_all(values, NEAR, 0, 0, tiled=True)  12.1 us
    dot_general x3, matrix products, rows_dot(): lax.dot_general(left, right, (((0,), (0,)), ((), ())), preferred_element_...  8.94 us
    ppermute x5, waiting for transfers between devices, swap(): return lax.ppermute(values, 'core', [(0, 1), (1, 0)])  8.75 us
    unnamed x44, local copies, waits for them, and re-layouts  8.4 us
    ppermute x5, starting transfers between devices, swap(): return lax.ppermute(values, 'core', [(0, 1), (1, 0)])  8.11 us
  transfers between devices with their start and end apart: 15, of which 12 were waited for; matrix products, arithmetic and copies ran while one was open for 4% of the time, Pallas kernels for 0%

profile of v2, /device:TPU:1, one launch (start us, length us, event | category | flops | bytes accessed | tf_op | source)
XLA Modules:
  0.0 160.8 jit_solution(2919250521095993001)
XLA Ops:
  0.7 1.0 copy-done.4
  1.6 0.8 copy-done.11
  2.4 5.3 %collective-permute-start.2 = (bf16[64,384]{1,0:T(8,128)(2,1)S(1)}, bf16[64,384]{1,0:T(8,128)(2,1)S(1)}, u32[]{:S(2)}, u32[]{:S(2)}) collective-permute-start(bf16[64,384]{1,0:T(8,128)(2,1)S(1)} %pack_peaks.1.refs_0_), channel_id=1, source_target_pairs={{0,3},{1,0},{2,1},{3,2},{4,7},{5,4},{6,5},{7,6},{8,11},{9,8},{10,9... | collective-permute-start | bytes 147464 | tf_op jit(solution)/shard_map/ppermute | solution.py:160
  8.1 0.7 collective-permute-done.2.refs_3_
  8.9 0.6 copy-done.5
  9.5 3.5 %collective-permute-done.1.refs_2_ = bf16[64,384]{1,0:T(8,128)(2,1)S(1)} collective-permute-done((bf16[64,384]{1,0:T(8,128)(2,1)S(1)}, bf16[64,384]{1,0:T(8,128)(2,1)S(1)}, u32[]{:S(2)}, u32[]{:S(2)}) %collective-permute-start.1) | collective-permute-done | bytes 49184 | tf_op jit(solution)/shard_map/ppermute | solution.py:160
  12.9 0.6 copy-done.7
  13.6 0.6 copy-done.9
  14.2 0.8 copy-done.3
  15.0 0.8 copy-done.6
  15.8 0.8 copy-done.8
  16.6 0.8 copy-done.10
  17.4 3.3 %build_dense.1 = (bf16[256,768]{1,0:T(8,128)(2,1)S(1)}, bf16[256,768]{1,0:T(8,128)(2,1)S(1)}) custom-call(s32[3]{0:T(128)S(1)} %pad_add_fusion.place_ref, bf16[64,384]{1,0:T(8,128)(2,1)S(1)} %copy-done.3, bf16[64,384]{1,0:T(8,128)(2,1)S(1)} %copy-done.10, bf16[64,384]{1,0:T(8,128)(2,1)S(1)} %copy-done.8, bf16[64,384]{1,0:T(8,128)(2,1)S(1)} %copy-done.6), custom_call_target="tpu_custom_call" | custom-call | tf_op jit(solution)/shard_map/build_dense/pallas_call | solution.py:120
  20.7 1.1 collective-permute-start.3
  21.7 1.3 collective-permute-done.3
  23.1 3.0 %convolution_convert_fusion.2 = bf16[256,2048]{1,0:T(8,128)(2,1)S(1)} fusion(bf16[256,768]{1,0:T(8,128)(2,1)S(1)} %collective-permute-done.3, bf16[768,2048]{1,0:T(8,128)(2,1)} %param.7), kind=kOutput, calls=%fused_computation.5 | convolution fusion | flops 805830656 | bytes 4587520 | tf_op jit(solution)/shard_map/dot_general | solution.py:195
  26.6 2.3 %collective-permute-done.4 = bf16[256,2048]{1,0:T(8,128)(2,1)S(1)} collective-permute-done((bf16[256,2048]{1,0:T(8,128)(2,1)S(1)}, bf16[256,2048]{1,0:T(8,128)(2,1)S(1)}, u32[]{:S(2)}, u32[]{:S(2)}) %collective-permute-start.4) | collective-permute-done | bytes 1048608 | tf_op jit(solution)/shard_map/ppermute | solution.py:154
  28.9 1.0 fusion.1
  29.9 23.9 %all_to_all.20.parts_ref = bf16[32,8,2048]{2,1,0:T(8,128)(2,1)S(1)} all-to-all(bf16[32,8,2048]{2,1,0:T(8,128)(2,1)S(1)} %fusion.1), channel_id=1, replica_groups=mesh['x'=4,'zhi'=2,'y'=4,'core'=2,'zp'=2,'zq'=2] {'x','y','zq'}, dimensions={0} | all-to-all | bytes 2097152 | tf_op jit(solution)/shard_map/all_to_all | solution.py:166
  54.0 4.1 %collective-permute-start.7 = (bf16[8,2048]{1,0:T(8,128)(2,1)S(1)}, bf16[8,2048]{1,0:T(8,128)(2,1)S(1)}, u32[]{:S(2)}, u32[]{:S(2)}) collective-permute-start(bf16[8,2048]{1,0:T(8,128)(2,1)S(1)} %sum_parts.2), channel_id=1, source_target_pairs={{0,34},{2,0},{32,2},{34,32},{1,35},{3,1},{33,3},{35,33},{4,38},{6,... | collective-permute-start | bytes 98312 | tf_op jit(solution)/shard_map/ppermute | solution.py:160
  58.1 3.0 %collective-permute-start.5 = (bf16[8,2048]{1,0:T(8,128)(2,1)S(1)}, bf16[8,2048]{1,0:T(8,128)(2,1)S(1)}, u32[]{:S(2)}, u32[]{:S(2)}) collective-permute-start(bf16[8,2048]{1,0:T(8,128)(2,1)S(1)} %sum_parts.2), channel_id=1, source_target_pairs={{0,32},{2,34},{32,0},{34,2},{1,33},{3,35},{33,1},{35,3},{4,36},{6,... | collective-permute-start | bytes 98312 | tf_op jit(solution)/shard_map/ppermute | solution.py:160
  61.1 1.9 %collective-permute-done.6 = bf16[8,2048]{1,0:T(8,128)(2,1)S(1)} collective-permute-done((bf16[8,2048]{1,0:T(8,128)(2,1)S(1)}, bf16[8,2048]{1,0:T(8,128)(2,1)S(1)}, u32[]{:S(2)}, u32[]{:S(2)}) %collective-permute-start.6) | collective-permute-done | bytes 32800 | tf_op jit(solution)/shard_map/ppermute | solution.py:160
  63.0 1.9 %collective-permute-done.5 = bf16[8,2048]{1,0:T(8,128)(2,1)S(1)} collective-permute-done((bf16[8,2048]{1,0:T(8,128)(2,1)S(1)}, bf16[8,2048]{1,0:T(8,128)(2,1)S(1)}, u32[]{:S(2)}, u32[]{:S(2)}) %collective-permute-start.5) | collective-permute-done | bytes 32800 | tf_op jit(solution)/shard_map/ppermute | solution.py:160
  65.0 0.6 copy-done.17
  65.7 19.3 %all_to_all.21 = bf16[32,8,2048]{2,1,0:T(8,128)(2,1)S(1)} all-to-all(bf16[32,8,2048]{2,1,0:T(8,128)(2,1)S(1)} %broadcast_in_dim.4), channel_id=1, replica_groups=mesh['x'=4,'zhi'=2,'y'=4,'core'=2,'zp'=2,'zq'=2] {'x','y','zq'}, dimensions={0} | all-to-all | bytes 2097152 | tf_op jit(solution)/shard_map/all_to_all | solution.py:166
  85.0 2.8 %collective-permute-start.8 = (bf16[256,2048]{1,0:T(8,128)(2,1)S(1)}, bf16[256,2048]{1,0:T(8,128)(2,1)S(1)}, u32[]{:S(2)}, u32[]{:S(2)}) collective-permute-start(bf16[256,2048]{1,0:T(8,128)(2,1)S(1)} %bitcast.30), channel_id=1, source_target_pairs={{0,4},{4,0},{1,5},{5,1},{2,6},{6,2},{3,7},{7,3},{8,12},{12,8},{9,1... | collective-permute-start | bytes 3145736 | tf_op jit(solution)/shard_map/ppermute | solution.py:154
  87.8 2.3 %collective-permute-done.8 = bf16[256,2048]{1,0:T(8,128)(2,1)S(1)} collective-permute-done((bf16[256,2048]{1,0:T(8,128)(2,1)S(1)}, bf16[256,2048]{1,0:T(8,128)(2,1)S(1)}, u32[]{:S(2)}, u32[]{:S(2)}) %collective-permute-start.8) | collective-permute-done | bytes 1048608 | tf_op jit(solution)/shard_map/ppermute | solution.py:154
  90.1 1.0 copy-done.20
  91.1 1.0 fusion.5
  92.1 1.0 convolution_convert_fusion.1
  93.1 0.6 collective-permute-start.9
  93.8 1.8 %subtract_convert_fusion = (bf16[256,768]{1,0:T(8,128)(2,1)}, f32[256,768]{1,0:T(8,128)S(1)}) fusion(bf16[256,768]{1,0:T(8,128)(2,1)S(1)} %get-tuple-element.6, bf16[2048,768]{1,0:T(8,128)(2,1)S(1)} %copy-done, bf16[32,8,2048]{2,1,0:T(8,128)(2,1)S(1)} %all_to_all.21), kind=kOutput, calls=%fused_computation.17 | convolution fusion | flops 805896192 | bytes 5767168 | tf_op jit(solution)/shard_map/dot_general | solution.py:198
  95.5 0.5 collective-permute-done.9
  96.1 2.0 %fusion.6 = bf16[32,8,2048]{2,1,0:T(8,128)(2,1)} fusion(bf16[256,2048]{1,0:T(8,128)(2,1)S(1)} %collective-permute-done.9, bf16[2048,768]{1,0:T(8,128)(2,1)S(1)} %copy-done, f32[256,768]{1,0:T(8,128)S(1)} %get-tuple-element.11, bf16[256,768]{1,0:T(8,128)(2,1)S(1)} %get-tuple-element.6), kind=kOutput, calls=%fused_computation.13 | convolution fusion | flops 807469056 | bytes 6422528 | tf_op jit(solution)/shard_map/dot_general | solution.py:202
  98.1 4.7 %all-to-all-start.2 = ((bf16[32,8,2048]{2,1,0:T(8,128)(2,1)}), bf16[32,8,2048]{2,1,0:T(8,128)(2,1)}, u32[]{:S(2)}, u32[]{:S(2)}) async-start(bf16[32,8,2048]{2,1,0:T(8,128)(2,1)} %fusion.6), calls=%async_computation.2 | async-start | bytes 2097152 | tf_op jit(solution)/shard_map/all_to_all | solution.py:166
  102.7 5.2 %convolution_convert_fusion = bf16[2048,768]{1,0:T(8,128)(2,1)} fusion(bf16[256,2048]{1,0:T(8,128)(2,1)} %copy-done.20, bf16[256,2048]{1,0:T(8,128)(2,1)} %bitcast.31, bf16[256,768]{1,0:T(8,128)(2,1)} %copy-done.21, bf16[256,768]{1,0:T(8,128)(2,1)} %get-tuple-element.10), kind=kOutput, calls=%fused_computation.1 | convolution fusion | flops 1617952768 | bytes 6029312 | tf_op jit(solution)/shard_map/dot_general | solution.py:207
  108.0 12.1 %all-to-all-done.2.parts_ref = bf16[32,8,2048]{2,1,0:T(8,128)(2,1)} async-done(((bf16[32,8,2048]{2,1,0:T(8,128)(2,1)}), bf16[32,8,2048]{2,1,0:T(8,128)(2,1)}, u32[]{:S(2)}, u32[]{:S(2)}) %all-to-all-start.2) | async-done | bytes 1048608 | tf_op jit(solution)/shard_map/all_to_all | solution.py:166
  120.1 1.4 sum_parts.3
  121.6 3.3 %collective-permute-start.12 = (bf16[8,2048]{1,0:T(8,128)(2,1)S(1)}, bf16[8,2048]{1,0:T(8,128)(2,1)S(1)}, u32[]{:S(2)}, u32[]{:S(2)}) collective-permute-start(bf16[8,2048]{1,0:T(8,128)(2,1)S(1)} %sum_parts.3), channel_id=1, source_target_pairs={{0,34},{2,0},{32,2},{34,32},{1,35},{3,1},{33,3},{35,33},{4,38},{6,... | collective-permute-start | bytes 98312 | tf_op jit(solution)/shard_map/ppermute | solution.py:160
  124.9 2.2 %collective-permute-start.10 = (bf16[8,2048]{1,0:T(8,128)(2,1)S(1)}, bf16[8,2048]{1,0:T(8,128)(2,1)S(1)}, u32[]{:S(2)}, u32[]{:S(2)}) collective-permute-start(bf16[8,2048]{1,0:T(8,128)(2,1)S(1)} %sum_parts.3), channel_id=1, source_target_pairs={{0,32},{2,34},{32,0},{34,2},{1,33},{3,35},{33,1},{35,3},{4,36},{6,... | collective-permute-start | bytes 98312 | tf_op jit(solution)/shard_map/ppermute | solution.py:160
  127.0 2.9 %collective-permute-done.11 = bf16[8,2048]{1,0:T(8,128)(2,1)S(1)} collective-permute-done((bf16[8,2048]{1,0:T(8,128)(2,1)S(1)}, bf16[8,2048]{1,0:T(8,128)(2,1)S(1)}, u32[]{:S(2)}, u32[]{:S(2)}) %collective-permute-start.11) | collective-permute-done | bytes 32800 | tf_op jit(solution)/shard_map/ppermute | solution.py:160
  129.9 2.1 %collective-permute-done.10 = bf16[8,2048]{1,0:T(8,128)(2,1)S(1)} collective-permute-done((bf16[8,2048]{1,0:T(8,128)(2,1)S(1)}, bf16[8,2048]{1,0:T(8,128)(2,1)S(1)}, u32[]{:S(2)}, u32[]{:S(2)}) %collective-permute-start.10) | collective-permute-done | bytes 32800 | tf_op jit(solution)/shard_map/ppermute | solution.py:160
  132.0 0.9 fusion.17
  133.0 18.6 %all_to_all.22 = bf16[32,8,2048]{2,1,0:T(8,128)(2,1)S(1)} all-to-all(bf16[32,8,2048]{2,1,0:T(8,128)(2,1)S(1)} %broadcast_in_dim.5), channel_id=1, replica_groups=mesh['x'=4,'zhi'=2,'y'=4,'core'=2,'zp'=2,'zq'=2] {'x','y','zq'}, dimensions={0} | all-to-all | bytes 2097152 | tf_op jit(solution)/shard_map/all_to_all | solution.py:166
  151.6 3.2 %collective-permute-start.13 = (bf16[256,2048]{1,0:T(8,128)(2,1)S(1)}, bf16[256,2048]{1,0:T(8,128)(2,1)S(1)}, u32[]{:S(2)}, u32[]{:S(2)}) collective-permute-start(bf16[256,2048]{1,0:T(8,128)(2,1)S(1)} %bitcast.29), channel_id=1, source_target_pairs={{0,4},{4,0},{1,5},{5,1},{2,6},{6,2},{3,7},{7,3},{8,12},{12,8},{9,1... | collective-permute-start | bytes 3145736 | tf_op jit(solution)/shard_map/ppermute | solution.py:154
  154.8 2.3 %collective-permute-done.13 = bf16[256,2048]{1,0:T(8,128)(2,1)S(1)} collective-permute-done((bf16[256,2048]{1,0:T(8,128)(2,1)S(1)}, bf16[256,2048]{1,0:T(8,128)(2,1)S(1)}, u32[]{:S(2)}, u32[]{:S(2)}) %collective-permute-start.13) | collective-permute-done | bytes 1048608 | tf_op jit(solution)/shard_map/ppermute | solution.py:154
  157.1 1.0 fusion.22
  158.1 2.7 %add_convert_fusion = bf16[768,2048]{1,0:T(8,128)(2,1)} fusion(f32[768,2048]{1,0:T(8,128)S(1)} %fusion.22, bf16[256,768]{1,0:T(8,128)(2,1)S(1)} %get-tuple-element.6, bf16[32,8,2048]{2,1,0:T(8,128)(2,1)S(1)} %all_to_all.22), kind=kOutput, calls=%fused_computation | convolution fusion | flops 808452096 | bytes 10878976 | tf_op jit(solution)/shard_map/dot_general | solution.py:207
  (47 shorter events, 1.4 us)
Async XLA Ops:
  0.6 90.5 %copy-start = (bf16[2048,768]{1,0:T(8,128)(2,1)S(1)}, bf16[2048,768]{1,0:T(8,128)(2,1)}, u32[]{:S(2)}) copy-start(bf16[2048,768]{1,0:T(8,128)(2,1)} %param.9) | copy-start | bytes 9437188
  0.7 1.0 copy-start.4
  1.6 0.8 copy-start.11
  2.4 10.5 %copy-start.2 = (bf16[64,384]{1,0:T(8,128)(2,1)}, bf16[64,384]{1,0:T(8,128)(2,1)S(1)}, u32[]{:S(2)}) copy-start(bf16[64,384]{1,0:T(8,128)(2,1)S(1)} %pack_peaks.1.refs_0_) | copy-start | bytes 147460
  2.4 6.4 %collective-permute-start.2 = (bf16[64,384]{1,0:T(8,128)(2,1)S(1)}, bf16[64,384]{1,0:T(8,128)(2,1)S(1)}, u32[]{:S(2)}, u32[]{:S(2)}) collective-permute-start(bf16[64,384]{1,0:T(8,128)(2,1)S(1)} %pack_peaks.1.refs_0_), channel_id=1, source_target_pairs={{0,3},{1,0},{2,1},{3,2},{4,7},{5,4},{6,5},{7,6},{8,11},{9,8},{10,9... | collective-permute-start | bytes 147464 | tf_op jit(solution)/shard_map/ppermute | solution.py:160
  7.7 5.3 %collective-permute-start.1 = (bf16[64,384]{1,0:T(8,128)(2,1)S(1)}, bf16[64,384]{1,0:T(8,128)(2,1)S(1)}, u32[]{:S(2)}, u32[]{:S(2)}) collective-permute-start(bf16[64,384]{1,0:T(8,128)(2,1)S(1)} %pack_peaks.1.refs_0_), channel_id=1, source_target_pairs={{0,2},{1,3},{2,0},{3,1},{4,6},{5,7},{6,4},{7,5},{8,10},{9,11},{10,... | collective-permute-start | bytes 147464 | tf_op jit(solution)/shard_map/ppermute | solution.py:160
  7.7 5.9 %collective-permute-start = (bf16[64,384]{1,0:T(8,128)(2,1)S(1)}, bf16[64,384]{1,0:T(8,128)(2,1)S(1)}, u32[]{:S(2)}, u32[]{:S(2)}) collective-permute-start(bf16[64,384]{1,0:T(8,128)(2,1)S(1)} %pack_peaks.1.refs_0_), channel_id=1, source_target_pairs={{0,1},{1,2},{2,3},{3,0},{4,5},{5,6},{6,7},{7,4},{8,9},{9,10},{10,1... | collective-permute-start | bytes 147464 | tf_op jit(solution)/shard_map/ppermute | solution.py:160
  8.9 0.6 copy-start.5
  12.9 0.6 copy-start.7
  13.6 0.6 copy-start.9
  14.2 0.8 copy-start.3
  15.0 0.8 copy-start.6
  15.8 0.8 copy-start.8
  16.6 0.8 copy-start.10
  17.4 11.5 %copy-start.19 = (bf16[768,2048]{1,0:T(8,128)(2,1)S(1)}, bf16[768,2048]{1,0:T(8,128)(2,1)}, u32[]{:S(2)}) copy-start(bf16[768,2048]{1,0:T(8,128)(2,1)} %param.7) | copy-start | bytes 9437188
  20.7 2.4 %collective-permute-start.3 = (bf16[256,768]{1,0:T(8,128)(2,1)S(1)}, bf16[256,768]{1,0:T(8,128)(2,1)S(1)}, u32[]{:S(2)}, u32[]{:S(2)}) collective-permute-start(bf16[256,768]{1,0:T(8,128)(2,1)S(1)} %get-tuple-element.7), channel_id=1, source_target_pairs={{0,4},{4,0},{1,5},{5,1},{2,6},{6,2},{3,7},{7,3},{8,12},{12,8},{9,1... | collective-permute-start | bytes 1179656 | tf_op jit(solution)/shard_map/ppermute | solution.py:154
  23.1 67.0 %copy-start.13 = (bf16[256,768]{1,0:T(8,128)(2,1)}, bf16[256,768]{1,0:T(8,128)(2,1)S(1)}, u32[]{:S(2)}) copy-start(bf16[256,768]{1,0:T(8,128)(2,1)S(1)} %collective-permute-done.3) | copy-start | bytes 1179652
  26.1 2.7 %collective-permute-start.4 = (bf16[256,2048]{1,0:T(8,128)(2,1)S(1)}, bf16[256,2048]{1,0:T(8,128)(2,1)S(1)}, u32[]{:S(2)}, u32[]{:S(2)}) collective-permute-start(bf16[256,2048]{1,0:T(8,128)(2,1)S(1)} %convolution_convert_fusion.2), channel_id=1, source_target_pairs={{0,4},{4,0},{1,5},{5,1},{2,6},{6,2},{3,7},{7,3},{8,12},{12,8},{9,1... | collective-permute-start | bytes 3145736 | tf_op jit(solution)/shard_map/ppermute | solution.py:154
  28.9 36.7 %copy-start.18 = (f32[2048]{0:T(1024)S(1)}, f32[2048]{0:T(1024)}, u32[]{:S(2)}) copy-start(f32[2048]{0:T(1024)} %param.8) | copy-start | bytes 24580
  54.0 11.0 %copy-start.1 = (bf16[8,2048]{1,0:T(8,128)(2,1)}, bf16[8,2048]{1,0:T(8,128)(2,1)S(1)}, u32[]{:S(2)}) copy-start(bf16[8,2048]{1,0:T(8,128)(2,1)S(1)} %sum_parts.2) | copy-start | bytes 98308
  54.0 7.2 %collective-permute-start.7 = (bf16[8,2048]{1,0:T(8,128)(2,1)S(1)}, bf16[8,2048]{1,0:T(8,128)(2,1)S(1)}, u32[]{:S(2)}, u32[]{:S(2)}) collective-permute-start(bf16[8,2048]{1,0:T(8,128)(2,1)S(1)} %sum_parts.2), channel_id=1, source_target_pairs={{0,34},{2,0},{32,2},{34,32},{1,35},{3,1},{33,3},{35,33},{4,38},{6,... | collective-permute-start | bytes 98312 | tf_op jit(solution)/shard_map/ppermute | solution.py:160
  58.1 4.9 %collective-permute-start.6 = (bf16[8,2048]{1,0:T(8,128)(2,1)S(1)}, bf16[8,2048]{1,0:T(8,128)(2,1)S(1)}, u32[]{:S(2)}, u32[]{:S(2)}) collective-permute-start(bf16[8,2048]{1,0:T(8,128)(2,1)S(1)} %sum_parts.2), channel_id=1, source_target_pairs={{0,2},{2,32},{32,34},{34,0},{1,3},{3,33},{33,35},{35,1},{4,6},{6,3... | collective-permute-start | bytes 98312 | tf_op jit(solution)/shard_map/ppermute | solution.py:160
  58.1 6.8 %collective-permute-start.5 = (bf16[8,2048]{1,0:T(8,128)(2,1)S(1)}, bf16[8,2048]{1,0:T(8,128)(2,1)S(1)}, u32[]{:S(2)}, u32[]{:S(2)}) collective-permute-start(bf16[8,2048]{1,0:T(8,128)(2,1)S(1)} %sum_parts.2), channel_id=1, source_target_pairs={{0,32},{2,34},{32,0},{34,2},{1,33},{3,35},{33,1},{35,3},{4,36},{6,... | collective-permute-start | bytes 98312 | tf_op jit(solution)/shard_map/ppermute | solution.py:160
  61.1 3.8 %copy-start.15 = (bf16[8,2048]{1,0:T(8,128)(2,1)}, bf16[8,2048]{1,0:T(8,128)(2,1)S(1)}, u32[]{:S(2)}) copy-start(bf16[8,2048]{1,0:T(8,128)(2,1)S(1)} %collective-permute-done.7) | copy-start | bytes 98308
  63.0 2.0 %copy-start.16 = (bf16[8,2048]{1,0:T(8,128)(2,1)}, bf16[8,2048]{1,0:T(8,128)(2,1)S(1)}, u32[]{:S(2)}) copy-start(bf16[8,2048]{1,0:T(8,128)(2,1)S(1)} %collective-permute-done.6) | copy-start | bytes 98308
  64.9 0.6 copy-start.17
  85.0 8.8 %copy-start.12 = (bf16[32,8,2048]{2,1,0:T(8,128)(2,1)}, bf16[32,8,2048]{2,1,0:T(8,128)(2,1)S(1)}, u32[]{:S(2)}) copy-start(bf16[32,8,2048]{2,1,0:T(8,128)(2,1)S(1)} %all_to_all.21) | copy-start | bytes 3145732
  85.0 5.1 %collective-permute-start.8 = (bf16[256,2048]{1,0:T(8,128)(2,1)S(1)}, bf16[256,2048]{1,0:T(8,128)(2,1)S(1)}, u32[]{:S(2)}, u32[]{:S(2)}) collective-permute-start(bf16[256,2048]{1,0:T(8,128)(2,1)S(1)} %bitcast.30), channel_id=1, source_target_pairs={{0,4},{4,0},{1,5},{5,1},{2,6},{6,2},{3,7},{7,3},{8,12},{12,8},{9,1... | collective-permute-start | bytes 3145736 | tf_op jit(solution)/shard_map/ppermute | solution.py:154
  90.1 1.0 copy-start.20
  92.1 3.4 %copy-start.21 = (bf16[256,768]{1,0:T(8,128)(2,1)}, bf16[256,768]{1,0:T(8,128)(2,1)S(1)}, u32[]{:S(2)}) copy-start(bf16[256,768]{1,0:T(8,128)(2,1)S(1)} %fusion.5) | copy-start | bytes 1179652
  93.1 2.9 %collective-permute-start.9 = (bf16[256,2048]{1,0:T(8,128)(2,1)S(1)}, bf16[256,2048]{1,0:T(8,128)(2,1)S(1)}, u32[]{:S(2)}, u32[]{:S(2)}) collective-permute-start(bf16[256,2048]{1,0:T(8,128)(2,1)S(1)} %convolution_convert_fusion.1), channel_id=1, source_target_pairs={{0,4},{4,0},{1,5},{5,1},{2,6},{6,2},{3,7},{7,3},{8,12},{12,8},{9,1... | collective-permute-start | bytes 3145736 | tf_op jit(solution)/shard_map/ppermute | solution.py:154
  98.1 22.1 %all-to-all-start.2 = ((bf16[32,8,2048]{2,1,0:T(8,128)(2,1)}), bf16[32,8,2048]{2,1,0:T(8,128)(2,1)}, u32[]{:S(2)}, u32[]{:S(2)}) async-start(bf16[32,8,2048]{2,1,0:T(8,128)(2,1)} %fusion.6), calls=%async_computation.2 | async-start | bytes 2097152 | tf_op jit(solution)/shard_map/all_to_all | solution.py:166
  120.1 36.9 %copy-start.14 = (bf16[256,768]{1,0:T(8,128)(2,1)S(1)}, bf16[256,768]{1,0:T(8,128)(2,1)}, u32[]{:S(2)}) copy-start(bf16[256,768]{1,0:T(8,128)(2,1)} %copy-done.13) | copy-start | bytes 1179652
  121.6 5.5 %collective-permute-start.12 = (bf16[8,2048]{1,0:T(8,128)(2,1)S(1)}, bf16[8,2048]{1,0:T(8,128)(2,1)S(1)}, u32[]{:S(2)}, u32[]{:S(2)}) collective-permute-start(bf16[8,2048]{1,0:T(8,128)(2,1)S(1)} %sum_parts.3), channel_id=1, source_target_pairs={{0,34},{2,0},{32,2},{34,32},{1,35},{3,1},{33,3},{35,33},{4,38},{6,... | collective-permute-start | bytes 98312 | tf_op jit(solution)/shard_map/ppermute | solution.py:160
  124.9 5.0 %collective-permute-start.11 = (bf16[8,2048]{1,0:T(8,128)(2,1)S(1)}, bf16[8,2048]{1,0:T(8,128)(2,1)S(1)}, u32[]{:S(2)}, u32[]{:S(2)}) collective-permute-start(bf16[8,2048]{1,0:T(8,128)(2,1)S(1)} %sum_parts.3), channel_id=1, source_target_pairs={{0,2},{2,32},{32,34},{34,0},{1,3},{3,33},{33,35},{35,1},{4,6},{6,3... | collective-permute-start | bytes 98312 | tf_op jit(solution)/shard_map/ppermute | solution.py:160
  124.9 7.1 %collective-permute-start.10 = (bf16[8,2048]{1,0:T(8,128)(2,1)S(1)}, bf16[8,2048]{1,0:T(8,128)(2,1)S(1)}, u32[]{:S(2)}, u32[]{:S(2)}) collective-permute-start(bf16[8,2048]{1,0:T(8,128)(2,1)S(1)} %sum_parts.3), channel_id=1, source_target_pairs={{0,32},{2,34},{32,0},{34,2},{1,33},{3,35},{33,1},{35,3},{4,36},{6,... | collective-permute-start | bytes 98312 | tf_op jit(solution)/shard_map/ppermute | solution.py:160
  151.6 5.4 %collective-permute-start.13 = (bf16[256,2048]{1,0:T(8,128)(2,1)S(1)}, bf16[256,2048]{1,0:T(8,128)(2,1)S(1)}, u32[]{:S(2)}, u32[]{:S(2)}) collective-permute-start(bf16[256,2048]{1,0:T(8,128)(2,1)S(1)} %bitcast.29), channel_id=1, source_target_pairs={{0,4},{4,0},{1,5},{5,1},{2,6},{6,2},{3,7},{7,3},{8,12},{12,8},{9,1... | collective-permute-start | bytes 3145736 | tf_op jit(solution)/shard_map/ppermute | solution.py:154

commit v3 on v2

--- a/solution.py
+++ b/solution.py
@@ -120,7 +120,9 @@
     return pl.pallas_call(
         functools.partial(dense_kernel, groups=len(blocks)),
         out_shape=(jax.ShapeDtypeStruct((rows, width), BF16),) * 2,
-        in_specs=[pl.BlockSpec(memory_space=pltpu.SMEM)] + [vmem] * len(blocks),
+        grid=(1,),
+        in_specs=[pl.BlockSpec(memory_space=pltpu.SMEM)]
+        + [pl.BlockSpec(block.shape, lambda i: (0, 0)) for block in blocks],
         out_specs=(vmem, vmem),
         compiler_params=pltpu.CompilerParams(vmem_limit_bytes=8 << 20),
         name="build_dense",
@@ -186,21 +188,24 @@
     partner = position + (1 - 2 * core) * stride
     place = jnp.stack([position * width, partner * width, group]).astype(jnp.int32)
     packed = pack_peaks(core.reshape(1), peak_bins, peak_values)
-    dense_own, dense_sent = build_dense(
+    enc_weights = (enc_weight, swap(enc_weight))
+    dec_weights = (dec_weight, swap(dec_weight))
+    dense_own, dense_pair = build_dense(
         place, [packed] + from_others(packed, SPECTRA_AXES), width
     )
-    dense_other = swap(dense_sent)
-
-    def encode(block):
-        return jnp.dot(block, enc_weight, preferred_element_type=F32)
-
-    def residual(block, hidden):
-        recon = jnp.dot(hidden, dec_weight, preferred_element_type=F32)
+    dense = (dense_own, dense_pair)
+    dense_other = swap(dense_pair)
+
+    def encode(block, weight):
+        return jnp.dot(block, weight, preferred_element_type=F32)
+
+    def residual(block, hidden, weight):
+        recon = jnp.dot(hidden, weight, preferred_element_type=F32)
         return (recon - block.astype(F32)).astype(BF16)
 
-    def decode_back(resid):
+    def decode_back(resid, weight):
         return lax.dot_general(
-            resid, dec_weight, (((1,), (1,)), ((), ())), preferred_element_type=F32
+            resid, weight, (((1,), (1,)), ((), ())), preferred_element_type=F32
         )
 
     def rows_dot(left, right):
@@ -208,25 +213,22 @@
             left, right, (((0,), (0,)), ((), ())), preferred_element_type=F32
         )
 
-    def near_parts(own, other):
-        half = own + swap(other.astype(BF16)).astype(F32)
-        return near_exchange(half.astype(BF16).reshape(lax.axis_size(NEAR), -1, hidden_size))
-
-    parts = near_parts(encode(dense_own), encode(dense_other))
+    def near_parts(rows):
+        return near_exchange(rows.astype(BF16).reshape(lax.axis_size(NEAR), -1, hidden_size))
+
+    parts = near_parts(sum(map(encode, dense, enc_weights)))
     pre = far_sum(sum_parts(parts)) + enc_bias
-    hidden_own = near_gather(activation(pre).astype(BF16))
-    hidden_other = swap(hidden_own)
-    resid_own = residual(dense_own, hidden_own)
-    resid_other = residual(dense_other, hidden_other)
-    parts = near_parts(decode_back(resid_own), decode_back(resid_other))
+    hidden = near_gather(activation(pre).astype(BF16))
+    resid = [residual(block, hidden, weight) for block, weight in zip(dense, dec_weights)]
+    parts = near_parts(sum(map(decode_back, resid, dec_weights)))
     grad_dec = rows_dot(
-        jnp.concatenate([hidden_own, hidden_other]), jnp.concatenate([resid_own, resid_other])
+        jnp.concatenate([hidden, swap(hidden)]), jnp.concatenate([resid[0], swap(resid[1])])
     ).astype(BF16)
-    parts, grad_dec = lax.optimization_barrier((parts, grad_dec))
+    parts, grad_dec, dense_other = lax.optimization_barrier((parts, grad_dec, dense_other))
     back = far_sum(sum_parts(parts))
-    dpre_own = near_gather(slope_times(pre, back))
-    dpre_other = swap(dpre_own)
-    grad_enc = (rows_dot(dense_own, dpre_own) + rows_dot(dense_other, dpre_other)).astype(BF16)
+    dpre = near_gather(slope_times(pre, back))
+    grad_own, dpre_other = lax.optimization_barrier((rows_dot(dense_own, dpre), swap(dpre)))
+    grad_enc = (grad_own + rows_dot(dense_other, dpre_other)).astype(BF16)
     return (grad_enc, grad_dec)
 
 

time: 161 us -> 142 us (0.88)
  waiting for transfers between devices: 33.8 us -> 19.4 us
  local copies, waits for them, and re-layouts: 8.62 us -> 1.83 us
  starting transfers between devices: 31 us -> 33.4 us
  other arithmetic: 1.02 us -> 2.92 us
    all_to_all x1, waiting for transfers between devices: 12.1 us -> 4.94 us  [near_exchange(): return lax.all_to_all(values, NEAR, 0, 0, tiled=True)]
    unnamed x44 -> x10, local copies, waits for them, and re-layouts: 8.4 us -> 1.61 us
    ppermute x5 -> x6, starting transfers between devices: 8.11 us -> 13.9 us  [swap(): return lax.ppermute(values, 'core', [(0, 1), (1, 0)])]
    ppermute x5 -> x6, waiting for transfers between devices: 8.75 us -> 4.26 us  [swap(): return lax.ppermute(values, 'core', [(0, 1), (1, 0)])]
    convert_element_type x1 -> x2, other arithmetic: 0.05 us -> 2.75 us  [the longest x1 2.7 us: on_device(): grad_enc = (grad_own + rows_dot(dense_other, dpre_other)).astype(BF16)]
    ppermute x9, waiting for transfers between devices: 12.9 us -> 10.2 us  [from_others(): lax.ppermute(values, axes, [(i, (i + step) % count) for i in range(count)])]
    ppermute x9, starting transfers between devices: 18.3 us -> 15.6 us  [from_others(): lax.ppermute(values, axes, [(i, (i + step) % count) for i in range(count)])]
    dot_general x3, matrix products: 8.94 us -> 6.53 us  [rows_dot(): lax.dot_general(left, right, (((0,), (0,)), ((), ())), preferred_element_...]
  transfers between devices with their start and end apart: 15 -> 16, of which waited for: 12 -> 9; matrix products, arithmetic and copies ran while one was open for 4% -> 6% of each run, Pallas kernels for 0% -> 2%
where the time goes in v3:
time: 142 us; the launch traced here: 141 us
  blocking collectives  61 us (43%)
  starting transfers between devices  33.4 us (24%)
  waiting for transfers between devices  19.4 us (14%)
  matrix products  18 us (13%)
  Pallas kernels  3.63 us (3%)
  other arithmetic  2.92 us (2%)
  local copies, waits for them, and re-layouts  1.83 us (1%)
    all_to_all x3, blocking collectives, near_exchange(): return lax.all_to_all(values, NEAR, 0, 0, tiled=True)  61 us
    ppermute x9, starting transfers between devices, from_others(): lax.ppermute(values, axes, [(i, (i + step) % count) for i in range(count)])  15.6 us
    ppermute x6, starting transfers between devices, swap(): return lax.ppermute(values, 'core', [(0, 1), (1, 0)])  13.9 us
    ppermute x9, waiting for transfers between devices, from_others(): lax.ppermute(values, axes, [(i, (i + step) % count) for i in range(count)])  10.2 us
    dot_general x3, matrix products, rows_dot(): lax.dot_general(left, right, (((0,), (0,)), ((), ())), preferred_element_...  6.53 us
    all_to_all x1, waiting for transfers between devices, near_exchange(): return lax.all_to_all(values, NEAR, 0, 0, tiled=True)  4.94 us
    ppermute x6, waiting for transfers between devices, swap(): return lax.ppermute(values, 'core', [(0, 1), (1, 0)])  4.26 us
    dot_general x2, matrix products, decode_back(): lax.dot_general(resid, weight, (((1,), (1,)), ((), ())), preferred_elemen...  4.03 us
  transfers between devices with their start and end apart: 16, of which 9 were waited for; matrix products, arithmetic and copies ran while one was open for 6% of the time, Pallas kernels for 2%

profile of v3, /device:TPU:1, one launch (start us, length us, event | category | flops | bytes accessed | tf_op | source)
XLA Modules:
  0.0 141.0 jit_solution(1612394634940584870)
XLA Ops:
  0.6 3.3 %collective-permute-start.3 = (bf16[768,2048]{1,0:T(8,128)(2,1)}, bf16[768,2048]{1,0:T(8,128)(2,1)}, u32[]{:S(2)}, u32[]{:S(2)}) collective-permute-start(bf16[768,2048]{1,0:T(8,128)(2,1)} %param.7), channel_id=1, source_target_pairs={{0,4},{4,0},{1,5},{5,1},{2,6},{6,2},{3,7},{7,3},{8,12},{12,8},{9,1... | collective-permute-start | bytes 9437192 | tf_op jit(solution)/shard_map/ppermute | solution.py:156
  4.0 0.8 copy-done
  4.8 0.8 copy-done.1
  5.6 2.7 %collective-permute-start.2 = (bf16[64,384]{1,0:T(8,128)(2,1)S(1)}, bf16[64,384]{1,0:T(8,128)(2,1)S(1)}, u32[]{:S(2)}, u32[]{:S(2)}) collective-permute-start(bf16[64,384]{1,0:T(8,128)(2,1)S(1)} %pack_peaks.1.refs_0_), channel_id=1, source_target_pairs={{0,3},{1,0},{2,1},{3,2},{4,7},{5,4},{6,5},{7,6},{8,11},{9,8},{10,9... | collective-permute-start | bytes 147464 | tf_op jit(solution)/shard_map/ppermute | solution.py:162
  8.3 0.0 collective-permute-start.1
  8.3 0.4 collective-permute-start
  8.6 0.1 pad_add_fusion.place_ref
  8.7 0.7 collective-permute-done.2.refs_3_
  9.4 2.7 %collective-permute-done.1.refs_2_ = bf16[64,384]{1,0:T(8,128)(2,1)S(1)} collective-permute-done((bf16[64,384]{1,0:T(8,128)(2,1)S(1)}, bf16[64,384]{1,0:T(8,128)(2,1)S(1)}, u32[]{:S(2)}, u32[]{:S(2)}) %collective-permute-start.1) | collective-permute-done | bytes 49184 | tf_op jit(solution)/shard_map/ppermute | solution.py:162
  12.1 1.0 collective-permute-done.refs_1_
  13.1 3.3 %build_dense.1 = (bf16[256,768]{1,0:T(8,128)(2,1)S(1)}, bf16[256,768]{1,0:T(8,128)(2,1)S(1)}) custom-call(s32[3]{0:T(128)S(1)} %pad_add_fusion.place_ref, bf16[64,384]{1,0:T(8,128)(2,1)S(1)} %pack_peaks.1.refs_0_, bf16[64,384]{1,0:T(8,128)(2,1)S(1)} %collective-permute-done.refs_1_, bf16[64,384]{1,0:T(8,128)(2,1)S(1)} %collective-permute-done.1.refs_2_, ...), custom_call_target="tpu_custom_call" | custom-call | tf_op jit(solution)/shard_map/build_dense/pallas_call | solution.py:120
  16.4 2.9 %fusion.25 = f32[256,2048]{1,0:T(8,128)S(1)} fusion(bf16[256,768]{1,0:T(8,128)(2,1)S(1)} %get-tuple-element.10, bf16[768,2048]{1,0:T(8,128)(2,1)} %collective-permute-done.3), kind=kOutput, calls=%fused_computation.36 | convolution fusion | flops 805306368 | bytes 5636096 | tf_op jit(solution)/shard_map/dot_general | solution.py:200
  19.3 1.1 fusion.3
  20.4 0.0 copy-start.3
  20.4 0.0 copy-start.4
  20.4 23.8 %all_to_all.20.parts_ref = bf16[32,8,2048]{2,1,0:T(8,128)(2,1)S(1)} all-to-all(bf16[32,8,2048]{2,1,0:T(8,128)(2,1)S(1)} %fusion.3), channel_id=1, replica_groups=mesh['x'=4,'zhi'=2,'y'=4,'core'=2,'zp'=2,'zq'=2] {'x','y','zq'}, dimensions={0} | all-to-all | bytes 2097152 | tf_op jit(solution)/shard_map/all_to_all | solution.py:168
  44.2 0.1 sum_parts.2
  44.3 4.6 %collective-permute-start.6 = (bf16[8,2048]{1,0:T(8,128)(2,1)S(1)}, bf16[8,2048]{1,0:T(8,128)(2,1)S(1)}, u32[]{:S(2)}, u32[]{:S(2)}) collective-permute-start(bf16[8,2048]{1,0:T(8,128)(2,1)S(1)} %sum_parts.2), channel_id=1, source_target_pairs={{0,34},{2,0},{32,2},{34,32},{1,35},{3,1},{33,3},{35,33},{4,38},{6,... | collective-permute-start | bytes 98312 | tf_op jit(solution)/shard_map/ppermute | solution.py:162
  49.0 0.0 collective-permute-start.5
  49.0 2.2 %collective-permute-start.4 = (bf16[8,2048]{1,0:T(8,128)(2,1)S(1)}, bf16[8,2048]{1,0:T(8,128)(2,1)S(1)}, u32[]{:S(2)}, u32[]{:S(2)}) collective-permute-start(bf16[8,2048]{1,0:T(8,128)(2,1)S(1)} %sum_parts.2), channel_id=1, source_target_pairs={{0,32},{2,34},{32,0},{34,2},{1,33},{3,35},{33,1},{35,3},{4,36},{6,... | collective-permute-start | bytes 98312 | tf_op jit(solution)/shard_map/ppermute | solution.py:162
  51.2 3.5 %collective-permute-start.7 = (bf16[2048,768]{1,0:T(8,128)(2,1)S(1)}, bf16[2048,768]{1,0:T(8,128)(2,1)S(1)}, u32[]{:S(2)}, u32[]{:S(2)}) collective-permute-start(bf16[2048,768]{1,0:T(8,128)(2,1)S(1)} %copy-done.3), channel_id=1, source_target_pairs={{0,4},{4,0},{1,5},{5,1},{2,6},{6,2},{3,7},{7,3},{8,12},{12,8},{9,1... | collective-permute-start | bytes 9437192 | tf_op jit(solution)/shard_map/ppermute | solution.py:156
  54.6 1.1 collective-permute-done.4
  55.8 0.1 broadcast_in_dim.4
  55.9 19.1 %all_to_all.21 = bf16[32,8,2048]{2,1,0:T(8,128)(2,1)S(1)} all-to-all(bf16[32,8,2048]{2,1,0:T(8,128)(2,1)S(1)} %broadcast_in_dim.4), channel_id=1, replica_groups=mesh['x'=4,'zhi'=2,'y'=4,'core'=2,'zp'=2,'zq'=2] {'x','y','zq'}, dimensions={0} | all-to-all | bytes 2097152 | tf_op jit(solution)/shard_map/all_to_all | solution.py:168
  75.0 1.7 %subtract_convert_fusion = (bf16[256,768]{1,0:T(8,128)(2,1)}, f32[256,768]{1,0:T(8,128)S(1)}) fusion(bf16[256,768]{1,0:T(8,128)(2,1)S(1)} %get-tuple-element.9, bf16[2048,768]{1,0:T(8,128)(2,1)S(1)} %copy-done.3, bf16[32,8,2048]{2,1,0:T(8,128)(2,1)S(1)} %all_to_all.21), kind=kOutput, calls=%fused_computation.16 | convolution fusion | flops 805896192 | bytes 5767168 | tf_op jit(solution)/shard_map/dot_general | solution.py:203
  76.8 1.0 fusion.11
  77.8 1.7 %fusion.7 = bf16[256,768]{1,0:T(8,128)(2,1)} fusion(bf16[2048,768]{1,0:T(8,128)(2,1)S(1)} %collective-permute-done.7, bf16[256,768]{1,0:T(8,128)(2,1)S(1)} %get-tuple-element.10, bf16[32,8,2048]{2,1,0:T(8,128)(2,1)S(1)} %all_to_all.21), kind=kOutput, calls=%fused_computation.12 | convolution fusion | flops 805896192 | bytes 4980736 | tf_op jit(solution)/shard_map/dot_general | solution.py:203
  79.5 3.0 %fusion.2 = bf16[32,8,2048]{2,1,0:T(8,128)(2,1)} fusion(f32[256,2048]{1,0:T(8,128)S(1)} %fusion.11, bf16[256,768]{1,0:T(8,128)(2,1)} %fusion.7, bf16[2048,768]{1,0:T(8,128)(2,1)S(1)} %collective-permute-done.7), kind=kOutput, calls=%fused_computation.6 | convolution fusion | flops 806354944 | bytes 6684672 | tf_op jit(solution)/shard_map/dot_general | solution.py:207
  82.5 3.9 %all-to-all-start.2 = ((bf16[32,8,2048]{2,1,0:T(8,128)(2,1)}), bf16[32,8,2048]{2,1,0:T(8,128)(2,1)S(1)}, u32[]{:S(2)}, u32[]{:S(2)}) async-start(bf16[32,8,2048]{2,1,0:T(8,128)(2,1)} %fusion.2), calls=%async_computation.2 | async-start | bytes 2097152 | tf_op jit(solution)/shard_map/all_to_all | solution.py:168
  86.5 3.0 %collective-permute-start.8 = (bf16[256,2048]{1,0:T(8,128)(2,1)S(1)}, bf16[256,2048]{1,0:T(8,128)(2,1)S(1)}, u32[]{:S(2)}, u32[]{:S(2)}) collective-permute-start(bf16[256,2048]{1,0:T(8,128)(2,1)S(1)} %bitcast.31), channel_id=1, source_target_pairs={{0,4},{4,0},{1,5},{5,1},{2,6},{6,2},{3,7},{7,3},{8,12},{12,8},{9,1... | collective-permute-start | bytes 3145736 | tf_op jit(solution)/shard_map/ppermute | solution.py:156
  89.4 0.1 collective-permute-start.9
  89.5 0.4 collective-permute-start.10
  90.0 3.0 %collective-permute-done.9 = bf16[256,768]{1,0:T(8,128)(2,1)S(1)} collective-permute-done((bf16[256,768]{1,0:T(8,128)(2,1)}, bf16[256,768]{1,0:T(8,128)(2,1)S(1)}, u32[]{:S(2)}, u32[]{:S(2)}) %collective-permute-start.9) | collective-permute-done | bytes 393248 | tf_op jit(solution)/shard_map/ppermute | solution.py:156
  92.9 4.5 %convolution_convert_fusion = bf16[2048,768]{1,0:T(8,128)(2,1)} fusion(bf16[256,2048]{1,0:T(8,128)(2,1)S(1)} %collective-permute-done.8, bf16[256,2048]{1,0:T(8,128)(2,1)S(1)} %bitcast.32, bf16[256,768]{1,0:T(8,128)(2,1)S(1)} %collective-permute-done.9, bf16[256,768]{1,0:T(8,128)(2,1)} %get-tuple-element.16), kind=kOutput, calls=%fused_computation.1 | convolution fusion | flops 1617952768 | bytes 6029312 | tf_op jit(solution)/shard_map/dot_general | solution.py:212
  97.4 4.9 %all-to-all-done.2.parts_ref = bf16[32,8,2048]{2,1,0:T(8,128)(2,1)S(1)} async-done(((bf16[32,8,2048]{2,1,0:T(8,128)(2,1)}), bf16[32,8,2048]{2,1,0:T(8,128)(2,1)S(1)}, u32[]{:S(2)}, u32[]{:S(2)}) %all-to-all-start.2) | async-done | bytes 1048608 | tf_op jit(solution)/shard_map/all_to_all | solution.py:168
  102.4 0.1 sum_parts.3
  102.5 3.5 %collective-permute-start.13 = (bf16[8,2048]{1,0:T(8,128)(2,1)S(1)}, bf16[8,2048]{1,0:T(8,128)(2,1)S(1)}, u32[]{:S(2)}, u32[]{:S(2)}) collective-permute-start(bf16[8,2048]{1,0:T(8,128)(2,1)S(1)} %sum_parts.3), channel_id=1, source_target_pairs={{0,34},{2,0},{32,2},{34,32},{1,35},{3,1},{33,3},{35,33},{4,38},{6,... | collective-permute-start | bytes 98312 | tf_op jit(solution)/shard_map/ppermute | solution.py:162
  106.1 2.2 %collective-permute-start.11 = (bf16[8,2048]{1,0:T(8,128)(2,1)S(1)}, bf16[8,2048]{1,0:T(8,128)(2,1)S(1)}, u32[]{:S(2)}, u32[]{:S(2)}) collective-permute-start(bf16[8,2048]{1,0:T(8,128)(2,1)S(1)} %sum_parts.3), channel_id=1, source_target_pairs={{0,32},{2,34},{32,0},{34,2},{1,33},{3,35},{33,1},{35,3},{4,36},{6,... | collective-permute-start | bytes 98312 | tf_op jit(solution)/shard_map/ppermute | solution.py:162
  108.3 2.7 %collective-permute-done.12 = bf16[8,2048]{1,0:T(8,128)(2,1)S(1)} collective-permute-done((bf16[8,2048]{1,0:T(8,128)(2,1)S(1)}, bf16[8,2048]{1,0:T(8,128)(2,1)S(1)}, u32[]{:S(2)}, u32[]{:S(2)}) %collective-permute-start.12) | collective-permute-done | bytes 32800 | tf_op jit(solution)/shard_map/ppermute | solution.py:162
  111.0 2.0 %collective-permute-done.11 = bf16[8,2048]{1,0:T(8,128)(2,1)S(1)} collective-permute-done((bf16[8,2048]{1,0:T(8,128)(2,1)S(1)}, bf16[8,2048]{1,0:T(8,128)(2,1)S(1)}, u32[]{:S(2)}, u32[]{:S(2)}) %collective-permute-start.11) | collective-permute-done | bytes 32800 | tf_op jit(solution)/shard_map/ppermute | solution.py:162
  113.0 0.1 fusion.18
  113.1 0.1 broadcast_in_dim.5
  113.2 18.2 %all_to_all.22 = bf16[32,8,2048]{2,1,0:T(8,128)(2,1)S(1)} all-to-all(bf16[32,8,2048]{2,1,0:T(8,128)(2,1)S(1)} %broadcast_in_dim.5), channel_id=1, replica_groups=mesh['x'=4,'zhi'=2,'y'=4,'core'=2,'zp'=2,'zq'=2] {'x','y','zq'}, dimensions={0} | all-to-all | bytes 2097152 | tf_op jit(solution)/shard_map/all_to_all | solution.py:168
  131.4 3.6 %collective-permute-start.14 = (bf16[256,2048]{1,0:T(8,128)(2,1)S(1)}, bf16[256,2048]{1,0:T(8,128)(2,1)S(1)}, u32[]{:S(2)}, u32[]{:S(2)}) collective-permute-start(bf16[256,2048]{1,0:T(8,128)(2,1)S(1)} %bitcast.30), channel_id=1, source_target_pairs={{0,4},{4,0},{1,5},{5,1},{2,6},{6,2},{3,7},{7,3},{8,12},{12,8},{9,1... | collective-permute-start | bytes 3145736 | tf_op jit(solution)/shard_map/ppermute | solution.py:156
  135.0 1.0 fusion.20
  136.0 1.3 collective-permute-done.14
  137.3 1.0 fusion.26
  138.3 2.7 %add_convert_fusion = bf16[768,2048]{1,0:T(8,128)(2,1)} fusion(f32[768,2048]{1,0:T(8,128)S(1)} %fusion.20, f32[768,2048]{1,0:T(8,128)S(1)} %fusion.26), kind=kLoop, calls=%fused_computation | loop fusion | flops 3145728 | bytes 15728640 | tf_op jit(solution)/shard_map/convert_element_type | solution.py:231
  (16 shorter events, 0.1 us)
Async XLA Ops:
  0.6 15.8 %collective-permute-start.3 = (bf16[768,2048]{1,0:T(8,128)(2,1)}, bf16[768,2048]{1,0:T(8,128)(2,1)}, u32[]{:S(2)}, u32[]{:S(2)}) collective-permute-start(bf16[768,2048]{1,0:T(8,128)(2,1)} %param.7), channel_id=1, source_target_pairs={{0,4},{4,0},{1,5},{5,1},{2,6},{6,2},{3,7},{7,3},{8,12},{12,8},{9,1... | collective-permute-start | bytes 9437192 | tf_op jit(solution)/shard_map/ppermute | solution.py:156
  4.0 0.8 copy-start
  4.8 0.8 copy-start.1
  5.6 3.9 %collective-permute-start.2 = (bf16[64,384]{1,0:T(8,128)(2,1)S(1)}, bf16[64,384]{1,0:T(8,128)(2,1)S(1)}, u32[]{:S(2)}, u32[]{:S(2)}) collective-permute-start(bf16[64,384]{1,0:T(8,128)(2,1)S(1)} %pack_peaks.1.refs_0_), channel_id=1, source_target_pairs={{0,3},{1,0},{2,1},{3,2},{4,7},{5,4},{6,5},{7,6},{8,11},{9,8},{10,9... | collective-permute-start | bytes 147464 | tf_op jit(solution)/shard_map/ppermute | solution.py:162
  8.3 3.8 %collective-permute-start.1 = (bf16[64,384]{1,0:T(8,128)(2,1)S(1)}, bf16[64,384]{1,0:T(8,128)(2,1)S(1)}, u32[]{:S(2)}, u32[]{:S(2)}) collective-permute-start(bf16[64,384]{1,0:T(8,128)(2,1)S(1)} %pack_peaks.1.refs_0_), channel_id=1, source_target_pairs={{0,2},{1,3},{2,0},{3,1},{4,6},{5,7},{6,4},{7,5},{8,10},{9,11},{10,... | collective-permute-start | bytes 147464 | tf_op jit(solution)/shard_map/ppermute | solution.py:162
  8.3 4.8 %collective-permute-start = (bf16[64,384]{1,0:T(8,128)(2,1)S(1)}, bf16[64,384]{1,0:T(8,128)(2,1)S(1)}, u32[]{:S(2)}, u32[]{:S(2)}) collective-permute-start(bf16[64,384]{1,0:T(8,128)(2,1)S(1)} %pack_peaks.1.refs_0_), channel_id=1, source_target_pairs={{0,1},{1,2},{2,3},{3,0},{4,5},{5,6},{6,7},{7,4},{8,9},{9,10},{10,1... | collective-permute-start | bytes 147464 | tf_op jit(solution)/shard_map/ppermute | solution.py:162
  8.6 10.7 %copy-start.2 = (bf16[768,2048]{1,0:T(8,128)(2,1)S(1)}, bf16[768,2048]{1,0:T(8,128)(2,1)}, u32[]{:S(2)}) copy-start(bf16[768,2048]{1,0:T(8,128)(2,1)} %param.7) | copy-start | bytes 9437188
  20.4 30.8 %copy-start.3 = (bf16[2048,768]{1,0:T(8,128)(2,1)S(1)}, bf16[2048,768]{1,0:T(8,128)(2,1)}, u32[]{:S(2)}) copy-start(bf16[2048,768]{1,0:T(8,128)(2,1)} %param.9) | copy-start | bytes 9437188
  20.4 35.4 %copy-start.4 = (f32[2048]{0:T(1024)S(1)}, f32[2048]{0:T(1024)}, u32[]{:S(2)}) copy-start(f32[2048]{0:T(1024)} %param.8) | copy-start | bytes 24580
  44.3 10.3 %collective-permute-start.6 = (bf16[8,2048]{1,0:T(8,128)(2,1)S(1)}, bf16[8,2048]{1,0:T(8,128)(2,1)S(1)}, u32[]{:S(2)}, u32[]{:S(2)}) collective-permute-start(bf16[8,2048]{1,0:T(8,128)(2,1)S(1)} %sum_parts.2), channel_id=1, source_target_pairs={{0,34},{2,0},{32,2},{34,32},{1,35},{3,1},{33,3},{35,33},{4,38},{6,... | collective-permute-start | bytes 98312 | tf_op jit(solution)/shard_map/ppermute | solution.py:162
  49.0 5.7 %collective-permute-start.5 = (bf16[8,2048]{1,0:T(8,128)(2,1)S(1)}, bf16[8,2048]{1,0:T(8,128)(2,1)S(1)}, u32[]{:S(2)}, u32[]{:S(2)}) collective-permute-start(bf16[8,2048]{1,0:T(8,128)(2,1)S(1)} %sum_parts.2), channel_id=1, source_target_pairs={{0,2},{2,32},{32,34},{34,0},{1,3},{3,33},{33,35},{35,1},{4,6},{6,3... | collective-permute-start | bytes 98312 | tf_op jit(solution)/shard_map/ppermute | solution.py:162
  49.0 6.8 %collective-permute-start.4 = (bf16[8,2048]{1,0:T(8,128)(2,1)S(1)}, bf16[8,2048]{1,0:T(8,128)(2,1)S(1)}, u32[]{:S(2)}, u32[]{:S(2)}) collective-permute-start(bf16[8,2048]{1,0:T(8,128)(2,1)S(1)} %sum_parts.2), channel_id=1, source_target_pairs={{0,32},{2,34},{32,0},{34,2},{1,33},{3,35},{33,1},{35,3},{4,36},{6,... | collective-permute-start | bytes 98312 | tf_op jit(solution)/shard_map/ppermute | solution.py:162
  51.2 26.6 %collective-permute-start.7 = (bf16[2048,768]{1,0:T(8,128)(2,1)S(1)}, bf16[2048,768]{1,0:T(8,128)(2,1)S(1)}, u32[]{:S(2)}, u32[]{:S(2)}) collective-permute-start(bf16[2048,768]{1,0:T(8,128)(2,1)S(1)} %copy-done.3), channel_id=1, source_target_pairs={{0,4},{4,0},{1,5},{5,1},{2,6},{6,2},{3,7},{7,3},{8,12},{12,8},{9,1... | collective-permute-start | bytes 9437192 | tf_op jit(solution)/shard_map/ppermute | solution.py:156
  82.5 19.8 %all-to-all-start.2 = ((bf16[32,8,2048]{2,1,0:T(8,128)(2,1)}), bf16[32,8,2048]{2,1,0:T(8,128)(2,1)S(1)}, u32[]{:S(2)}, u32[]{:S(2)}) async-start(bf16[32,8,2048]{2,1,0:T(8,128)(2,1)} %fusion.2), calls=%async_computation.2 | async-start | bytes 2097152 | tf_op jit(solution)/shard_map/all_to_all | solution.py:168
  86.5 6.4 %collective-permute-start.8 = (bf16[256,2048]{1,0:T(8,128)(2,1)S(1)}, bf16[256,2048]{1,0:T(8,128)(2,1)S(1)}, u32[]{:S(2)}, u32[]{:S(2)}) collective-permute-start(bf16[256,2048]{1,0:T(8,128)(2,1)S(1)} %bitcast.31), channel_id=1, source_target_pairs={{0,4},{4,0},{1,5},{5,1},{2,6},{6,2},{3,7},{7,3},{8,12},{12,8},{9,1... | collective-permute-start | bytes 3145736 | tf_op jit(solution)/shard_map/ppermute | solution.py:156
  89.4 3.5 %collective-permute-start.9 = (bf16[256,768]{1,0:T(8,128)(2,1)}, bf16[256,768]{1,0:T(8,128)(2,1)S(1)}, u32[]{:S(2)}, u32[]{:S(2)}) collective-permute-start(bf16[256,768]{1,0:T(8,128)(2,1)} %fusion.7), channel_id=1, source_target_pairs={{0,4},{4,0},{1,5},{5,1},{2,6},{6,2},{3,7},{7,3},{8,12},{12,8},{9,1... | collective-permute-start | bytes 1179656 | tf_op jit(solution)/shard_map/ppermute | solution.py:156
  89.5 7.9 %collective-permute-start.10 = (bf16[256,768]{1,0:T(8,128)(2,1)S(1)}, bf16[256,768]{1,0:T(8,128)(2,1)S(1)}, u32[]{:S(2)}, u32[]{:S(2)}) collective-permute-start(bf16[256,768]{1,0:T(8,128)(2,1)S(1)} %get-tuple-element.10), channel_id=1, source_target_pairs={{0,4},{4,0},{1,5},{5,1},{2,6},{6,2},{3,7},{7,3},{8,12},{12,8},{9,1... | collective-permute-start | bytes 1179656 | tf_op jit(solution)/shard_map/ppermute | solution.py:156
  102.5 5.7 %collective-permute-start.13 = (bf16[8,2048]{1,0:T(8,128)(2,1)S(1)}, bf16[8,2048]{1,0:T(8,128)(2,1)S(1)}, u32[]{:S(2)}, u32[]{:S(2)}) collective-permute-start(bf16[8,2048]{1,0:T(8,128)(2,1)S(1)} %sum_parts.3), channel_id=1, source_target_pairs={{0,34},{2,0},{32,2},{34,32},{1,35},{3,1},{33,3},{35,33},{4,38},{6,... | collective-permute-start | bytes 98312 | tf_op jit(solution)/shard_map/ppermute | solution.py:162
  106.1 4.9 %collective-permute-start.12 = (bf16[8,2048]{1,0:T(8,128)(2,1)S(1)}, bf16[8,2048]{1,0:T(8,128)(2,1)S(1)}, u32[]{:S(2)}, u32[]{:S(2)}) collective-permute-start(bf16[8,2048]{1,0:T(8,128)(2,1)S(1)} %sum_parts.3), channel_id=1, source_target_pairs={{0,2},{2,32},{32,34},{34,0},{1,3},{3,33},{33,35},{35,1},{4,6},{6,3... | collective-permute-start | bytes 98312 | tf_op jit(solution)/shard_map/ppermute | solution.py:162
  106.1 6.9 %collective-permute-start.11 = (bf16[8,2048]{1,0:T(8,128)(2,1)S(1)}, bf16[8,2048]{1,0:T(8,128)(2,1)S(1)}, u32[]{:S(2)}, u32[]{:S(2)}) collective-permute-start(bf16[8,2048]{1,0:T(8,128)(2,1)S(1)} %sum_parts.3), channel_id=1, source_target_pairs={{0,32},{2,34},{32,0},{34,2},{1,33},{3,35},{33,1},{35,3},{4,36},{6,... | collective-permute-start | bytes 98312 | tf_op jit(solution)/shard_map/ppermute | solution.py:162
  131.4 5.9 %collective-permute-start.14 = (bf16[256,2048]{1,0:T(8,128)(2,1)S(1)}, bf16[256,2048]{1,0:T(8,128)(2,1)S(1)}, u32[]{:S(2)}, u32[]{:S(2)}) collective-permute-start(bf16[256,2048]{1,0:T(8,128)(2,1)S(1)} %bitcast.30), channel_id=1, source_target_pairs={{0,4},{4,0},{1,5},{5,1},{2,6},{6,2},{3,7},{7,3},{8,12},{12,8},{9,1... | collective-permute-start | bytes 3145736 | tf_op jit(solution)/shard_map/ppermute | solution.py:156

commit v4 on v3

v4 whole, which is shorter than its diff:
```python
import functools

import jax
import jax.numpy as jnp
from jax import lax
from jax.experimental import pallas as pl
from jax.experimental.pallas import tpu as pltpu
from jax.sharding import Mesh
from jax.sharding import PartitionSpec as P

SHAPE = (4, 2, 4, 2, 2, 2)
NAMES = ("x", "zhi", "y", "core", "zp", "zq")
NEAR = ("x", "y", "zq")
FAR = ("zhi", "zp")
SPECTRA_AXES = ("zp", "zq")
DEPTH = ("zhi", "zp", "zq")
LANES = 128
STEP = 512
CHUNK = 512
BF16 = jnp.bfloat16
F32 = jnp.float32
SMEM_SPEC = pl.BlockSpec(memory_space=pltpu.SMEM)
VMEM_SPEC = pl.BlockSpec(memory_space=pltpu.VMEM)
HBM_SPEC = pl.BlockSpec(memory_space=pltpu.HBM)


def activation(values):
    return jax.nn.gelu(values, approximate=True)


def slope_times(pre, back):
    _, pullback = jax.vjp(activation, pre)
    return pullback(back)[0].astype(BF16)


def pack_kernel(core_ref, bins_ref, values_ref, out_hbm, out_ref, sem):
    rows, lanes = out_ref.shape
    peaks = lanes // 3
    first = pl.multiple_of(core_ref[0] * rows, rows)
    bins = bins_ref[pl.ds(first, rows), :]
    out_ref[:, :peaks] = ((bins >> 9) - 192).astype(F32).astype(BF16)
    out_ref[:, peaks : 2 * peaks] = ((bins & (STEP - 1)) - 256).astype(F32).astype(BF16)
    out_ref[:, 2 * peaks :] = values_ref[pl.ds(first, rows), :]
    copy = pltpu.make_async_copy(out_ref, out_hbm, sem)
    copy.start()
    copy.wait()


def pack_peaks(core, bins, values):
    rows, peaks = bins.shape
    packed = (rows // 2, 3 * peaks)
    whole = pl.BlockSpec(bins.shape, lambda i: (0, 0))
    return pl.pallas_call(
        pack_kernel,
        out_shape=jax.ShapeDtypeStruct(packed, BF16),
        grid=(1,),
        in_specs=[SMEM_SPEC, whole, whole],
        out_specs=HBM_SPEC,
        scratch_shapes=[pltpu.VMEM(packed, BF16), pltpu.SemaphoreType.DMA],
        compiler_params=pltpu.CompilerParams(vmem_limit_bytes=4 << 20),
        name="pack_peaks",
    )(core, bins, values)


def dense_rows(bins, values, firsts, tiles, consts):
    lane, upper, which = consts
    low = (bins & (LANES - 1)).astype(BF16)
    twice = jnp.concatenate([values, values], axis=0).astype(BF16)
    picked = []
    for first in firsts:
        local = bins - first
        inside = (local >= 0) & (local < tiles * LANES)
        high = jnp.where(inside, local >> 7, -9).astype(F32)
        high = jnp.concatenate([high, high], axis=0).astype(BF16) - upper
        for tile in range(0, tiles, 2):
            picked.append(jnp.where(high == tile, twice, jnp.zeros_like(twice)))
    left = jnp.concatenate(
        [
            jnp.concatenate(
                [jnp.where(which == row, one, jnp.zeros_like(one)) for one in picked], axis=0
            )
            for row in range(8)
        ],
        axis=1,
    )
    ones = jnp.ones((LANES, LANES), BF16)
    right = jnp.concatenate(
        [jnp.where(low[row][None, :] == lane, ones, jnp.zeros_like(ones)) for row in range(8)],
        axis=1,
    )
    return lax.dot_general(left, right, (((1,), (1,)), ((), ())), preferred_element_type=F32)


def encode_kernel(place_ref, *refs, groups):
    packed_hbm, weight_hbm = refs[:groups], refs[groups : groups + 2]
    own_hbm, pair_hbm, rows_hbm = refs[groups + 2 : groups + 5]
    packed_refs, weight_refs, own_ref, pair_ref, rows_ref, sems = refs[groups + 5 :]
    packed_in = [
        pltpu.make_async_copy(packed_hbm[k], packed_refs.at[k], sems.at[k]) for k in range(groups)
    ]
    weight_in = [
        pltpu.make_async_copy(weight_hbm[k], weight_refs.at[k], sems.at[groups + k])
        for k in range(2)
    ]
    for copy in packed_in + weight_in:
        copy.start()
    _, rows, lanes = packed_refs.shape
    peaks = lanes // 3
    tiles = own_ref.shape[1] // LANES
    firsts = (place_ref[0], place_ref[1])
    lane = lax.broadcasted_iota(jnp.int32, (LANES, 1), 0).astype(BF16)
    row16 = lax.broadcasted_iota(jnp.int32, (16, LANES), 0)
    consts = (lane, (row16 >= 8).astype(jnp.int32).astype(BF16), (row16 & 7).astype(BF16))
    for back in range(groups):
        base = lax.rem(place_ref[2] + groups - back, groups) * rows
        packed_in[back].wait()

        def step(group, carry, back=back, base=base):
            row = pl.multiple_of(group * 16, 16)
            block = packed_refs[back, pl.ds(row, 16), :].astype(F32)
            bins = (block[:, :peaks].astype(jnp.int32) + 192) * STEP
            bins = bins + block[:, peaks : 2 * peaks].astype(jnp.int32) + 256
            values = block[:, 2 * peaks :]
            sums = [
                dense_rows(bins[h : h + 8], values[h : h + 8], firsts, tiles, consts)
                for h in (0, 8)
            ]
            target = pl.multiple_of(base + row, 16)
            for ref, skip in ((own_ref, 0), (pair_ref, tiles)):
                for tile in range(tiles):
                    at = (skip + tile) * 8
                    ref[pl.ds(target, 16), tile * LANES : (tile + 1) * LANES] = jnp.concatenate(
                        [one[at : at + 8] for one in sums], axis=0
                    ).astype(BF16)
            return carry

        lax.fori_loop(0, rows // 16, step, 0, unroll=True)
    out = [
        pltpu.make_async_copy(own_ref, own_hbm, sems.at[groups + 2]),
        pltpu.make_async_copy(pair_ref, pair_hbm, sems.at[groups + 3]),
    ]
    for copy in out:
        copy.start()
    for copy in weight_in:
        copy.wait()
    parts, part_rows, columns = rows_ref.shape
    for first in range(0, columns, CHUNK):
        at = slice(first, first + CHUNK)
        total = jnp.dot(own_ref[...], weight_refs[0, :, at], preferred_element_type=F32)
        total += jnp.dot(pair_ref[...], weight_refs[1, :, at], preferred_element_type=F32)
        rows_ref[:, :, at] = total.reshape(parts, part_rows, CHUNK).astype(BF16)
        copy = pltpu.make_async_copy(
            rows_ref.at[:, :, pl.ds(first, CHUNK)],
            rows_hbm.at[:, :, pl.ds(first, CHUNK)],
            sems.at[groups + 4 + first // CHUNK],
        )
        copy.start()
        out.append(copy)
    for copy in out:
        copy.wait()


def encode_rows(place, blocks, weights, parts):
    width, columns = weights[0].shape
    groups = len(blocks)
    rows = blocks[0].shape[0] * groups
    dense = jax.ShapeDtypeStruct((rows, width), BF16)
    product = (parts, rows // parts, columns)
    return pl.pallas_call(
        functools.partial(encode_kernel, groups=groups),
        out_shape=(dense, dense, jax.ShapeDtypeStruct(product, BF16)),
        in_specs=[SMEM_SPEC] + [HBM_SPEC] * (groups + 2),
        out_specs=(HBM_SPEC,) * 3,
        scratch_shapes=[
            pltpu.VMEM((groups,) + blocks[0].shape, BF16),
            pltpu.VMEM((2, width, columns), BF16),
            pltpu.VMEM((rows, width), BF16),
            pltpu.VMEM((rows, width), BF16),
            pltpu.VMEM(product, BF16),
            pltpu.SemaphoreType.DMA((groups + 4 + columns // CHUNK,)),
        ],
        compiler_params=pltpu.CompilerParams(vmem_limit_bytes=50 << 20),
        name="encode_rows",
    )(place, *blocks, *weights)


def decode_kernel(hidden_ref, own_hbm, pair_hbm, own_w, pair_w, own_out, pair_out, rows_hbm, *scratch):
    weight_refs, dense_refs, resid_refs, total_ref, rows_ref, sems, out_sems = scratch
    chunks, hidden_size, block = weight_refs.shape
    half = chunks // 2
    dense_in = [
        pltpu.make_async_copy(source, dense_refs.at[k], sems.at[chunks + k])
        for k, source in enumerate((own_hbm, pair_hbm))
    ]
    copies = []
    for chunk in range(chunks):
        source = own_w if chunk < half else pair_w
        at = pl.ds((chunk % half) * block, block)
        copies.append(
            pltpu.make_async_copy(source.at[:, at], weight_refs.at[chunk], sems.at[chunk])
        )
    for copy in copies[:1] + dense_in + copies[1:]:
        copy.start()
    parts, part_rows, _ = rows_ref.shape
    hidden = hidden_ref[...].reshape(parts * part_rows, hidden_size)
    out = []
    for chunk in range(chunks):
        side = chunk // half
        at = slice((chunk % half) * block, (chunk % half + 1) * block)
        copies[chunk].wait()
        recon = jnp.dot(hidden, weight_refs[chunk], preferred_element_type=F32)
        if chunk % half == 0:
            dense_in[side].wait()
        resid = (recon - dense_refs[side, :, at].astype(F32)).astype(BF16)
        resid_refs[side, :, at] = resid
        if chunk % half == half - 1:
            copy = pltpu.make_async_copy(
                resid_refs.at[side], (own_out, pair_out)[side], out_sems.at[side]
            )
            copy.start()
            out.append(copy)
        for first in range(0, hidden_size, CHUNK):
            to = slice(first, first + CHUNK)
            term = lax.dot_general(
                resid,
                weight_refs[chunk, to, :],
                (((1,), (1,)), ((), ())),
                preferred_element_type=F32,
            )
            if chunk == 0:
                total_ref[:, to] = term
            elif chunk < chunks - 1:
                total_ref[:, to] += term
            else:
                total = total_ref[:, to] + term
                rows_ref[:, :, to] = total.reshape(parts, part_rows, CHUNK).astype(BF16)
                copy = pltpu.make_async_copy(
                    rows_ref.at[:, :, pl.ds(first, CHUNK)],
                    rows_hbm.at[:, :, pl.ds(first, CHUNK)],
                    out_sems.at[2 + first // CHUNK],
                )
                copy.start()
                out.append(copy)
    for copy in out:
        copy.wait()


def decode_rows(hidden, dense, weights):
    _, _, hidden_size = hidden.shape
    rows, width = dense[0].shape
    resid = jax.ShapeDtypeStruct((rows, width), BF16)
    block = 2 * LANES
    chunks = 2 * width // block
    return pl.pallas_call(
        decode_kernel,
        out_shape=(resid, resid, jax.ShapeDtypeStruct(hidden.shape, BF16)),
        in_specs=[VMEM_SPEC] + [HBM_SPEC] * 4,
        out_specs=(HBM_SPEC,) * 3,
        scratch_shapes=[
            pltpu.VMEM((chunks, hidden_size, block), BF16),
            pltpu.VMEM((2, rows, width), BF16),
            pltpu.VMEM((2, rows, width), BF16),
            pltpu.VMEM((rows, hidden_size), F32),
            pltpu.VMEM(hidden.shape, BF16),
            pltpu.SemaphoreType.DMA((chunks + 2,)),
            pltpu.SemaphoreType.DMA((2 + hidden_size // CHUNK,)),
        ],
        compiler_params=pltpu.CompilerParams(vmem_limit_bytes=50 << 20),
        name="decode_rows",
    )(hidden, *dense, *weights)


def weight_grad_kernel(own_ref, other_ref, left_ref, right_ref, out_ref):
    total = lax.dot_general(
        own_ref[...], left_ref[...], (((0,), (0,)), ((), ())), preferred_element_type=F32
    )
    total += lax.dot_general(
        other_ref[...], right_ref[...], (((0,), (0,)), ((), ())), preferred_element_type=F32
    )
    out_ref[...] = total.astype(BF16)


def weight_grad(own, other, left, right):
    rows, width = own.shape
    columns = left.shape[1]
    block = pl.BlockSpec((rows, LANES), lambda i: (0, i))
    return pl.pallas_call(
        weight_grad_kernel,
        out_shape=jax.ShapeDtypeStruct((width, columns), BF16),
        grid=(width // LANES,),
        in_specs=[block, block, VMEM_SPEC, VMEM_SPEC],
        out_specs=pl.BlockSpec((LANES, columns), lambda i: (i, 0)),
        compiler_params=pltpu.CompilerParams(vmem_limit_bytes=16 << 20),
        name="weight_grad",
    )(own, other, left, right)


def sum_kernel(parts_ref, out_ref):
    count, _, columns = parts_ref.shape
    block = 4 * LANES
    for first in range(0, columns, block):
        at = slice(first, first + block)
        total = parts_ref[0, :, at].astype(F32)
        for part in range(1, count):
            total = total + parts_ref[part, :, at].astype(F32)
        out_ref[:, at] = total.astype(out_ref.dtype)


def sum_parts(parts):
    return pl.pallas_call(
        sum_kernel,
        out_shape=jax.ShapeDtypeStruct(parts.shape[1:], BF16),
        in_specs=[VMEM_SPEC],
        out_specs=VMEM_SPEC,
        compiler_params=pltpu.CompilerParams(vmem_limit_bytes=4 << 20),
        name="sum_parts",
    )(parts)


def swap(values):
    return lax.ppermute(values, "core", [(0, 1), (1, 0)])


def from_others(values, axes, steps):
    count = lax.axis_size(axes)
    return [
        lax.ppermute(values, axes, [(i, (i + step) % count) for i in range(count)])
        for step in steps
    ]


def near_exchange(values):
    return lax.all_to_all(values, NEAR, 0, 0, tiled=True)


def far_sum(sent):
    one, two, three = [block.astype(F32) for block in from_others(sent, FAR, (1, 2, 3))]
    return (sent.astype(F32) + two) + (one + three)


def near_gather(values):
    count = lax.axis_size(NEAR)
    sent = jnp.broadcast_to(values[None], (count,) + values.shape)
    return near_exchange(sent)


def on_device(peak_bins, peak_values, enc_weight, enc_bias, dec_weight):
    width, hidden_size = enc_weight.shape
    core = lax.axis_index("core")
    group = lax.axis_index(SPECTRA_AXES)
    position = lax.axis_index(NAMES)
    stride = lax.axis_size(SPECTRA_AXES)
    partner = position + (1 - 2 * core) * stride
    place = jnp.stack([position * width, partner * width, group]).astype(jnp.int32)
    packed = pack_peaks(core.reshape(1), peak_bins, peak_values)
    enc_weights = (enc_weight, swap(enc_weight))
    dec_weights = (dec_weight, swap(dec_weight))
    peaks = [packed] + from_others(packed, DEPTH, (1, 2, -1))
    dense_own, dense_pair, rows = encode_rows(place, peaks, enc_weights, lax.axis_size(NEAR))
    dense_other = swap(dense_pair)
    pre = far_sum(sum_parts(near_exchange(rows))) + enc_bias
    hidden = near_gather(activation(pre).astype(BF16))
    resid_own, resid_pair, rows = decode_rows(hidden, (dense_own, dense_pair), dec_weights)
    parts = near_exchange(rows)
    hidden = hidden.reshape(-1, hidden_size)
    grad_dec = lax.dot_general(
        jnp.concatenate([hidden, swap(hidden)]),
        jnp.concatenate([resid_own, swap(resid_pair)]),
        (((0,), (0,)), ((), ())),
        preferred_element_type=F32,
    ).astype(BF16)
    parts, grad_dec, dense_other = lax.optimization_barrier((parts, grad_dec, dense_other))
    back = far_sum(sum_parts(parts))
    dpre = near_gather(slope_times(pre, back)).reshape(-1, hidden_size)
    grad_enc = weight_grad(dense_own, dense_other, dpre, swap(dpre))
    return (grad_enc, grad_dec)


def solution(mesh):
    fine = Mesh(mesh.devices.reshape(SHAPE), NAMES)
    placed = (
        P(SPECTRA_AXES, None),
        P(SPECTRA_AXES, None),
        P(NAMES, None),
        P(),
        P(None, NAMES),
    )
    return jax.shard_map(
        on_device,
        mesh=fine,
        in_specs=placed,
        out_specs=(P(NAMES, None), P(None, NAMES)),
        check_vma=False,
    )
```

time: 142 us -> 147 us (1.035)
  blocking collectives: 61 us -> 19.7 us
  waiting for transfers between devices: 19.4 us -> 51.9 us
  Pallas kernels: 3.63 us -> 22.2 us
  matrix products: 18 us -> 4.5 us
  starting transfers between devices: 33.4 us -> 44 us
  other arithmetic: 2.92 us -> 0.21 us
  local copies, waits for them, and re-layouts: 1.83 us -> 3.55 us
    all_to_all x3 -> x1, blocking collectives: 61 us -> 19.7 us  [near_exchange(): return lax.all_to_all(values, NEAR, 0, 0, tiled=True)]
    all_to_all x1 -> x3, waiting for transfers between devices: 4.94 us -> 34.3 us  [near_exchange(): return lax.all_to_all(values, NEAR, 0, 0, tiled=True)]
    pallas_call x2 -> x4, Pallas kernels: 3.34 us -> 21.9 us  [the longest x1 10.5 us: decode_rows(): pl.pallas_call(decode_kernel, out_shape=(resid, resid, jax.ShapeDtypeStru...]
    dot_general x9 -> x1, matrix products: 18 us -> 4.5 us  [on_device(): lax.dot_general(jnp.concatenate([hidden, swap(hidden)]), jnp.concatenate(...]
    all_to_all x1 -> x3, starting transfers between devices: 3.93 us -> 15.1 us  [near_exchange(): return lax.all_to_all(values, NEAR, 0, 0, tiled=True)]
    convert_element_type x1 -> x0, other arithmetic: 2.7 us -> none  [on_device(): grad_enc = (grad_own + rows_dot(dense_other, dpre_other)).astype(BF16)]
    ppermute x6, starting transfers between devices: 13.9 us -> 11.7 us  [swap(): return lax.ppermute(values, 'core', [(0, 1), (1, 0)])]
    ppermute x9, waiting for transfers between devices: 10.2 us -> 12.4 us  [from_others(): lax.ppermute(values, axes, [(i, (i + step) % count) for i in range(count)])]
  transfers between devices with their start and end apart: 16 -> 18, of which waited for: 9 -> 11; matrix products, arithmetic and copies ran while one was open for 6% -> 4% of each run, Pallas kernels for 2% -> 0%
where the time goes in v4:
time: 147 us
  waiting for transfers between devices  51.9 us (35%)
  starting transfers between devices  44 us (30%)
  Pallas kernels  22.2 us (15%)
  blocking collectives  19.7 us (13%)
  matrix products  4.5 us (3%)
  local copies, waits for them, and re-layouts  3.55 us (2%)
    all_to_all x3, waiting for transfers between devices, near_exchange(): return lax.all_to_all(values, NEAR, 0, 0, tiled=True)  34.3 us
    all_to_all x1, blocking collectives, near_exchange(): return lax.all_to_all(values, NEAR, 0, 0, tiled=True)  19.7 us
    ppermute x9, starting transfers between devices, from_others(): lax.ppermute(values, axes, [(i, (i + step) % count) for i in range(count)])  17.2 us
    all_to_all x3, starting transfers between devices, near_exchange(): return lax.all_to_all(values, NEAR, 0, 0, tiled=True)  15.1 us
    ppermute x9, waiting for transfers between devices, from_others(): lax.ppermute(values, axes, [(i, (i + step) % count) for i in range(count)])  12.4 us
    ppermute x6, starting transfers between devices, swap(): return lax.ppermute(values, 'core', [(0, 1), (1, 0)])  11.7 us
    pallas_call x1, Pallas kernels, decode_rows(): pl.pallas_call(decode_kernel, out_shape=(resid, resid, jax.ShapeDtypeStru...  10.5 us
    pallas_call x1, Pallas kernels, encode_rows(): pl.pallas_call(functools.partial(encode_kernel, groups=groups), out_shape...  7 us
  transfers between devices with their start and end apart: 18, of which 11 were waited for; matrix products, arithmetic and copies ran while one was open for 4% of the time, Pallas kernels for 0%

profile of v4, /device:TPU:1, one launch (start us, length us, event | category | flops | bytes accessed | tf_op | source)
XLA Modules:
  0.0 146.8 jit_solution(15509476881777889860)
XLA Ops:
  0.6 3.3 %collective-permute-start.3 = (bf16[768,2048]{1,0:T(8,128)(2,1)}, bf16[768,2048]{1,0:T(8,128)(2,1)}, u32[]{:S(2)}, u32[]{:S(2)}) collective-permute-start(bf16[768,2048]{1,0:T(8,128)(2,1)} %refs_4_.1), channel_id=1, source_target_pairs={{0,4},{4,0},{1,5},{5,1},{2,6},{6,2},{3,7},{7,3},{8,12},{12,8},{9,1... | collective-permute-start | bytes 9437192 | tf_op jit(solution)/shard_map/ppermute | solution.py:321
  4.0 0.8 copy-done
  4.8 0.8 copy-done.1
  5.6 0.1 pack_peaks.1.refs_0_
  5.6 3.9 %collective-permute-start.2 = (bf16[64,384]{1,0:T(8,128)(2,1)S(1)}, bf16[64,384]{1,0:T(8,128)(2,1)S(1)}, u32[]{:S(2)}, u32[]{:S(2)}) collective-permute-start(bf16[64,384]{1,0:T(8,128)(2,1)S(1)} %pack_peaks.1.refs_0_), channel_id=1, source_target_pairs={{0,35},{1,0},{2,1},{3,2},{32,3},{33,32},{34,33},{35,34},{4,39},{5,... | collective-permute-start | bytes 147464 | tf_op jit(solution)/shard_map/ppermute | solution.py:327
  9.6 0.0 collective-permute-start.1
  9.6 0.0 collective-permute-start
  9.6 0.1 pad_add_fusion.place_ref
  9.6 1.1 collective-permute-done.2.refs_3_
  10.7 4.8 %collective-permute-done.1.refs_2_ = bf16[64,384]{1,0:T(8,128)(2,1)S(1)} collective-permute-done((bf16[64,384]{1,0:T(8,128)(2,1)S(1)}, bf16[64,384]{1,0:T(8,128)(2,1)S(1)}, u32[]{:S(2)}, u32[]{:S(2)}) %collective-permute-start.1) | collective-permute-done | bytes 49184 | tf_op jit(solution)/shard_map/ppermute | solution.py:327
  15.5 0.0 collective-permute-done.refs_1_
  15.5 7.0 %encode_rows.1 = (bf16[256,768]{1,0:T(8,128)(2,1)S(1)}, bf16[256,768]{1,0:T(8,128)(2,1)S(1)}, bf16[32,8,2048]{2,1,0:T(8,128)(2,1)}) custom-call(s32[3]{0:T(128)S(1)} %pad_add_fusion.place_ref, bf16[64,384]{1,0:T(8,128)(2,1)S(1)} %pack_peaks.1.refs_0_, bf16[64,384]{1,0:T(8,128)(2,1)S(1)} %collective-permute-done.refs_1_, ...), custom_call_target="tpu_custom_call" | custom-call | tf_op jit(solution)/shard_map/encode_rows/pallas_call | solution.py:169
  22.5 0.0 copy-start.4
  22.5 7.1 %all-to-all-start = ((bf16[32,8,2048]{2,1,0:T(8,128)(2,1)}), bf16[32,8,2048]{2,1,0:T(8,128)(2,1)S(1)}, u32[]{:S(2)}, u32[]{:S(2)}) async-start(bf16[32,8,2048]{2,1,0:T(8,128)(2,1)} %get-tuple-element.12), calls=%async_computation | async-start | bytes 2097152 | tf_op jit(solution)/shard_map/all_to_all | solution.py:333
  29.6 1.6 %collective-permute-start.7 = (bf16[2048,768]{1,0:T(8,128)(2,1)}, bf16[2048,768]{1,0:T(8,128)(2,1)}, u32[]{:S(2)}, u32[]{:S(2)}) collective-permute-start(bf16[2048,768]{1,0:T(8,128)(2,1)} %own_w.1), channel_id=1, source_target_pairs={{0,4},{4,0},{1,5},{5,1},{2,6},{6,2},{3,7},{7,3},{8,12},{12,8},{9,1... | collective-permute-start | bytes 9437192 | tf_op jit(solution)/shard_map/ppermute | solution.py:321
  31.2 14.5 %all-to-all-done.parts_ref = bf16[32,8,2048]{2,1,0:T(8,128)(2,1)S(1)} async-done(((bf16[32,8,2048]{2,1,0:T(8,128)(2,1)}), bf16[32,8,2048]{2,1,0:T(8,128)(2,1)S(1)}, u32[]{:S(2)}, u32[]{:S(2)}) %all-to-all-start) | async-done | bytes 1048608 | tf_op jit(solution)/shard_map/all_to_all | solution.py:333
  45.7 0.1 sum_parts.2
  45.9 2.7 %collective-permute-start.6 = (bf16[8,2048]{1,0:T(8,128)(2,1)S(1)}, bf16[8,2048]{1,0:T(8,128)(2,1)S(1)}, u32[]{:S(2)}, u32[]{:S(2)}) collective-permute-start(bf16[8,2048]{1,0:T(8,128)(2,1)S(1)} %sum_parts.2), channel_id=1, source_target_pairs={{0,34},{2,0},{32,2},{34,32},{1,35},{3,1},{33,3},{35,33},{4,38},{6,... | collective-permute-start | bytes 98312 | tf_op jit(solution)/shard_map/ppermute | solution.py:327
  48.6 3.8 %collective-permute-start.4 = (bf16[8,2048]{1,0:T(8,128)(2,1)S(1)}, bf16[8,2048]{1,0:T(8,128)(2,1)S(1)}, u32[]{:S(2)}, u32[]{:S(2)}) collective-permute-start(bf16[8,2048]{1,0:T(8,128)(2,1)S(1)} %sum_parts.2), channel_id=1, source_target_pairs={{0,32},{2,34},{32,0},{34,2},{1,33},{3,35},{33,1},{35,3},{4,36},{6,... | collective-permute-start | bytes 98312 | tf_op jit(solution)/shard_map/ppermute | solution.py:327
  52.5 0.0 collective-permute-done.6
  52.5 1.0 collective-permute-done.5
  53.5 1.9 %collective-permute-done.4 = bf16[8,2048]{1,0:T(8,128)(2,1)S(1)} collective-permute-done((bf16[8,2048]{1,0:T(8,128)(2,1)S(1)}, bf16[8,2048]{1,0:T(8,128)(2,1)S(1)}, u32[]{:S(2)}, u32[]{:S(2)}) %collective-permute-start.4) | collective-permute-done | bytes 32800 | tf_op jit(solution)/shard_map/ppermute | solution.py:327
  55.5 1.1 broadcast_in_dim.4
  56.5 4.1 %all-to-all-start.1 = ((bf16[32,8,2048]{2,1,0:T(8,128)(2,1)}), bf16[32,8,2048]{2,1,0:T(8,128)(2,1)S(1)}, u32[]{:S(2)}, u32[]{:S(2)}) async-start(bf16[32,8,2048]{2,1,0:T(8,128)(2,1)} %broadcast_in_dim.4), calls=%async_computation.1 | async-start | bytes 2097152 | tf_op jit(solution)/shard_map/all_to_all | solution.py:333
  60.7 0.0 collective-permute-done.7.pair_w
  60.7 15.3 %all-to-all-done.1.hidden_ref = bf16[32,8,2048]{2,1,0:T(8,128)(2,1)S(1)} async-done(((bf16[32,8,2048]{2,1,0:T(8,128)(2,1)}), bf16[32,8,2048]{2,1,0:T(8,128)(2,1)S(1)}, u32[]{:S(2)}, u32[]{:S(2)}) %all-to-all-start.1) | async-done | bytes 1048608 | tf_op jit(solution)/shard_map/all_to_all | solution.py:333
  75.9 10.5 %decode_rows.1 = (bf16[256,768]{1,0:T(8,128)(2,1)S(1)}, bf16[256,768]{1,0:T(8,128)(2,1)S(1)}, bf16[32,8,2048]{2,1,0:T(8,128)(2,1)}) custom-call(bf16[32,8,2048]{2,1,0:T(8,128)(2,1)S(1)} %all-to-all-done.1.hidden_ref, bf16[256,768]{1,0:T(8,128)(2,1)S(1)} %get-tuple-element.11.own_hbm.own_ref, bf16[256,768]{1,0:T(8,128)(2,1)S(1)} %get-tuple-element.13.pair_hbm, ...), custom_call_target="tpu_custom_call" | custom-call | tf_op jit(solution)/shard_map/decode_rows/pallas_call | solution.py:254
  86.4 0.0 copy-start.3
  86.4 0.7 copy-done.3
  87.2 3.9 %all-to-all-start.2 = ((bf16[32,8,2048]{2,1,0:T(8,128)(2,1)}), bf16[32,8,2048]{2,1,0:T(8,128)(2,1)S(1)}, u32[]{:S(2)}, u32[]{:S(2)}) async-start(bf16[32,8,2048]{2,1,0:T(8,128)(2,1)} %get-tuple-element.14), calls=%async_computation.2 | async-start | bytes 2097152 | tf_op jit(solution)/shard_map/all_to_all | solution.py:333
  91.1 3.4 %collective-permute-start.8 = (bf16[256,2048]{1,0:T(8,128)(2,1)S(1)}, bf16[256,2048]{1,0:T(8,128)(2,1)S(1)}, u32[]{:S(2)}, u32[]{:S(2)}) collective-permute-start(bf16[256,2048]{1,0:T(8,128)(2,1)S(1)} %bitcast.8), channel_id=1, source_target_pairs={{0,4},{4,0},{1,5},{5,1},{2,6},{6,2},{3,7},{7,3},{8,12},{12,8},{9,1... | collective-permute-start | bytes 3145736 | tf_op jit(solution)/shard_map/ppermute | solution.py:321
  94.5 0.1 collective-permute-start.9
  94.6 0.4 collective-permute-start.10
  95.0 3.0 %collective-permute-done.9 = bf16[256,768]{1,0:T(8,128)(2,1)S(1)} collective-permute-done((bf16[256,768]{1,0:T(8,128)(2,1)}, bf16[256,768]{1,0:T(8,128)(2,1)S(1)}, u32[]{:S(2)}, u32[]{:S(2)}) %collective-permute-start.9) | collective-permute-done | bytes 393248 | tf_op jit(solution)/shard_map/ppermute | solution.py:321
  98.0 0.0 collective-permute-done.8
  98.0 4.5 %convolution_convert_fusion = bf16[2048,768]{1,0:T(8,128)(2,1)} fusion(bf16[256,2048]{1,0:T(8,128)(2,1)S(1)} %collective-permute-done.8, bf16[256,2048]{1,0:T(8,128)(2,1)S(1)} %bitcast.9, bf16[256,768]{1,0:T(8,128)(2,1)S(1)} %collective-permute-done.9, bf16[256,768]{1,0:T(8,128)(2,1)} %copy-done.2), kind=kOutput, calls=%fused_computation | convolution fusion | flops 1617952768 | bytes 6029312 | tf_op jit(solution)/shard_map/dot_general | solution.py:366
  102.5 4.5 %all-to-all-done.2.parts_ref = bf16[32,8,2048]{2,1,0:T(8,128)(2,1)S(1)} async-done(((bf16[32,8,2048]{2,1,0:T(8,128)(2,1)}), bf16[32,8,2048]{2,1,0:T(8,128)(2,1)S(1)}, u32[]{:S(2)}, u32[]{:S(2)}) %all-to-all-start.2) | async-done | bytes 1048608 | tf_op jit(solution)/shard_map/all_to_all | solution.py:333
  107.0 0.1 sum_parts.3
  107.1 3.6 %collective-permute-start.13 = (bf16[8,2048]{1,0:T(8,128)(2,1)S(1)}, bf16[8,2048]{1,0:T(8,128)(2,1)S(1)}, u32[]{:S(2)}, u32[]{:S(2)}) collective-permute-start(bf16[8,2048]{1,0:T(8,128)(2,1)S(1)} %sum_parts.3), channel_id=1, source_target_pairs={{0,34},{2,0},{32,2},{34,32},{1,35},{3,1},{33,3},{35,33},{4,38},{6,... | collective-permute-start | bytes 98312 | tf_op jit(solution)/shard_map/ppermute | solution.py:327
  110.7 3.1 %collective-permute-start.11 = (bf16[8,2048]{1,0:T(8,128)(2,1)S(1)}, bf16[8,2048]{1,0:T(8,128)(2,1)S(1)}, u32[]{:S(2)}, u32[]{:S(2)}) collective-permute-start(bf16[8,2048]{1,0:T(8,128)(2,1)S(1)} %sum_parts.3), channel_id=1, source_target_pairs={{0,32},{2,34},{32,0},{34,2},{1,33},{3,35},{33,1},{35,3},{4,36},{6,... | collective-permute-start | bytes 98312 | tf_op jit(solution)/shard_map/ppermute | solution.py:327
  113.8 1.7 %collective-permute-done.12 = bf16[8,2048]{1,0:T(8,128)(2,1)S(1)} collective-permute-done((bf16[8,2048]{1,0:T(8,128)(2,1)S(1)}, bf16[8,2048]{1,0:T(8,128)(2,1)S(1)}, u32[]{:S(2)}, u32[]{:S(2)}) %collective-permute-start.12) | collective-permute-done | bytes 32800 | tf_op jit(solution)/shard_map/ppermute | solution.py:327
  115.6 1.8 %collective-permute-done.11 = bf16[8,2048]{1,0:T(8,128)(2,1)S(1)} collective-permute-done((bf16[8,2048]{1,0:T(8,128)(2,1)S(1)}, bf16[8,2048]{1,0:T(8,128)(2,1)S(1)}, u32[]{:S(2)}, u32[]{:S(2)}) %collective-permute-start.11) | collective-permute-done | bytes 32800 | tf_op jit(solution)/shard_map/ppermute | solution.py:327
  117.4 0.1 fusion.12
  117.5 0.1 broadcast_in_dim.5
  117.6 19.7 %all_to_all.20 = bf16[32,8,2048]{2,1,0:T(8,128)(2,1)S(1)} all-to-all(bf16[32,8,2048]{2,1,0:T(8,128)(2,1)S(1)} %broadcast_in_dim.5), channel_id=1, replica_groups=mesh['x'=4,'zhi'=2,'y'=4,'core'=2,'zp'=2,'zq'=2] {'x','y','zq'}, dimensions={0} | all-to-all | bytes 2097152 | tf_op jit(solution)/shard_map/all_to_all | solution.py:333
  137.3 2.8 %collective-permute-start.14 = (bf16[256,2048]{1,0:T(8,128)(2,1)S(1)}, bf16[256,2048]{1,0:T(8,128)(2,1)S(1)}, u32[]{:S(2)}, u32[]{:S(2)}) collective-permute-start(bf16[256,2048]{1,0:T(8,128)(2,1)S(1)} %bitcast.6), channel_id=1, source_target_pairs={{0,4},{4,0},{1,5},{5,1},{2,6},{6,2},{3,7},{7,3},{8,12},{12,8},{9,1... | collective-permute-start | bytes 3145736 | tf_op jit(solution)/shard_map/ppermute | solution.py:321
  140.1 2.3 %collective-permute-done.14.right_ref = bf16[256,2048]{1,0:T(8,128)(2,1)S(1)} collective-permute-done((bf16[256,2048]{1,0:T(8,128)(2,1)S(1)}, bf16[256,2048]{1,0:T(8,128)(2,1)S(1)}, u32[]{:S(2)}, u32[]{:S(2)}) %collective-permute-start.14) | collective-permute-done | bytes 1048608 | tf_op jit(solution)/shard_map/ppermute | solution.py:321
  142.4 4.4 %weight_grad.1 = bf16[768,2048]{1,0:T(8,128)(2,1)} custom-call(bf16[256,768]{1,0:T(8,128)(2,1)S(1)} %get-tuple-element.11.own_hbm.own_ref, bf16[256,768]{1,0:T(8,128)(2,1)S(1)} %collective-permute-done.10.other_ref, bf16[256,2048]{1,0:T(8,128)(2,1)S(1)} %bitcast.7, bf16[256,2048]{1,0:T(8,128)(2,1)S(1)} %collective-permute-done.14.right_ref), custom_call_target="tpu_custom_call" | custom-call | tf_op jit(solution)/shard_map/weight_grad/pallas_call | solution.py:287
  (11 shorter events, 0.1 us)
Async XLA Ops:
  0.6 14.9 %collective-permute-start.3 = (bf16[768,2048]{1,0:T(8,128)(2,1)}, bf16[768,2048]{1,0:T(8,128)(2,1)}, u32[]{:S(2)}, u32[]{:S(2)}) collective-permute-start(bf16[768,2048]{1,0:T(8,128)(2,1)} %refs_4_.1), channel_id=1, source_target_pairs={{0,4},{4,0},{1,5},{5,1},{2,6},{6,2},{3,7},{7,3},{8,12},{12,8},{9,1... | collective-permute-start | bytes 9437192 | tf_op jit(solution)/shard_map/ppermute | solution.py:321
  4.0 0.8 copy-start
  4.8 0.8 copy-start.1
  5.6 5.1 %collective-permute-start.2 = (bf16[64,384]{1,0:T(8,128)(2,1)S(1)}, bf16[64,384]{1,0:T(8,128)(2,1)S(1)}, u32[]{:S(2)}, u32[]{:S(2)}) collective-permute-start(bf16[64,384]{1,0:T(8,128)(2,1)S(1)} %pack_peaks.1.refs_0_), channel_id=1, source_target_pairs={{0,35},{1,0},{2,1},{3,2},{32,3},{33,32},{34,33},{35,34},{4,39},{5,... | collective-permute-start | bytes 147464 | tf_op jit(solution)/shard_map/ppermute | solution.py:327
  9.6 6.0 %collective-permute-start.1 = (bf16[64,384]{1,0:T(8,128)(2,1)S(1)}, bf16[64,384]{1,0:T(8,128)(2,1)S(1)}, u32[]{:S(2)}, u32[]{:S(2)}) collective-permute-start(bf16[64,384]{1,0:T(8,128)(2,1)S(1)} %pack_peaks.1.refs_0_), channel_id=1, source_target_pairs={{0,2},{1,3},{2,32},{3,33},{32,34},{33,35},{34,0},{35,1},{4,6},{5,7... | collective-permute-start | bytes 147464 | tf_op jit(solution)/shard_map/ppermute | solution.py:327
  9.6 6.0 %collective-permute-start = (bf16[64,384]{1,0:T(8,128)(2,1)S(1)}, bf16[64,384]{1,0:T(8,128)(2,1)S(1)}, u32[]{:S(2)}, u32[]{:S(2)}) collective-permute-start(bf16[64,384]{1,0:T(8,128)(2,1)S(1)} %pack_peaks.1.refs_0_), channel_id=1, source_target_pairs={{0,1},{1,2},{2,3},{3,32},{32,33},{33,34},{34,35},{35,0},{4,5},{5,6... | collective-permute-start | bytes 147464 | tf_op jit(solution)/shard_map/ppermute | solution.py:327
  22.5 32.9 %copy-start.4 = (f32[2048]{0:T(1024)S(1)}, f32[2048]{0:T(1024)}, u32[]{:S(2)}) copy-start(f32[2048]{0:T(1024)} %param.8) | copy-start | bytes 24580
  22.5 23.2 %all-to-all-start = ((bf16[32,8,2048]{2,1,0:T(8,128)(2,1)}), bf16[32,8,2048]{2,1,0:T(8,128)(2,1)S(1)}, u32[]{:S(2)}, u32[]{:S(2)}) async-start(bf16[32,8,2048]{2,1,0:T(8,128)(2,1)} %get-tuple-element.12), calls=%async_computation | async-start | bytes 2097152 | tf_op jit(solution)/shard_map/all_to_all | solution.py:333
  29.6 31.1 %collective-permute-start.7 = (bf16[2048,768]{1,0:T(8,128)(2,1)}, bf16[2048,768]{1,0:T(8,128)(2,1)}, u32[]{:S(2)}, u32[]{:S(2)}) collective-permute-start(bf16[2048,768]{1,0:T(8,128)(2,1)} %own_w.1), channel_id=1, source_target_pairs={{0,4},{4,0},{1,5},{5,1},{2,6},{6,2},{3,7},{7,3},{8,12},{12,8},{9,1... | collective-permute-start | bytes 9437192 | tf_op jit(solution)/shard_map/ppermute | solution.py:321
  45.9 6.6 %collective-permute-start.6 = (bf16[8,2048]{1,0:T(8,128)(2,1)S(1)}, bf16[8,2048]{1,0:T(8,128)(2,1)S(1)}, u32[]{:S(2)}, u32[]{:S(2)}) collective-permute-start(bf16[8,2048]{1,0:T(8,128)(2,1)S(1)} %sum_parts.2), channel_id=1, source_target_pairs={{0,34},{2,0},{32,2},{34,32},{1,35},{3,1},{33,3},{35,33},{4,38},{6,... | collective-permute-start | bytes 98312 | tf_op jit(solution)/shard_map/ppermute | solution.py:327
  48.6 4.9 %collective-permute-start.5 = (bf16[8,2048]{1,0:T(8,128)(2,1)S(1)}, bf16[8,2048]{1,0:T(8,128)(2,1)S(1)}, u32[]{:S(2)}, u32[]{:S(2)}) collective-permute-start(bf16[8,2048]{1,0:T(8,128)(2,1)S(1)} %sum_parts.2), channel_id=1, source_target_pairs={{0,2},{2,32},{32,34},{34,0},{1,3},{3,33},{33,35},{35,1},{4,6},{6,3... | collective-permute-start | bytes 98312 | tf_op jit(solution)/shard_map/ppermute | solution.py:327
  48.6 6.8 %collective-permute-start.4 = (bf16[8,2048]{1,0:T(8,128)(2,1)S(1)}, bf16[8,2048]{1,0:T(8,128)(2,1)S(1)}, u32[]{:S(2)}, u32[]{:S(2)}) collective-permute-start(bf16[8,2048]{1,0:T(8,128)(2,1)S(1)} %sum_parts.2), channel_id=1, source_target_pairs={{0,32},{2,34},{32,0},{34,2},{1,33},{3,35},{33,1},{35,3},{4,36},{6,... | collective-permute-start | bytes 98312 | tf_op jit(solution)/shard_map/ppermute | solution.py:327
  56.5 19.4 %all-to-all-start.1 = ((bf16[32,8,2048]{2,1,0:T(8,128)(2,1)}), bf16[32,8,2048]{2,1,0:T(8,128)(2,1)S(1)}, u32[]{:S(2)}, u32[]{:S(2)}) async-start(bf16[32,8,2048]{2,1,0:T(8,128)(2,1)} %broadcast_in_dim.4), calls=%async_computation.1 | async-start | bytes 2097152 | tf_op jit(solution)/shard_map/all_to_all | solution.py:333
  86.4 0.7 copy-start.3
  87.2 7.4 %copy-start.2 = (bf16[256,768]{1,0:T(8,128)(2,1)}, bf16[256,768]{1,0:T(8,128)(2,1)S(1)}, u32[]{:S(2)}) copy-start(bf16[256,768]{1,0:T(8,128)(2,1)S(1)} %get-tuple-element.15) | copy-start | bytes 1179652
  87.2 19.8 %all-to-all-start.2 = ((bf16[32,8,2048]{2,1,0:T(8,128)(2,1)}), bf16[32,8,2048]{2,1,0:T(8,128)(2,1)S(1)}, u32[]{:S(2)}, u32[]{:S(2)}) async-start(bf16[32,8,2048]{2,1,0:T(8,128)(2,1)} %get-tuple-element.14), calls=%async_computation.2 | async-start | bytes 2097152 | tf_op jit(solution)/shard_map/all_to_all | solution.py:333
  91.1 6.9 %collective-permute-start.8 = (bf16[256,2048]{1,0:T(8,128)(2,1)S(1)}, bf16[256,2048]{1,0:T(8,128)(2,1)S(1)}, u32[]{:S(2)}, u32[]{:S(2)}) collective-permute-start(bf16[256,2048]{1,0:T(8,128)(2,1)S(1)} %bitcast.8), channel_id=1, source_target_pairs={{0,4},{4,0},{1,5},{5,1},{2,6},{6,2},{3,7},{7,3},{8,12},{12,8},{9,1... | collective-permute-start | bytes 3145736 | tf_op jit(solution)/shard_map/ppermute | solution.py:321
  94.5 3.5 %collective-permute-start.9 = (bf16[256,768]{1,0:T(8,128)(2,1)}, bf16[256,768]{1,0:T(8,128)(2,1)S(1)}, u32[]{:S(2)}, u32[]{:S(2)}) collective-permute-start(bf16[256,768]{1,0:T(8,128)(2,1)} %copy-done.3), channel_id=1, source_target_pairs={{0,4},{4,0},{1,5},{5,1},{2,6},{6,2},{3,7},{7,3},{8,12},{12,8},{9,1... | collective-permute-start | bytes 1179656 | tf_op jit(solution)/shard_map/ppermute | solution.py:321
  94.6 7.9 %collective-permute-start.10 = (bf16[256,768]{1,0:T(8,128)(2,1)S(1)}, bf16[256,768]{1,0:T(8,128)(2,1)S(1)}, u32[]{:S(2)}, u32[]{:S(2)}) collective-permute-start(bf16[256,768]{1,0:T(8,128)(2,1)S(1)} %get-tuple-element.13.pair_hbm), channel_id=1, source_target_pairs={{0,4},{4,0},{1,5},{5,1},{2,6},{6,2},{3,7},{7,3},{8,12},{12,8},{9,1... | collective-permute-start | bytes 1179656 | tf_op jit(solution)/shard_map/ppermute | solution.py:321
  107.1 6.7 %collective-permute-start.13 = (bf16[8,2048]{1,0:T(8,128)(2,1)S(1)}, bf16[8,2048]{1,0:T(8,128)(2,1)S(1)}, u32[]{:S(2)}, u32[]{:S(2)}) collective-permute-start(bf16[8,2048]{1,0:T(8,128)(2,1)S(1)} %sum_parts.3), channel_id=1, source_target_pairs={{0,34},{2,0},{32,2},{34,32},{1,35},{3,1},{33,3},{35,33},{4,38},{6,... | collective-permute-start | bytes 98312 | tf_op jit(solution)/shard_map/ppermute | solution.py:327
  110.7 4.9 %collective-permute-start.12 = (bf16[8,2048]{1,0:T(8,128)(2,1)S(1)}, bf16[8,2048]{1,0:T(8,128)(2,1)S(1)}, u32[]{:S(2)}, u32[]{:S(2)}) collective-permute-start(bf16[8,2048]{1,0:T(8,128)(2,1)S(1)} %sum_parts.3), channel_id=1, source_target_pairs={{0,2},{2,32},{32,34},{34,0},{1,3},{3,33},{33,35},{35,1},{4,6},{6,3... | collective-permute-start | bytes 98312 | tf_op jit(solution)/shard_map/ppermute | solution.py:327
  110.7 6.7 %collective-permute-start.11 = (bf16[8,2048]{1,0:T(8,128)(2,1)S(1)}, bf16[8,2048]{1,0:T(8,128)(2,1)S(1)}, u32[]{:S(2)}, u32[]{:S(2)}) collective-permute-start(bf16[8,2048]{1,0:T(8,128)(2,1)S(1)} %sum_parts.3), channel_id=1, source_target_pairs={{0,32},{2,34},{32,0},{34,2},{1,33},{3,35},{33,1},{35,3},{4,36},{6,... | collective-permute-start | bytes 98312 | tf_op jit(solution)/shard_map/ppermute | solution.py:327
  137.3 5.1 %collective-permute-start.14 = (bf16[256,2048]{1,0:T(8,128)(2,1)S(1)}, bf16[256,2048]{1,0:T(8,128)(2,1)S(1)}, u32[]{:S(2)}, u32[]{:S(2)}) collective-permute-start(bf16[256,2048]{1,0:T(8,128)(2,1)S(1)} %bitcast.6), channel_id=1, source_target_pairs={{0,4},{4,0},{1,5},{5,1},{2,6},{6,2},{3,7},{7,3},{8,12},{12,8},{9,1... | collective-permute-start | bytes 3145736 | tf_op jit(solution)/shard_map/ppermute | solution.py:321

commit v5 on v3

--- a/solution.py
+++ b/solution.py
@@ -15,6 +15,8 @@
 SPECTRA_AXES = ("zp", "zq")
 LANES = 128
 STEP = 512
+PACK_VMEM = 60 << 20
+DENSE_VMEM = 8 << 20
 BF16 = jnp.bfloat16
 F32 = jnp.float32
 
@@ -40,13 +42,15 @@
 
 def pack_peaks(core, bins, values):
     rows, peaks = bins.shape
-    vmem = pl.BlockSpec(memory_space=pltpu.VMEM)
+    whole = pl.BlockSpec(bins.shape, lambda i: (0, 0))
+    packed = (rows // 2, 3 * peaks)
     return pl.pallas_call(
         pack_kernel,
-        out_shape=jax.ShapeDtypeStruct((rows // 2, 3 * peaks), BF16),
-        in_specs=[pl.BlockSpec(memory_space=pltpu.SMEM), vmem, vmem],
-        out_specs=vmem,
-        compiler_params=pltpu.CompilerParams(vmem_limit_bytes=4 << 20),
+        out_shape=jax.ShapeDtypeStruct(packed, BF16),
+        grid=(1,),
+        in_specs=[pl.BlockSpec(memory_space=pltpu.SMEM), whole, whole],
+        out_specs=pl.BlockSpec(packed, lambda i: (0, 0)),
+        compiler_params=pltpu.CompilerParams(vmem_limit_bytes=PACK_VMEM),
         name="pack_peaks",
     )(core, bins, values)
 
@@ -80,53 +84,64 @@
     return lax.dot_general(left, right, (((1,), (1,)), ((), ())), preferred_element_type=F32)
 
 
-def dense_kernel(place_ref, *refs, groups):
-    packed_refs, (own_ref, other_ref) = refs[:groups], refs[groups:]
-    peaks = packed_refs[0].shape[1] // 3
-    rows = packed_refs[0].shape[0]
+def dense_kernel(place_ref, packed_ref, *refs, back, groups):
+    own_ref, pair_ref = refs[-2:]
+    rows, lanes = packed_ref.shape
+    peaks = lanes // 3
     tiles = own_ref.shape[1] // LANES
     firsts = (place_ref[0], place_ref[1])
     lane = lax.broadcasted_iota(jnp.int32, (LANES, 1), 0).astype(BF16)
     row16 = lax.broadcasted_iota(jnp.int32, (16, LANES), 0)
     consts = (lane, (row16 >= 8).astype(jnp.int32).astype(BF16), (row16 & 7).astype(BF16))
-    for back, packed_ref in enumerate(packed_refs):
-        base = lax.rem(place_ref[2] + groups - back, groups) * rows
-
-        def step(group, carry, packed_ref=packed_ref, base=base):
-            row = pl.multiple_of(group * 16, 16)
-            block = packed_ref[pl.ds(row, 16), :].astype(F32)
-            bins = (block[:, :peaks].astype(jnp.int32) + 192) * STEP
-            bins = bins + block[:, peaks : 2 * peaks].astype(jnp.int32) + 256
-            values = block[:, 2 * peaks :]
-            sums = [
-                dense_rows(bins[h : h + 8], values[h : h + 8], firsts, tiles, consts)
-                for h in (0, 8)
+    base = lax.rem(place_ref[2] + groups - back, groups) * rows
+
+    def step(group, carry):
+        row = pl.multiple_of(group * 16, 16)
+        block = packed_ref[pl.ds(row, 16), :].astype(F32)
+        bins = (block[:, :peaks].astype(jnp.int32) + 192) * STEP
+        bins = bins + block[:, peaks : 2 * peaks].astype(jnp.int32) + 256
+        values = block[:, 2 * peaks :]
+        sums = [
+            dense_rows(bins[h : h + 8], values[h : h + 8], firsts, tiles, consts)
+            for h in (0, 8)
+        ]
+        target = pl.multiple_of(base + row, 16)
+        for ref, skip in ((own_ref, 0), (pair_ref, tiles)):
+            for tile in range(tiles):
+                at = (skip + tile) * 8
+                ref[pl.ds(target, 16), tile * LANES : (tile + 1) * LANES] = jnp.concatenate(
+                    [one[at : at + 8] for one in sums], axis=0
+                ).astype(BF16)
+        return carry
+
+    lax.fori_loop(0, rows // 16, step, 0, unroll=True)
+
+
+def build_dense(place, blocks, width):
+    groups = len(blocks)
+    part = blocks[0].shape
+    rows = part[0] * groups
+    vmem = pl.BlockSpec(memory_space=pltpu.VMEM)
+    dense = ()
+    for back, block in enumerate(blocks):
+        dense = pl.pallas_call(
+            functools.partial(dense_kernel, back=back, groups=groups),
+            out_shape=(jax.ShapeDtypeStruct((rows, width), BF16),) * 2,
+            grid=(1,),
+            in_specs=[
+                pl.BlockSpec(memory_space=pltpu.SMEM),
+                pl.BlockSpec(part, lambda i: (0, 0)),
             ]
-            target = pl.multiple_of(base + row, 16)
-            for ref, skip in ((own_ref, 0), (other_ref, tiles)):
-                for tile in range(tiles):
-                    at = (skip + tile) * 8
-                    ref[pl.ds(target, 16), tile * LANES : (tile + 1) * LANES] = jnp.concatenate(
-                        [one[at : at + 8] for one in sums], axis=0
-                    ).astype(BF16)
-            return carry
-
-        lax.fori_loop(0, rows // 16, step, 0, unroll=True)
-
-
-def build_dense(place, blocks, width):
-    rows = blocks[0].shape[0] * len(blocks)
-    vmem = pl.BlockSpec(memory_space=pltpu.VMEM)
-    return pl.pallas_call(
-        functools.partial(dense_kernel, groups=len(blocks)),
-        out_shape=(jax.ShapeDtypeStruct((rows, width), BF16),) * 2,
-        grid=(1,),
-        in_specs=[pl.BlockSpec(memory_space=pltpu.SMEM)]
-        + [pl.BlockSpec(block.shape, lambda i: (0, 0)) for block in blocks],
-        out_specs=(vmem, vmem),
-        compiler_params=pltpu.CompilerParams(vmem_limit_bytes=8 << 20),
-        name="build_dense",
-    )(place, *blocks)
+            + [vmem] * len(dense),
+            out_specs=(vmem, vmem),
+            input_output_aliases={2 + k: k for k in range(len(dense))},
+            compiler_params=pltpu.CompilerParams(vmem_limit_bytes=DENSE_VMEM),
+            cost_estimate=pl.CostEstimate(
+                flops=1_000_000_000, bytes_accessed=3_000_000, transcendentals=0
+            ),
+            name="build_dense",
+        )(place, block, *dense)
+    return dense
 
 
 def sum_kernel(parts_ref, out_ref):
@@ -189,7 +204,6 @@
     place = jnp.stack([position * width, partner * width, group]).astype(jnp.int32)
     packed = pack_peaks(core.reshape(1), peak_bins, peak_values)
     enc_weights = (enc_weight, swap(enc_weight))
-    dec_weights = (dec_weight, swap(dec_weight))
     dense_own, dense_pair = build_dense(
         place, [packed] + from_others(packed, SPECTRA_AXES), width
     )
@@ -217,9 +231,13 @@
         return near_exchange(rows.astype(BF16).reshape(lax.axis_size(NEAR), -1, hidden_size))
 
     parts = near_parts(sum(map(encode, dense, enc_weights)))
+    parts, sent_weight = lax.optimization_barrier((parts, dec_weight))
+    dec_weights = (dec_weight, swap(sent_weight))
     pre = far_sum(sum_parts(parts)) + enc_bias
     hidden = near_gather(activation(pre).astype(BF16))
-    resid = [residual(block, hidden, weight) for block, weight in zip(dense, dec_weights)]
+    resid = lax.optimization_barrier(
+        [residual(block, hidden, weight) for block, weight in zip(dense, dec_weights)]
+    )
     parts = near_parts(sum(map(decode_back, resid, dec_weights)))
     grad_dec = rows_dot(
         jnp.concatenate([hidden, swap(hidden)]), jnp.concatenate([resid[0], swap(resid[1])])
@@ -227,8 +245,8 @@
     parts, grad_dec, dense_other = lax.optimization_barrier((parts, grad_dec, dense_other))
     back = far_sum(sum_parts(parts))
     dpre = near_gather(slope_times(pre, back))
-    grad_own, dpre_other = lax.optimization_barrier((rows_dot(dense_own, dpre), swap(dpre)))
-    grad_enc = (grad_own + rows_dot(dense_other, dpre_other)).astype(BF16)
+    grad_own = lax.optimization_barrier(rows_dot(dense_own, dpre))
+    grad_enc = (rows_dot(dense_other, swap(dpre)) + grad_own).astype(BF16)
     return (grad_enc, grad_dec)
 
 

time: 142 us -> 140 us (0.986)
  Pallas kernels: 3.63 us -> 7.15 us
  other arithmetic: 2.92 us -> 0.21 us
  waiting for transfers between devices: 19.4 us -> 17.4 us
    pallas_call x2 -> x5, Pallas kernels: 3.34 us -> 6.86 us  [the longest x4 5.38 us: build_dense(): pl.pallas_call(functools.partial(dense_kernel, back=back, groups=groups),...]
    convert_element_type x1 -> x0, other arithmetic: 2.7 us -> none  [on_device(): grad_enc = (grad_own + rows_dot(dense_other, dpre_other)).astype(BF16)]
    dot_general x3, matrix products: 6.53 us -> 9.18 us  [rows_dot(): lax.dot_general(left, right, (((0,), (0,)), ((), ())), preferred_element_...]
    ppermute x9, waiting for transfers between devices: 10.2 us -> 8.33 us  [from_others(): lax.ppermute(values, axes, [(i, (i + step) % count) for i in range(count)])]
    dot_general x2, matrix products: 3.5 us -> 2.02 us  [residual(): recon = jnp.dot(hidden, weight, preferred_element_type=F32)]
  transfers between devices with their start and end apart: 16 -> 16, of which waited for: 9 -> 8; matrix products, arithmetic and copies ran while one was open for 6% -> 5% of each run, Pallas kernels for 2% -> 5%
where the time goes in v5:
time: 140 us
  blocking collectives  60.9 us (44%)
  starting transfers between devices  33.9 us (24%)
  matrix products  18.3 us (13%)
  waiting for transfers between devices  17.4 us (12%)
  Pallas kernels  7.15 us (5%)
    all_to_all x3, blocking collectives, near_exchange(): return lax.all_to_all(values, NEAR, 0, 0, tiled=True)  60.9 us
    ppermute x9, starting transfers between devices, from_others(): lax.ppermute(values, axes, [(i, (i + step) % count) for i in range(count)])  17 us
    ppermute x6, starting transfers between devices, swap(): return lax.ppermute(values, 'core', [(0, 1), (1, 0)])  13 us
    dot_general x3, matrix products, rows_dot(): lax.dot_general(left, right, (((0,), (0,)), ((), ())), preferred_element_...  9.18 us
    ppermute x9, waiting for transfers between devices, from_others(): lax.ppermute(values, axes, [(i, (i + step) % count) for i in range(count)])  8.33 us
    pallas_call x4, Pallas kernels, build_dense(): pl.pallas_call(functools.partial(dense_kernel, back=back, groups=groups),...  5.38 us
    all_to_all x1, waiting for transfers between devices, near_exchange(): return lax.all_to_all(values, NEAR, 0, 0, tiled=True)  4.86 us
    ppermute x6, waiting for transfers between devices, swap(): return lax.ppermute(values, 'core', [(0, 1), (1, 0)])  4.18 us
  transfers between devices with their start and end apart: 16, of which 8 were waited for; matrix products, arithmetic and copies ran while one was open for 5% of the time, Pallas kernels for 5%

profile of v5, /device:TPU:1, one launch (start us, length us, event | category | flops | bytes accessed | tf_op | source)
XLA Modules:
  0.0 139.8 jit_solution(5214087947846297339)
XLA Ops:
  0.6 3.3 %collective-permute-start.3 = (bf16[768,2048]{1,0:T(8,128)(2,1)}, bf16[768,2048]{1,0:T(8,128)(2,1)}, u32[]{:S(2)}, u32[]{:S(2)}) collective-permute-start(bf16[768,2048]{1,0:T(8,128)(2,1)} %param.7), channel_id=1, source_target_pairs={{0,4},{4,0},{1,5},{5,1},{2,6},{6,2},{3,7},{7,3},{8,12},{12,8},{9,1... | collective-permute-start | bytes 9437192 | tf_op jit(solution)/shard_map/ppermute | solution.py:171
  4.0 1.5 %pack_peaks.1.packed_ref = bf16[64,384]{1,0:T(8,128)(2,1)} custom-call(s32[1]{0:T(128)} %bitcast.3.core_ref, s32[128,128]{1,0:T(8,128)} %bins_ref.1, bf16[128,128]{1,0:T(8,128)(2,1)} %values_ref.1), custom_call_target="tpu_custom_call" | custom-call | tf_op jit(solution)/shard_map/pack_peaks/pallas_call | solution.py:47
  5.4 2.9 %collective-permute-start.1 = (bf16[64,384]{1,0:T(8,128)(2,1)}, bf16[64,384]{1,0:T(8,128)(2,1)S(1)}, u32[]{:S(2)}, u32[]{:S(2)}) collective-permute-start(bf16[64,384]{1,0:T(8,128)(2,1)} %pack_peaks.1.packed_ref), channel_id=1, source_target_pairs={{0,2},{1,3},{2,0},{3,1},{4,6},{5,7},{6,4},{7,5},{8,10},{9,11},{10,... | collective-permute-start | bytes 147464 | tf_op jit(solution)/shard_map/ppermute | solution.py:177
  8.3 0.7 collective-permute-start
  9.1 0.1 pad_add_fusion.place_ref
  9.1 0.8 copy-done
  9.9 1.3 build_dense.4
  11.3 1.3 build_dense.5
  12.7 1.4 build_dense.6
  14.0 1.3 build_dense.7
  15.4 0.0 copy-start.1
  15.4 3.0 %fusion.26 = f32[256,2048]{1,0:T(8,128)S(1)} fusion(bf16[256,768]{1,0:T(8,128)(2,1)S(1)} %get-tuple-element.24, bf16[768,2048]{1,0:T(8,128)(2,1)} %collective-permute-done.3), kind=kOutput, calls=%fused_computation.35 | convolution fusion | flops 805306368 | bytes 5636096 | tf_op jit(solution)/shard_map/dot_general | solution.py:214
  18.4 0.0 copy-start.2
  18.4 1.1 fusion.3
  19.5 0.0 copy-start.4
  19.5 23.8 %all_to_all.20.parts_ref = bf16[32,8,2048]{2,1,0:T(8,128)(2,1)S(1)} all-to-all(bf16[32,8,2048]{2,1,0:T(8,128)(2,1)S(1)} %fusion.3), channel_id=1, replica_groups=mesh['x'=4,'zhi'=2,'y'=4,'core'=2,'zp'=2,'zq'=2] {'x','y','zq'}, dimensions={0} | all-to-all | bytes 2097152 | tf_op jit(solution)/shard_map/all_to_all | solution.py:183
  43.3 2.4 %collective-permute-start.7 = (bf16[2048,768]{1,0:T(8,128)(2,1)S(1)}, bf16[2048,768]{1,0:T(8,128)(2,1)S(1)}, u32[]{:S(2)}, u32[]{:S(2)}) collective-permute-start(bf16[2048,768]{1,0:T(8,128)(2,1)S(1)} %copy-done.2), channel_id=1, source_target_pairs={{0,4},{4,0},{1,5},{5,1},{2,6},{6,2},{3,7},{7,3},{8,12},{12,8},{9,1... | collective-permute-start | bytes 9437192 | tf_op jit(solution)/shard_map/ppermute | solution.py:171
  45.7 0.1 sum_parts.2
  45.8 4.5 %collective-permute-start.6 = (bf16[8,2048]{1,0:T(8,128)(2,1)S(1)}, bf16[8,2048]{1,0:T(8,128)(2,1)S(1)}, u32[]{:S(2)}, u32[]{:S(2)}) collective-permute-start(bf16[8,2048]{1,0:T(8,128)(2,1)S(1)} %sum_parts.2), channel_id=1, source_target_pairs={{0,34},{2,0},{32,2},{34,32},{1,35},{3,1},{33,3},{35,33},{4,38},{6,... | collective-permute-start | bytes 98312 | tf_op jit(solution)/shard_map/ppermute | solution.py:177
  50.3 2.9 %collective-permute-start.4 = (bf16[8,2048]{1,0:T(8,128)(2,1)S(1)}, bf16[8,2048]{1,0:T(8,128)(2,1)S(1)}, u32[]{:S(2)}, u32[]{:S(2)}) collective-permute-start(bf16[8,2048]{1,0:T(8,128)(2,1)S(1)} %sum_parts.2), channel_id=1, source_target_pairs={{0,32},{2,34},{32,0},{34,2},{1,33},{3,35},{33,1},{35,3},{4,36},{6,... | collective-permute-start | bytes 98312 | tf_op jit(solution)/shard_map/ppermute | solution.py:177
  53.2 2.0 %collective-permute-done.5 = bf16[8,2048]{1,0:T(8,128)(2,1)S(1)} collective-permute-done((bf16[8,2048]{1,0:T(8,128)(2,1)S(1)}, bf16[8,2048]{1,0:T(8,128)(2,1)S(1)}, u32[]{:S(2)}, u32[]{:S(2)}) %collective-permute-start.5) | collective-permute-done | bytes 32800 | tf_op jit(solution)/shard_map/ppermute | solution.py:177
  55.2 1.8 %collective-permute-done.4 = bf16[8,2048]{1,0:T(8,128)(2,1)S(1)} collective-permute-done((bf16[8,2048]{1,0:T(8,128)(2,1)S(1)}, bf16[8,2048]{1,0:T(8,128)(2,1)S(1)}, u32[]{:S(2)}, u32[]{:S(2)}) %collective-permute-start.4) | collective-permute-done | bytes 32800 | tf_op jit(solution)/shard_map/ppermute | solution.py:177
  57.0 0.1 broadcast_in_dim.4
  57.2 18.7 %all_to_all.21 = bf16[32,8,2048]{2,1,0:T(8,128)(2,1)S(1)} all-to-all(bf16[32,8,2048]{2,1,0:T(8,128)(2,1)S(1)} %broadcast_in_dim.4), channel_id=1, replica_groups=mesh['x'=4,'zhi'=2,'y'=4,'core'=2,'zp'=2,'zq'=2] {'x','y','zq'}, dimensions={0} | all-to-all | bytes 2097152 | tf_op jit(solution)/shard_map/all_to_all | solution.py:183
  75.9 1.0 subtract_convert_fusion
  76.9 1.0 fusion.7
  77.9 1.0 fusion.27
  79.0 2.0 %fusion.2 = bf16[32,8,2048]{2,1,0:T(8,128)(2,1)} fusion(f32[256,2048]{1,0:T(8,128)S(1)} %fusion.27, bf16[256,768]{1,0:T(8,128)(2,1)S(1)} %fusion.7, bf16[2048,768]{1,0:T(8,128)(2,1)S(1)} %collective-permute-done.7), kind=kOutput, calls=%fused_computation.6 | convolution fusion | flops 806354944 | bytes 6684672 | tf_op jit(solution)/shard_map/dot_general | solution.py:221
  81.0 3.9 %all-to-all-start.2 = ((bf16[32,8,2048]{2,1,0:T(8,128)(2,1)}), bf16[32,8,2048]{2,1,0:T(8,128)(2,1)S(1)}, u32[]{:S(2)}, u32[]{:S(2)}) async-start(bf16[32,8,2048]{2,1,0:T(8,128)(2,1)} %fusion.2), calls=%async_computation.2 | async-start | bytes 2097152 | tf_op jit(solution)/shard_map/all_to_all | solution.py:183
  85.0 3.2 %collective-permute-start.8 = (bf16[256,2048]{1,0:T(8,128)(2,1)S(1)}, bf16[256,2048]{1,0:T(8,128)(2,1)S(1)}, u32[]{:S(2)}, u32[]{:S(2)}) collective-permute-start(bf16[256,2048]{1,0:T(8,128)(2,1)S(1)} %bitcast.32), channel_id=1, source_target_pairs={{0,4},{4,0},{1,5},{5,1},{2,6},{6,2},{3,7},{7,3},{8,12},{12,8},{9,1... | collective-permute-start | bytes 3145736 | tf_op jit(solution)/shard_map/ppermute | solution.py:171
  88.2 0.1 collective-permute-start.9
  88.3 0.4 collective-permute-start.10
  88.7 1.8 %collective-permute-done.8 = bf16[256,2048]{1,0:T(8,128)(2,1)S(1)} collective-permute-done((bf16[256,2048]{1,0:T(8,128)(2,1)S(1)}, bf16[256,2048]{1,0:T(8,128)(2,1)S(1)}, u32[]{:S(2)}, u32[]{:S(2)}) %collective-permute-start.8) | collective-permute-done | bytes 1048608 | tf_op jit(solution)/shard_map/ppermute | solution.py:171
  90.5 1.1 collective-permute-done.9
  91.6 4.5 %convolution_convert_fusion = bf16[2048,768]{1,0:T(8,128)(2,1)} fusion(bf16[256,2048]{1,0:T(8,128)(2,1)S(1)} %collective-permute-done.8, bf16[256,2048]{1,0:T(8,128)(2,1)S(1)} %bitcast.33, bf16[256,768]{1,0:T(8,128)(2,1)S(1)} %collective-permute-done.9, bf16[256,768]{1,0:T(8,128)(2,1)} %copy-done.3), kind=kOutput, calls=%fused_computation.1 | convolution fusion | flops 1617952768 | bytes 6029312 | tf_op jit(solution)/shard_map/dot_general | solution.py:226
  96.1 4.9 %all-to-all-done.2.parts_ref = bf16[32,8,2048]{2,1,0:T(8,128)(2,1)S(1)} async-done(((bf16[32,8,2048]{2,1,0:T(8,128)(2,1)}), bf16[32,8,2048]{2,1,0:T(8,128)(2,1)S(1)}, u32[]{:S(2)}, u32[]{:S(2)}) %all-to-all-start.2) | async-done | bytes 1048608 | tf_op jit(solution)/shard_map/all_to_all | solution.py:183
  100.9 0.1 sum_parts.3
  101.1 3.8 %collective-permute-start.13 = (bf16[8,2048]{1,0:T(8,128)(2,1)S(1)}, bf16[8,2048]{1,0:T(8,128)(2,1)S(1)}, u32[]{:S(2)}, u32[]{:S(2)}) collective-permute-start(bf16[8,2048]{1,0:T(8,128)(2,1)S(1)} %sum_parts.3), channel_id=1, source_target_pairs={{0,34},{2,0},{32,2},{34,32},{1,35},{3,1},{33,3},{35,33},{4,38},{6,... | collective-permute-start | bytes 98312 | tf_op jit(solution)/shard_map/ppermute | solution.py:177
  104.9 2.2 %collective-permute-start.11 = (bf16[8,2048]{1,0:T(8,128)(2,1)S(1)}, bf16[8,2048]{1,0:T(8,128)(2,1)S(1)}, u32[]{:S(2)}, u32[]{:S(2)}) collective-permute-start(bf16[8,2048]{1,0:T(8,128)(2,1)S(1)} %sum_parts.3), channel_id=1, source_target_pairs={{0,32},{2,34},{32,0},{34,2},{1,33},{3,35},{33,1},{35,3},{4,36},{6,... | collective-permute-start | bytes 98312 | tf_op jit(solution)/shard_map/ppermute | solution.py:177
  107.1 2.7 %collective-permute-done.12 = bf16[8,2048]{1,0:T(8,128)(2,1)S(1)} collective-permute-done((bf16[8,2048]{1,0:T(8,128)(2,1)S(1)}, bf16[8,2048]{1,0:T(8,128)(2,1)S(1)}, u32[]{:S(2)}, u32[]{:S(2)}) %collective-permute-start.12) | collective-permute-done | bytes 32800 | tf_op jit(solution)/shard_map/ppermute | solution.py:177
  109.8 1.9 %collective-permute-done.11 = bf16[8,2048]{1,0:T(8,128)(2,1)S(1)} collective-permute-done((bf16[8,2048]{1,0:T(8,128)(2,1)S(1)}, bf16[8,2048]{1,0:T(8,128)(2,1)S(1)}, u32[]{:S(2)}, u32[]{:S(2)}) %collective-permute-start.11) | collective-permute-done | bytes 32800 | tf_op jit(solution)/shard_map/ppermute | solution.py:177
  111.6 0.1 fusion.17
  111.7 0.1 broadcast_in_dim.5
  111.9 18.4 %all_to_all.22 = bf16[32,8,2048]{2,1,0:T(8,128)(2,1)S(1)} all-to-all(bf16[32,8,2048]{2,1,0:T(8,128)(2,1)S(1)} %broadcast_in_dim.5), channel_id=1, replica_groups=mesh['x'=4,'zhi'=2,'y'=4,'core'=2,'zp'=2,'zq'=2] {'x','y','zq'}, dimensions={0} | all-to-all | bytes 2097152 | tf_op jit(solution)/shard_map/all_to_all | solution.py:183
  130.3 3.5 %collective-permute-start.14 = (bf16[256,2048]{1,0:T(8,128)(2,1)S(1)}, bf16[256,2048]{1,0:T(8,128)(2,1)S(1)}, u32[]{:S(2)}, u32[]{:S(2)}) collective-permute-start(bf16[256,2048]{1,0:T(8,128)(2,1)S(1)} %bitcast.31), channel_id=1, source_target_pairs={{0,4},{4,0},{1,5},{5,1},{2,6},{6,2},{3,7},{7,3},{8,12},{12,8},{9,1... | collective-permute-start | bytes 3145736 | tf_op jit(solution)/shard_map/ppermute | solution.py:171
  133.8 1.0 fusion.19
  134.8 1.3 collective-permute-done.14
  136.1 3.7 %add_convert_fusion = bf16[768,2048]{1,0:T(8,128)(2,1)} fusion(f32[768,2048]{1,0:T(8,128)S(1)} %fusion.19, bf16[256,768]{1,0:T(8,128)(2,1)} %collective-permute-done.10, bf16[256,2048]{1,0:T(8,128)(2,1)S(1)} %collective-permute-done.14), kind=kOutput, calls=%fused_computation | convolution fusion | flops 808452096 | bytes 10878976 | tf_op jit(solution)/shard_map/dot_general | solution.py:226
  (18 shorter events, 0.1 us)
Async XLA Ops:
  0.6 14.8 %collective-permute-start.3 = (bf16[768,2048]{1,0:T(8,128)(2,1)}, bf16[768,2048]{1,0:T(8,128)(2,1)}, u32[]{:S(2)}, u32[]{:S(2)}) collective-permute-start(bf16[768,2048]{1,0:T(8,128)(2,1)} %param.7), channel_id=1, source_target_pairs={{0,4},{4,0},{1,5},{5,1},{2,6},{6,2},{3,7},{7,3},{8,12},{12,8},{9,1... | collective-permute-start | bytes 9437192 | tf_op jit(solution)/shard_map/ppermute | solution.py:171
  5.4 5.8 %collective-permute-start.2 = (bf16[64,384]{1,0:T(8,128)(2,1)}, bf16[64,384]{1,0:T(8,128)(2,1)S(1)}, u32[]{:S(2)}, u32[]{:S(2)}) collective-permute-start(bf16[64,384]{1,0:T(8,128)(2,1)} %pack_peaks.1.packed_ref), channel_id=1, source_target_pairs={{0,1},{1,2},{2,3},{3,0},{4,5},{5,6},{6,7},{7,4},{8,9},{9,10},{10,1... | collective-permute-start | bytes 147464 | tf_op jit(solution)/shard_map/ppermute | solution.py:177
  5.4 7.2 %collective-permute-start.1 = (bf16[64,384]{1,0:T(8,128)(2,1)}, bf16[64,384]{1,0:T(8,128)(2,1)S(1)}, u32[]{:S(2)}, u32[]{:S(2)}) collective-permute-start(bf16[64,384]{1,0:T(8,128)(2,1)} %pack_peaks.1.packed_ref), channel_id=1, source_target_pairs={{0,2},{1,3},{2,0},{3,1},{4,6},{5,7},{6,4},{7,5},{8,10},{9,11},{10,... | collective-permute-start | bytes 147464 | tf_op jit(solution)/shard_map/ppermute | solution.py:177
  8.3 5.7 %collective-permute-start = (bf16[64,384]{1,0:T(8,128)(2,1)}, bf16[64,384]{1,0:T(8,128)(2,1)S(1)}, u32[]{:S(2)}, u32[]{:S(2)}) collective-permute-start(bf16[64,384]{1,0:T(8,128)(2,1)} %pack_peaks.1.packed_ref), channel_id=1, source_target_pairs={{0,3},{1,0},{2,1},{3,2},{4,7},{5,4},{6,5},{7,6},{8,11},{9,8},{10,9... | collective-permute-start | bytes 147464 | tf_op jit(solution)/shard_map/ppermute | solution.py:177
  9.1 0.8 copy-start
  15.4 3.0 %copy-start.1 = (bf16[768,2048]{1,0:T(8,128)(2,1)S(1)}, bf16[768,2048]{1,0:T(8,128)(2,1)}, u32[]{:S(2)}) copy-start(bf16[768,2048]{1,0:T(8,128)(2,1)} %param.7) | copy-start | bytes 9437188
  18.4 24.9 %copy-start.2 = (bf16[2048,768]{1,0:T(8,128)(2,1)S(1)}, bf16[2048,768]{1,0:T(8,128)(2,1)}, u32[]{:S(2)}) copy-start(bf16[2048,768]{1,0:T(8,128)(2,1)} %param.9) | copy-start | bytes 9437188
  19.5 37.5 %copy-start.4 = (f32[2048]{0:T(1024)S(1)}, f32[2048]{0:T(1024)}, u32[]{:S(2)}) copy-start(f32[2048]{0:T(1024)} %param.8) | copy-start | bytes 24580
  43.3 33.6 %collective-permute-start.7 = (bf16[2048,768]{1,0:T(8,128)(2,1)S(1)}, bf16[2048,768]{1,0:T(8,128)(2,1)S(1)}, u32[]{:S(2)}, u32[]{:S(2)}) collective-permute-start(bf16[2048,768]{1,0:T(8,128)(2,1)S(1)} %copy-done.2), channel_id=1, source_target_pairs={{0,4},{4,0},{1,5},{5,1},{2,6},{6,2},{3,7},{7,3},{8,12},{12,8},{9,1... | collective-permute-start | bytes 9437192 | tf_op jit(solution)/shard_map/ppermute | solution.py:171
  45.8 7.4 %collective-permute-start.6 = (bf16[8,2048]{1,0:T(8,128)(2,1)S(1)}, bf16[8,2048]{1,0:T(8,128)(2,1)S(1)}, u32[]{:S(2)}, u32[]{:S(2)}) collective-permute-start(bf16[8,2048]{1,0:T(8,128)(2,1)S(1)} %sum_parts.2), channel_id=1, source_target_pairs={{0,34},{2,0},{32,2},{34,32},{1,35},{3,1},{33,3},{35,33},{4,38},{6,... | collective-permute-start | bytes 98312 | tf_op jit(solution)/shard_map/ppermute | solution.py:177
  50.3 4.9 %collective-permute-start.5 = (bf16[8,2048]{1,0:T(8,128)(2,1)S(1)}, bf16[8,2048]{1,0:T(8,128)(2,1)S(1)}, u32[]{:S(2)}, u32[]{:S(2)}) collective-permute-start(bf16[8,2048]{1,0:T(8,128)(2,1)S(1)} %sum_parts.2), channel_id=1, source_target_pairs={{0,2},{2,32},{32,34},{34,0},{1,3},{3,33},{33,35},{35,1},{4,6},{6,3... | collective-permute-start | bytes 98312 | tf_op jit(solution)/shard_map/ppermute | solution.py:177
  50.3 6.7 %collective-permute-start.4 = (bf16[8,2048]{1,0:T(8,128)(2,1)S(1)}, bf16[8,2048]{1,0:T(8,128)(2,1)S(1)}, u32[]{:S(2)}, u32[]{:S(2)}) collective-permute-start(bf16[8,2048]{1,0:T(8,128)(2,1)S(1)} %sum_parts.2), channel_id=1, source_target_pairs={{0,32},{2,34},{32,0},{34,2},{1,33},{3,35},{33,1},{35,3},{4,36},{6,... | collective-permute-start | bytes 98312 | tf_op jit(solution)/shard_map/ppermute | solution.py:177
  76.9 2.0 %copy-start.3 = (bf16[256,768]{1,0:T(8,128)(2,1)}, bf16[256,768]{1,0:T(8,128)(2,1)S(1)}, u32[]{:S(2)}) copy-start(bf16[256,768]{1,0:T(8,128)(2,1)S(1)} %subtract_convert_fusion) | copy-start | bytes 1179652
  81.0 19.9 %all-to-all-start.2 = ((bf16[32,8,2048]{2,1,0:T(8,128)(2,1)}), bf16[32,8,2048]{2,1,0:T(8,128)(2,1)S(1)}, u32[]{:S(2)}, u32[]{:S(2)}) async-start(bf16[32,8,2048]{2,1,0:T(8,128)(2,1)} %fusion.2), calls=%async_computation.2 | async-start | bytes 2097152 | tf_op jit(solution)/shard_map/all_to_all | solution.py:183
  85.0 5.5 %collective-permute-start.8 = (bf16[256,2048]{1,0:T(8,128)(2,1)S(1)}, bf16[256,2048]{1,0:T(8,128)(2,1)S(1)}, u32[]{:S(2)}, u32[]{:S(2)}) collective-permute-start(bf16[256,2048]{1,0:T(8,128)(2,1)S(1)} %bitcast.32), channel_id=1, source_target_pairs={{0,4},{4,0},{1,5},{5,1},{2,6},{6,2},{3,7},{7,3},{8,12},{12,8},{9,1... | collective-permute-start | bytes 3145736 | tf_op jit(solution)/shard_map/ppermute | solution.py:171
  88.2 3.4 %collective-permute-start.9 = (bf16[256,768]{1,0:T(8,128)(2,1)S(1)}, bf16[256,768]{1,0:T(8,128)(2,1)S(1)}, u32[]{:S(2)}, u32[]{:S(2)}) collective-permute-start(bf16[256,768]{1,0:T(8,128)(2,1)S(1)} %fusion.7), channel_id=1, source_target_pairs={{0,4},{4,0},{1,5},{5,1},{2,6},{6,2},{3,7},{7,3},{8,12},{12,8},{9,1... | collective-permute-start | bytes 1179656 | tf_op jit(solution)/shard_map/ppermute | solution.py:171
  88.3 7.8 %collective-permute-start.10 = (bf16[256,768]{1,0:T(8,128)(2,1)S(1)}, bf16[256,768]{1,0:T(8,128)(2,1)}, u32[]{:S(2)}, u32[]{:S(2)}) collective-permute-start(bf16[256,768]{1,0:T(8,128)(2,1)S(1)} %get-tuple-element.24), channel_id=1, source_target_pairs={{0,4},{4,0},{1,5},{5,1},{2,6},{6,2},{3,7},{7,3},{8,12},{12,8},{9,1... | collective-permute-start | bytes 1179656 | tf_op jit(solution)/shard_map/ppermute | solution.py:171
  101.1 6.0 %collective-permute-start.13 = (bf16[8,2048]{1,0:T(8,128)(2,1)S(1)}, bf16[8,2048]{1,0:T(8,128)(2,1)S(1)}, u32[]{:S(2)}, u32[]{:S(2)}) collective-permute-start(bf16[8,2048]{1,0:T(8,128)(2,1)S(1)} %sum_parts.3), channel_id=1, source_target_pairs={{0,34},{2,0},{32,2},{34,32},{1,35},{3,1},{33,3},{35,33},{4,38},{6,... | collective-permute-start | bytes 98312 | tf_op jit(solution)/shard_map/ppermute | solution.py:177
  104.9 4.9 %collective-permute-start.12 = (bf16[8,2048]{1,0:T(8,128)(2,1)S(1)}, bf16[8,2048]{1,0:T(8,128)(2,1)S(1)}, u32[]{:S(2)}, u32[]{:S(2)}) collective-permute-start(bf16[8,2048]{1,0:T(8,128)(2,1)S(1)} %sum_parts.3), channel_id=1, source_target_pairs={{0,2},{2,32},{32,34},{34,0},{1,3},{3,33},{33,35},{35,1},{4,6},{6,3... | collective-permute-start | bytes 98312 | tf_op jit(solution)/shard_map/ppermute | solution.py:177
  104.9 6.7 %collective-permute-start.11 = (bf16[8,2048]{1,0:T(8,128)(2,1)S(1)}, bf16[8,2048]{1,0:T(8,128)(2,1)S(1)}, u32[]{:S(2)}, u32[]{:S(2)}) collective-permute-start(bf16[8,2048]{1,0:T(8,128)(2,1)S(1)} %sum_parts.3), channel_id=1, source_target_pairs={{0,32},{2,34},{32,0},{34,2},{1,33},{3,35},{33,1},{35,3},{4,36},{6,... | collective-permute-start | bytes 98312 | tf_op jit(solution)/shard_map/ppermute | solution.py:177
  130.3 5.8 %collective-permute-start.14 = (bf16[256,2048]{1,0:T(8,128)(2,1)S(1)}, bf16[256,2048]{1,0:T(8,128)(2,1)S(1)}, u32[]{:S(2)}, u32[]{:S(2)}) collective-permute-start(bf16[256,2048]{1,0:T(8,128)(2,1)S(1)} %bitcast.31), channel_id=1, source_target_pairs={{0,4},{4,0},{1,5},{5,1},{2,6},{6,2},{3,7},{7,3},{8,12},{12,8},{9,1... | collective-permute-start | bytes 3145736 | tf_op jit(solution)/shard_map/ppermute | solution.py:171

commit v6 on v5

--- a/solution.py
+++ b/solution.py
@@ -15,7 +15,7 @@
 SPECTRA_AXES = ("zp", "zq")
 LANES = 128
 STEP = 512
-PACK_VMEM = 60 << 20
+PACK_VMEM = 50 << 20
 DENSE_VMEM = 8 << 20
 BF16 = jnp.bfloat16
 F32 = jnp.float32
@@ -49,7 +49,7 @@
         out_shape=jax.ShapeDtypeStruct(packed, BF16),
         grid=(1,),
         in_specs=[pl.BlockSpec(memory_space=pltpu.SMEM), whole, whole],
-        out_specs=pl.BlockSpec(packed, lambda i: (0, 0)),
+        out_specs=pl.BlockSpec(memory_space=pltpu.VMEM),
         compiler_params=pltpu.CompilerParams(vmem_limit_bytes=PACK_VMEM),
         name="pack_peaks",
     )(core, bins, values)
@@ -84,18 +84,17 @@
     return lax.dot_general(left, right, (((1,), (1,)), ((), ())), preferred_element_type=F32)
 
 
-def dense_kernel(place_ref, packed_ref, *refs, back, groups):
-    own_ref, pair_ref = refs[-2:]
-    rows, lanes = packed_ref.shape
+def dense_kernel(place_ref, *refs, backs, groups):
+    packed_refs, (own_ref, pair_ref) = refs[: len(backs)], refs[-2:]
+    rows, lanes = packed_refs[0].shape
     peaks = lanes // 3
     tiles = own_ref.shape[1] // LANES
     firsts = (place_ref[0], place_ref[1])
     lane = lax.broadcasted_iota(jnp.int32, (LANES, 1), 0).astype(BF16)
     row16 = lax.broadcasted_iota(jnp.int32, (16, LANES), 0)
     consts = (lane, (row16 >= 8).astype(jnp.int32).astype(BF16), (row16 & 7).astype(BF16))
-    base = lax.rem(place_ref[2] + groups - back, groups) * rows
-
-    def step(group, carry):
+
+    def step(group, carry, packed_ref, base):
         row = pl.multiple_of(group * 16, 16)
         block = packed_ref[pl.ds(row, 16), :].astype(F32)
         bins = (block[:, :peaks].astype(jnp.int32) + 192) * STEP
@@ -114,7 +113,10 @@
                 ).astype(BF16)
         return carry
 
-    lax.fori_loop(0, rows // 16, step, 0, unroll=True)
+    for back, packed_ref in zip(backs, packed_refs):
+        base = lax.rem(place_ref[2] + groups - back, groups) * rows
+        block_step = functools.partial(step, packed_ref=packed_ref, base=base)
+        lax.fori_loop(0, rows // 16, block_step, 0, unroll=True)
 
 
 def build_dense(place, blocks, width):
@@ -123,24 +125,23 @@
     rows = part[0] * groups
     vmem = pl.BlockSpec(memory_space=pltpu.VMEM)
     dense = ()
-    for back, block in enumerate(blocks):
+    for first in range(0, groups, 2):
+        backs = (first, first + 1)
         dense = pl.pallas_call(
-            functools.partial(dense_kernel, back=back, groups=groups),
+            functools.partial(dense_kernel, backs=backs, groups=groups),
             out_shape=(jax.ShapeDtypeStruct((rows, width), BF16),) * 2,
             grid=(1,),
-            in_specs=[
-                pl.BlockSpec(memory_space=pltpu.SMEM),
-                pl.BlockSpec(part, lambda i: (0, 0)),
-            ]
+            in_specs=[pl.BlockSpec(memory_space=pltpu.SMEM)]
+            + [pl.BlockSpec(part, lambda i: (0, 0))] * 2
             + [vmem] * len(dense),
             out_specs=(vmem, vmem),
-            input_output_aliases={2 + k: k for k in range(len(dense))},
+            input_output_aliases={3 + k: k for k in range(len(dense))},
             compiler_params=pltpu.CompilerParams(vmem_limit_bytes=DENSE_VMEM),
             cost_estimate=pl.CostEstimate(
                 flops=1_000_000_000, bytes_accessed=3_000_000, transcendentals=0
             ),
             name="build_dense",
-        )(place, block, *dense)
+        )(place, *blocks[first : first + 2], *dense)
     return dense
 
 
@@ -183,15 +184,19 @@
     return lax.all_to_all(values, NEAR, 0, 0, tiled=True)
 
 
-def far_sum(sent):
-    one, two, three = [block.astype(F32) for block in from_others(sent, FAR)]
-    return (sent.astype(F32) + two) + (one + three)
+def copies_to(values, axes):
+    count = lax.axis_size(axes)
+    sent = jnp.broadcast_to(values[None], (count,) + values.shape)
+    return lax.all_to_all(sent, axes, 0, 0, tiled=True)
+
+
+def far_sum(values):
+    blocks = copies_to(values, FAR).astype(F32)
+    return (blocks[0] + blocks[1]) + (blocks[2] + blocks[3])
 
 
 def near_gather(values):
-    count = lax.axis_size(NEAR)
-    sent = jnp.broadcast_to(values[None], (count,) + values.shape)
-    return near_exchange(sent).reshape(-1, values.shape[-1])
+    return copies_to(values, NEAR).reshape(-1, values.shape[-1])
 
 
 def on_device(peak_bins, peak_values, enc_weight, enc_bias, dec_weight):

time: 140 us -> 143 us (1.021)
  blocking collectives: 60.9 us -> 82.7 us
  starting transfers between devices: 33.9 us -> 22.5 us
  waiting for transfers between devices: 17.4 us -> 11.9 us
  Pallas kernels: 7.15 us -> 4.31 us
    all_to_all x0 -> x4, blocking collectives: none -> 59.8 us  [copies_to(): return lax.all_to_all(sent, axes, 0, 0, tiled=True)]
    all_to_all x3 -> x1, blocking collectives: 60.9 us -> 22.9 us  [near_exchange(): return lax.all_to_all(values, NEAR, 0, 0, tiled=True)]
    ppermute x9 -> x3, starting transfers between devices: 17 us -> 3.34 us  [from_others(): lax.ppermute(values, axes, [(i, (i + step) % count) for i in range(count)])]
    ppermute x9 -> x3, waiting for transfers between devices: 8.33 us -> 2.88 us  [from_others(): lax.ppermute(values, axes, [(i, (i + step) % count) for i in range(count)])]
    ppermute x6, starting transfers between devices: 13 us -> 15.2 us  [swap(): return lax.ppermute(values, 'core', [(0, 1), (1, 0)])]
    pallas_call x1, Pallas kernels: 1.47 us -> 0.01 us  [pack_peaks(): pl.pallas_call(pack_kernel, out_shape=jax.ShapeDtypeStruct(packed, BF16),...]
    pallas_call x4 -> x2, Pallas kernels: 5.38 us -> 4 us  [build_dense(): pl.pallas_call(functools.partial(dense_kernel, backs=backs, groups=groups...]
  transfers between devices with their start and end apart: 16 -> 10, of which waited for: 8 -> 6; matrix products, arithmetic and copies ran while one was open for 5% -> 5% of each run, Pallas kernels for 5% -> 3%
where the time goes in v6:
time: 143 us
  blocking collectives  82.7 us (58%)
  starting transfers between devices  22.5 us (16%)
  matrix products  18.3 us (13%)
  waiting for transfers between devices  11.9 us (8%)
  Pallas kernels  4.31 us (3%)
  local copies, waits for them, and re-layouts  1.86 us (1%)
    all_to_all x4, blocking collectives, copies_to(): return lax.all_to_all(sent, axes, 0, 0, tiled=True)  59.8 us
    all_to_all x1, blocking collectives, near_exchange(): return lax.all_to_all(values, NEAR, 0, 0, tiled=True)  22.9 us
    ppermute x6, starting transfers between devices, swap(): return lax.ppermute(values, 'core', [(0, 1), (1, 0)])  15.2 us
    dot_general x3, matrix products, rows_dot(): lax.dot_general(left, right, (((0,), (0,)), ((), ())), preferred_element_...  9.18 us
    all_to_all x1, waiting for transfers between devices, near_exchange(): return lax.all_to_all(values, NEAR, 0, 0, tiled=True)  4.84 us
    ppermute x6, waiting for transfers between devices, swap(): return lax.ppermute(values, 'core', [(0, 1), (1, 0)])  4.19 us
    dot_general x2, matrix products, encode(): return jnp.dot(block, weight, preferred_element_type=F32)  4.07 us
    pallas_call x2, Pallas kernels, build_dense(): pl.pallas_call(functools.partial(dense_kernel, backs=backs, groups=groups...  4 us
  transfers between devices with their start and end apart: 10, of which 6 were waited for; matrix products, arithmetic and copies ran while one was open for 5% of the time, Pallas kernels for 3%

profile of v6, /device:TPU:1, one launch (start us, length us, event | category | flops | bytes accessed | tf_op | source)
XLA Modules:
  0.0 142.6 jit_solution(1551184347026722288)
XLA Ops:
  0.6 3.3 %collective-permute-start.3 = (bf16[768,2048]{1,0:T(8,128)(2,1)}, bf16[768,2048]{1,0:T(8,128)(2,1)}, u32[]{:S(2)}, u32[]{:S(2)}) collective-permute-start(bf16[768,2048]{1,0:T(8,128)(2,1)} %param.7), channel_id=1, source_target_pairs={{0,4},{4,0},{1,5},{5,1},{2,6},{6,2},{3,7},{7,3},{8,12},{12,8},{9,1... | collective-permute-start | bytes 9437192 | tf_op jit(solution)/shard_map/ppermute | solution.py:172
  4.0 0.8 copy-done
  4.8 0.8 copy-done.1
  5.6 0.1 collective-permute-start.2
  5.7 3.3 %collective-permute-start.1 = (bf16[64,384]{1,0:T(8,128)(2,1)S(1)}, bf16[64,384]{1,0:T(8,128)(2,1)S(1)}, u32[]{:S(2)}, u32[]{:S(2)}) collective-permute-start(bf16[64,384]{1,0:T(8,128)(2,1)S(1)} %pack_peaks.1.refs_0_), channel_id=1, source_target_pairs={{0,3},{1,0},{2,1},{3,2},{4,7},{5,4},{6,5},{7,6},{8,11},{9,8},{10,9... | collective-permute-start | bytes 147464 | tf_op jit(solution)/shard_map/ppermute | solution.py:178
  8.9 0.0 collective-permute-start
  8.9 0.1 pad_add_fusion.place_ref
  9.0 1.8 %collective-permute-done.2.refs_1_ = bf16[64,384]{1,0:T(8,128)(2,1)S(1)} collective-permute-done((bf16[64,384]{1,0:T(8,128)(2,1)S(1)}, bf16[64,384]{1,0:T(8,128)(2,1)S(1)}, u32[]{:S(2)}, u32[]{:S(2)}) %collective-permute-start.2) | collective-permute-done | bytes 49184 | tf_op jit(solution)/shard_map/ppermute | solution.py:178
  10.8 2.0 %build_dense.2 = (bf16[256,768]{1,0:T(8,128)(2,1)S(1)}, bf16[256,768]{1,0:T(8,128)(2,1)S(1)}) custom-call(s32[3]{0:T(128)S(1)} %pad_add_fusion.place_ref, bf16[64,384]{1,0:T(8,128)(2,1)S(1)} %pack_peaks.1.refs_0_, bf16[64,384]{1,0:T(8,128)(2,1)S(1)} %collective-permute-done.2.refs_1_), custom_call_target="tpu_custom_call" | custom-call | flops 1000000000 | bytes 3000000 | tf_op jit(solution)/shard_map/build_dense/pallas_call | solution.py:130
  12.8 0.0 collective-permute-done.1.refs_1_
  12.8 1.1 collective-permute-done.refs_0_
  13.9 2.0 %build_dense.3 = (bf16[256,768]{1,0:T(8,128)(2,1)S(1)}, bf16[256,768]{1,0:T(8,128)(2,1)S(1)}) custom-call(s32[3]{0:T(128)S(1)} %pad_add_fusion.place_ref, bf16[64,384]{1,0:T(8,128)(2,1)S(1)} %collective-permute-done.refs_0_, bf16[64,384]{1,0:T(8,128)(2,1)S(1)} %collective-permute-done.1.refs_1_, ...), custom_call_target="tpu_custom_call", output_to_operand_aliasing={{0}: (3, {}), {1}: (4, {})} | custom-call | flops 1000000000 | bytes 3000000 | tf_op jit(solution)/shard_map/build_dense/pallas_call | solution.py:130
  15.9 0.0 copy-start.2
  15.9 0.0 collective-permute-done.3
  15.9 3.0 %fusion.32 = f32[256,2048]{1,0:T(8,128)S(1)} fusion(bf16[256,768]{1,0:T(8,128)(2,1)S(1)} %get-tuple-element.16, bf16[768,2048]{1,0:T(8,128)(2,1)} %collective-permute-done.3), kind=kOutput, calls=%fused_computation.43 | convolution fusion | flops 805306368 | bytes 5636096 | tf_op jit(solution)/shard_map/dot_general | solution.py:219
  18.9 0.0 copy-done.2
  18.9 0.0 copy-start.3
  19.0 1.1 fusion.3
  20.0 0.0 copy-start.5
  20.0 22.9 %all_to_all.30.parts_ref = bf16[32,8,2048]{2,1,0:T(8,128)(2,1)S(1)} all-to-all(bf16[32,8,2048]{2,1,0:T(8,128)(2,1)S(1)} %fusion.3), channel_id=1, replica_groups=mesh['x'=4,'zhi'=2,'y'=4,'core'=2,'zp'=2,'zq'=2] {'x','y','zq'}, dimensions={0} | all-to-all | bytes 2097152 | tf_op jit(solution)/shard_map/all_to_all | solution.py:184
  42.9 2.3 %collective-permute-start.4 = (bf16[2048,768]{1,0:T(8,128)(2,1)S(1)}, bf16[2048,768]{1,0:T(8,128)(2,1)S(1)}, u32[]{:S(2)}, u32[]{:S(2)}) collective-permute-start(bf16[2048,768]{1,0:T(8,128)(2,1)S(1)} %copy-done.3), channel_id=1, source_target_pairs={{0,4},{4,0},{1,5},{5,1},{2,6},{6,2},{3,7},{7,3},{8,12},{12,8},{9,1... | collective-permute-start | bytes 9437192 | tf_op jit(solution)/shard_map/ppermute | solution.py:172
  45.2 0.1 sum_parts.2
  45.4 14.4 %all_to_all.31 = bf16[4,8,2048]{2,1,0:T(8,128)(2,1)S(1)} all-to-all(bf16[4,8,2048]{2,1,0:T(8,128)(2,1)S(1)} %broadcast_in_dim.12), channel_id=1, replica_groups=mesh['x'=4,'zhi'=2,'y'=4,'core'=2,'zp'=2,'zq'=2] {'zhi','zp'}, dimensions={0} | all-to-all | bytes 262144 | tf_op jit(solution)/shard_map/all_to_all | solution.py:190
  59.8 0.1 broadcast_in_dim.14
  59.9 18.7 %all_to_all.32 = bf16[32,8,2048]{2,1,0:T(8,128)(2,1)S(1)} all-to-all(bf16[32,8,2048]{2,1,0:T(8,128)(2,1)S(1)} %broadcast_in_dim.14), channel_id=1, replica_groups=mesh['x'=4,'zhi'=2,'y'=4,'core'=2,'zp'=2,'zq'=2] {'x','y','zq'}, dimensions={0} | all-to-all | bytes 2097152 | tf_op jit(solution)/shard_map/all_to_all | solution.py:190
  78.6 1.0 subtract_convert_fusion
  79.7 0.0 collective-permute-done.4
  79.7 1.0 fusion.7
  80.7 1.0 fusion.33
  81.7 2.0 %fusion.2 = bf16[32,8,2048]{2,1,0:T(8,128)(2,1)} fusion(f32[256,2048]{1,0:T(8,128)S(1)} %fusion.33, bf16[256,768]{1,0:T(8,128)(2,1)S(1)} %fusion.7, bf16[2048,768]{1,0:T(8,128)(2,1)S(1)} %collective-permute-done.4), kind=kOutput, calls=%fused_computation.6 | convolution fusion | flops 806354944 | bytes 6684672 | tf_op jit(solution)/shard_map/dot_general | solution.py:226
  83.7 3.9 %all-to-all-start.3 = ((bf16[32,8,2048]{2,1,0:T(8,128)(2,1)}), bf16[32,8,2048]{2,1,0:T(8,128)(2,1)S(1)}, u32[]{:S(2)}, u32[]{:S(2)}) async-start(bf16[32,8,2048]{2,1,0:T(8,128)(2,1)} %fusion.2), calls=%async_computation.3 | async-start | bytes 2097152 | tf_op jit(solution)/shard_map/all_to_all | solution.py:184
  87.7 3.2 %collective-permute-start.5 = (bf16[256,2048]{1,0:T(8,128)(2,1)S(1)}, bf16[256,2048]{1,0:T(8,128)(2,1)S(1)}, u32[]{:S(2)}, u32[]{:S(2)}) collective-permute-start(bf16[256,2048]{1,0:T(8,128)(2,1)S(1)} %bitcast.36), channel_id=1, source_target_pairs={{0,4},{4,0},{1,5},{5,1},{2,6},{6,2},{3,7},{7,3},{8,12},{12,8},{9,1... | collective-permute-start | bytes 3145736 | tf_op jit(solution)/shard_map/ppermute | solution.py:172
  90.9 0.3 collective-permute-start.6
  91.2 0.2 collective-permute-start.7
  91.4 1.8 %collective-permute-done.5 = bf16[256,2048]{1,0:T(8,128)(2,1)S(1)} collective-permute-done((bf16[256,2048]{1,0:T(8,128)(2,1)S(1)}, bf16[256,2048]{1,0:T(8,128)(2,1)S(1)}, u32[]{:S(2)}, u32[]{:S(2)}) %collective-permute-start.5) | collective-permute-done | bytes 1048608 | tf_op jit(solution)/shard_map/ppermute | solution.py:172
  93.2 1.1 collective-permute-done.6
  94.3 4.5 %convolution_convert_fusion = bf16[2048,768]{1,0:T(8,128)(2,1)} fusion(bf16[256,2048]{1,0:T(8,128)(2,1)S(1)} %collective-permute-done.5, bf16[256,2048]{1,0:T(8,128)(2,1)S(1)} %bitcast.37, bf16[256,768]{1,0:T(8,128)(2,1)S(1)} %collective-permute-done.6, bf16[256,768]{1,0:T(8,128)(2,1)} %copy-done.4), kind=kOutput, calls=%fused_computation.1 | convolution fusion | flops 1617952768 | bytes 6029312 | tf_op jit(solution)/shard_map/dot_general | solution.py:231
  98.8 0.0 collective-permute-done.7
  98.8 4.8 %all-to-all-done.3.parts_ref = bf16[32,8,2048]{2,1,0:T(8,128)(2,1)S(1)} async-done(((bf16[32,8,2048]{2,1,0:T(8,128)(2,1)}), bf16[32,8,2048]{2,1,0:T(8,128)(2,1)S(1)}, u32[]{:S(2)}, u32[]{:S(2)}) %all-to-all-start.3) | async-done | bytes 1048608 | tf_op jit(solution)/shard_map/all_to_all | solution.py:184
  103.7 0.1 sum_parts.3
  103.8 10.8 %all_to_all.33 = bf16[4,8,2048]{2,1,0:T(8,128)(2,1)S(1)} all-to-all(bf16[4,8,2048]{2,1,0:T(8,128)(2,1)S(1)} %broadcast_in_dim.15), channel_id=1, replica_groups=mesh['x'=4,'zhi'=2,'y'=4,'core'=2,'zp'=2,'zq'=2] {'zhi','zp'}, dimensions={0} | all-to-all | bytes 262144 | tf_op jit(solution)/shard_map/all_to_all | solution.py:190
  114.6 0.1 fusion.22
  114.7 0.1 broadcast_in_dim.34
  114.8 15.9 %all_to_all.34 = bf16[32,8,2048]{2,1,0:T(8,128)(2,1)S(1)} all-to-all(bf16[32,8,2048]{2,1,0:T(8,128)(2,1)S(1)} %broadcast_in_dim.34), channel_id=1, replica_groups=mesh['x'=4,'zhi'=2,'y'=4,'core'=2,'zp'=2,'zq'=2] {'x','y','zq'}, dimensions={0} | all-to-all | bytes 2097152 | tf_op jit(solution)/shard_map/all_to_all | solution.py:190
  130.8 5.9 %collective-permute-start.8 = (bf16[256,2048]{1,0:T(8,128)(2,1)S(1)}, bf16[256,2048]{1,0:T(8,128)(2,1)S(1)}, u32[]{:S(2)}, u32[]{:S(2)}) collective-permute-start(bf16[256,2048]{1,0:T(8,128)(2,1)S(1)} %bitcast.35), channel_id=1, source_target_pairs={{0,4},{4,0},{1,5},{5,1},{2,6},{6,2},{3,7},{7,3},{8,12},{12,8},{9,1... | collective-permute-start | bytes 3145736 | tf_op jit(solution)/shard_map/ppermute | solution.py:172
  136.7 1.0 fusion.24
  137.7 1.3 collective-permute-done.8
  139.0 3.7 %add_convert_fusion = bf16[768,2048]{1,0:T(8,128)(2,1)} fusion(f32[768,2048]{1,0:T(8,128)S(1)} %fusion.24, bf16[256,768]{1,0:T(8,128)(2,1)} %collective-permute-done.7, bf16[256,2048]{1,0:T(8,128)(2,1)S(1)} %collective-permute-done.8), kind=kOutput, calls=%fused_computation | convolution fusion | flops 808452096 | bytes 10878976 | tf_op jit(solution)/shard_map/dot_general | solution.py:231
  (12 shorter events, 0.1 us)
Async XLA Ops:
  0.6 15.3 %collective-permute-start.3 = (bf16[768,2048]{1,0:T(8,128)(2,1)}, bf16[768,2048]{1,0:T(8,128)(2,1)}, u32[]{:S(2)}, u32[]{:S(2)}) collective-permute-start(bf16[768,2048]{1,0:T(8,128)(2,1)} %param.7), channel_id=1, source_target_pairs={{0,4},{4,0},{1,5},{5,1},{2,6},{6,2},{3,7},{7,3},{8,12},{12,8},{9,1... | collective-permute-start | bytes 9437192 | tf_op jit(solution)/shard_map/ppermute | solution.py:172
  4.0 0.8 copy-start
  4.8 0.8 copy-start.1
  5.6 5.2 %collective-permute-start.2 = (bf16[64,384]{1,0:T(8,128)(2,1)S(1)}, bf16[64,384]{1,0:T(8,128)(2,1)S(1)}, u32[]{:S(2)}, u32[]{:S(2)}) collective-permute-start(bf16[64,384]{1,0:T(8,128)(2,1)S(1)} %pack_peaks.1.refs_0_), channel_id=1, source_target_pairs={{0,1},{1,2},{2,3},{3,0},{4,5},{5,6},{6,7},{7,4},{8,9},{9,10},{10,1... | collective-permute-start | bytes 147464 | tf_op jit(solution)/shard_map/ppermute | solution.py:178
  5.7 7.1 %collective-permute-start.1 = (bf16[64,384]{1,0:T(8,128)(2,1)S(1)}, bf16[64,384]{1,0:T(8,128)(2,1)S(1)}, u32[]{:S(2)}, u32[]{:S(2)}) collective-permute-start(bf16[64,384]{1,0:T(8,128)(2,1)S(1)} %pack_peaks.1.refs_0_), channel_id=1, source_target_pairs={{0,3},{1,0},{2,1},{3,2},{4,7},{5,4},{6,5},{7,6},{8,11},{9,8},{10,9... | collective-permute-start | bytes 147464 | tf_op jit(solution)/shard_map/ppermute | solution.py:178
  8.9 5.0 %collective-permute-start = (bf16[64,384]{1,0:T(8,128)(2,1)S(1)}, bf16[64,384]{1,0:T(8,128)(2,1)S(1)}, u32[]{:S(2)}, u32[]{:S(2)}) collective-permute-start(bf16[64,384]{1,0:T(8,128)(2,1)S(1)} %pack_peaks.1.refs_0_), channel_id=1, source_target_pairs={{0,2},{1,3},{2,0},{3,1},{4,6},{5,7},{6,4},{7,5},{8,10},{9,11},{10,... | collective-permute-start | bytes 147464 | tf_op jit(solution)/shard_map/ppermute | solution.py:178
  15.9 3.0 %copy-start.2 = (bf16[768,2048]{1,0:T(8,128)(2,1)S(1)}, bf16[768,2048]{1,0:T(8,128)(2,1)}, u32[]{:S(2)}) copy-start(bf16[768,2048]{1,0:T(8,128)(2,1)} %param.7) | copy-start | bytes 9437188
  18.9 24.0 %copy-start.3 = (bf16[2048,768]{1,0:T(8,128)(2,1)S(1)}, bf16[2048,768]{1,0:T(8,128)(2,1)}, u32[]{:S(2)}) copy-start(bf16[2048,768]{1,0:T(8,128)(2,1)} %param.9) | copy-start | bytes 9437188
  20.0 39.7 %copy-start.5 = (f32[2048]{0:T(1024)S(1)}, f32[2048]{0:T(1024)}, u32[]{:S(2)}) copy-start(f32[2048]{0:T(1024)} %param.8) | copy-start | bytes 24580
  42.9 36.7 %collective-permute-start.4 = (bf16[2048,768]{1,0:T(8,128)(2,1)S(1)}, bf16[2048,768]{1,0:T(8,128)(2,1)S(1)}, u32[]{:S(2)}, u32[]{:S(2)}) collective-permute-start(bf16[2048,768]{1,0:T(8,128)(2,1)S(1)} %copy-done.3), channel_id=1, source_target_pairs={{0,4},{4,0},{1,5},{5,1},{2,6},{6,2},{3,7},{7,3},{8,12},{12,8},{9,1... | collective-permute-start | bytes 9437192 | tf_op jit(solution)/shard_map/ppermute | solution.py:172
  79.7 2.0 %copy-start.4 = (bf16[256,768]{1,0:T(8,128)(2,1)}, bf16[256,768]{1,0:T(8,128)(2,1)S(1)}, u32[]{:S(2)}) copy-start(bf16[256,768]{1,0:T(8,128)(2,1)S(1)} %subtract_convert_fusion) | copy-start | bytes 1179652
  83.7 19.9 %all-to-all-start.3 = ((bf16[32,8,2048]{2,1,0:T(8,128)(2,1)}), bf16[32,8,2048]{2,1,0:T(8,128)(2,1)S(1)}, u32[]{:S(2)}, u32[]{:S(2)}) async-start(bf16[32,8,2048]{2,1,0:T(8,128)(2,1)} %fusion.2), calls=%async_computation.3 | async-start | bytes 2097152 | tf_op jit(solution)/shard_map/all_to_all | solution.py:184
  87.7 5.5 %collective-permute-start.5 = (bf16[256,2048]{1,0:T(8,128)(2,1)S(1)}, bf16[256,2048]{1,0:T(8,128)(2,1)S(1)}, u32[]{:S(2)}, u32[]{:S(2)}) collective-permute-start(bf16[256,2048]{1,0:T(8,128)(2,1)S(1)} %bitcast.36), channel_id=1, source_target_pairs={{0,4},{4,0},{1,5},{5,1},{2,6},{6,2},{3,7},{7,3},{8,12},{12,8},{9,1... | collective-permute-start | bytes 3145736 | tf_op jit(solution)/shard_map/ppermute | solution.py:172
  90.9 3.4 %collective-permute-start.6 = (bf16[256,768]{1,0:T(8,128)(2,1)S(1)}, bf16[256,768]{1,0:T(8,128)(2,1)S(1)}, u32[]{:S(2)}, u32[]{:S(2)}) collective-permute-start(bf16[256,768]{1,0:T(8,128)(2,1)S(1)} %fusion.7), channel_id=1, source_target_pairs={{0,4},{4,0},{1,5},{5,1},{2,6},{6,2},{3,7},{7,3},{8,12},{12,8},{9,1... | collective-permute-start | bytes 1179656 | tf_op jit(solution)/shard_map/ppermute | solution.py:172
  91.2 7.6 %collective-permute-start.7 = (bf16[256,768]{1,0:T(8,128)(2,1)S(1)}, bf16[256,768]{1,0:T(8,128)(2,1)}, u32[]{:S(2)}, u32[]{:S(2)}) collective-permute-start(bf16[256,768]{1,0:T(8,128)(2,1)S(1)} %get-tuple-element.16), channel_id=1, source_target_pairs={{0,4},{4,0},{1,5},{5,1},{2,6},{6,2},{3,7},{7,3},{8,12},{12,8},{9,1... | collective-permute-start | bytes 1179656 | tf_op jit(solution)/shard_map/ppermute | solution.py:172
  130.8 8.2 %collective-permute-start.8 = (bf16[256,2048]{1,0:T(8,128)(2,1)S(1)}, bf16[256,2048]{1,0:T(8,128)(2,1)S(1)}, u32[]{:S(2)}, u32[]{:S(2)}) collective-permute-start(bf16[256,2048]{1,0:T(8,128)(2,1)S(1)} %bitcast.35), channel_id=1, source_target_pairs={{0,4},{4,0},{1,5},{5,1},{2,6},{6,2},{3,7},{7,3},{8,12},{12,8},{9,1... | collective-permute-start | bytes 3145736 | tf_op jit(solution)/shard_map/ppermute | solution.py:172

commit v7 on v5

--- a/solution.py
+++ b/solution.py
@@ -204,6 +204,7 @@
     place = jnp.stack([position * width, partner * width, group]).astype(jnp.int32)
     packed = pack_peaks(core.reshape(1), peak_bins, peak_values)
     enc_weights = (enc_weight, swap(enc_weight))
+    dec_weights = (dec_weight, swap(dec_weight))
     dense_own, dense_pair = build_dense(
         place, [packed] + from_others(packed, SPECTRA_AXES), width
     )
@@ -231,13 +232,12 @@
         return near_exchange(rows.astype(BF16).reshape(lax.axis_size(NEAR), -1, hidden_size))
 
     parts = near_parts(sum(map(encode, dense, enc_weights)))
-    parts, sent_weight = lax.optimization_barrier((parts, dec_weight))
-    dec_weights = (dec_weight, swap(sent_weight))
     pre = far_sum(sum_parts(parts)) + enc_bias
     hidden = near_gather(activation(pre).astype(BF16))
-    resid = lax.optimization_barrier(
-        [residual(block, hidden, weight) for block, weight in zip(dense, dec_weights)]
-    )
+    resid = [
+        lax.optimization_barrier(residual(block, hidden, weight))
+        for block, weight in zip(dense, dec_weights)
+    ]
     parts = near_parts(sum(map(decode_back, resid, dec_weights)))
     grad_dec = rows_dot(
         jnp.concatenate([hidden, swap(hidden)]), jnp.concatenate([resid[0], swap(resid[1])])

time: 140 us -> 138 us (0.986)
  waiting for transfers between devices: 17.4 us -> 14.4 us
    ppermute x9, waiting for transfers between devices: 8.33 us -> 5.33 us  [from_others(): lax.ppermute(values, axes, [(i, (i + step) % count) for i in range(count)])]
    ppermute x6, starting transfers between devices: 13 us -> 14.7 us  [swap(): return lax.ppermute(values, 'core', [(0, 1), (1, 0)])]
  transfers between devices with their start and end apart: 16 -> 16, of which waited for: 8 -> 6; matrix products, arithmetic and copies ran while one was open for 5% -> 6% of each run, Pallas kernels for 5% -> 5%
where the time goes in v7:
time: 138 us
  blocking collectives  60.9 us (44%)
  starting transfers between devices  34.9 us (25%)
  matrix products  18.3 us (13%)
  waiting for transfers between devices  14.4 us (10%)
  Pallas kernels  7.15 us (5%)
    all_to_all x3, blocking collectives, near_exchange(): return lax.all_to_all(values, NEAR, 0, 0, tiled=True)  60.9 us
    ppermute x9, starting transfers between devices, from_others(): lax.ppermute(values, axes, [(i, (i + step) % count) for i in range(count)])  16.3 us
    ppermute x6, starting transfers between devices, swap(): return lax.ppermute(values, 'core', [(0, 1), (1, 0)])  14.7 us
    dot_general x3, matrix products, rows_dot(): lax.dot_general(left, right, (((0,), (0,)), ((), ())), preferred_element_...  9.18 us
    pallas_call x4, Pallas kernels, build_dense(): pl.pallas_call(functools.partial(dense_kernel, back=back, groups=groups),...  5.38 us
    ppermute x9, waiting for transfers between devices, from_others(): lax.ppermute(values, axes, [(i, (i + step) % count) for i in range(count)])  5.33 us
    all_to_all x1, waiting for transfers between devices, near_exchange(): return lax.all_to_all(values, NEAR, 0, 0, tiled=True)  4.92 us
    ppermute x6, waiting for transfers between devices, swap(): return lax.ppermute(values, 'core', [(0, 1), (1, 0)])  4.19 us
  transfers between devices with their start and end apart: 16, of which 6 were waited for; matrix products, arithmetic and copies ran while one was open for 6% of the time, Pallas kernels for 5%

profile of v7, /device:TPU:1, one launch (start us, length us, event | category | flops | bytes accessed | tf_op | source)
XLA Modules:
  0.0 137.8 jit_solution(11830662160717525543)
XLA Ops:
  0.6 3.3 %collective-permute-start.3 = (bf16[768,2048]{1,0:T(8,128)(2,1)}, bf16[768,2048]{1,0:T(8,128)(2,1)}, u32[]{:S(2)}, u32[]{:S(2)}) collective-permute-start(bf16[768,2048]{1,0:T(8,128)(2,1)} %param.7), channel_id=1, source_target_pairs={{0,4},{4,0},{1,5},{5,1},{2,6},{6,2},{3,7},{7,3},{8,12},{12,8},{9,1... | collective-permute-start | bytes 9437192 | tf_op jit(solution)/shard_map/ppermute | solution.py:171
  4.0 1.5 %pack_peaks.1.packed_ref = bf16[64,384]{1,0:T(8,128)(2,1)} custom-call(s32[1]{0:T(128)} %bitcast.3.core_ref, s32[128,128]{1,0:T(8,128)} %bins_ref.1, bf16[128,128]{1,0:T(8,128)(2,1)} %values_ref.1), custom_call_target="tpu_custom_call" | custom-call | tf_op jit(solution)/shard_map/pack_peaks/pallas_call | solution.py:47
  5.4 2.9 %collective-permute-start.1 = (bf16[64,384]{1,0:T(8,128)(2,1)}, bf16[64,384]{1,0:T(8,128)(2,1)S(1)}, u32[]{:S(2)}, u32[]{:S(2)}) collective-permute-start(bf16[64,384]{1,0:T(8,128)(2,1)} %pack_peaks.1.packed_ref), channel_id=1, source_target_pairs={{0,2},{1,3},{2,0},{3,1},{4,6},{5,7},{6,4},{7,5},{8,10},{9,11},{10,... | collective-permute-start | bytes 147464 | tf_op jit(solution)/shard_map/ppermute | solution.py:177
  8.3 0.7 collective-permute-start
  9.1 0.1 pad_add_fusion.place_ref
  9.1 0.8 copy-done
  9.9 1.3 build_dense.4
  11.3 1.3 build_dense.5
  12.6 0.0 collective-permute-done.1.packed_ref
  12.7 1.4 build_dense.6
  14.0 0.0 collective-permute-done.packed_ref
  14.0 1.3 build_dense.7
  15.4 0.0 copy-start.1
  15.4 3.0 %fusion.26 = f32[256,2048]{1,0:T(8,128)S(1)} fusion(bf16[256,768]{1,0:T(8,128)(2,1)S(1)} %get-tuple-element.20, bf16[768,2048]{1,0:T(8,128)(2,1)} %collective-permute-done.3), kind=kOutput, calls=%fused_computation.35 | convolution fusion | flops 805306368 | bytes 5636096 | tf_op jit(solution)/shard_map/dot_general | solution.py:215
  18.4 1.1 fusion.3
  19.5 0.0 copy-start.2
  19.5 0.0 copy-start.4
  19.5 24.1 %all_to_all.20.parts_ref = bf16[32,8,2048]{2,1,0:T(8,128)(2,1)S(1)} all-to-all(bf16[32,8,2048]{2,1,0:T(8,128)(2,1)S(1)} %fusion.3), channel_id=1, replica_groups=mesh['x'=4,'zhi'=2,'y'=4,'core'=2,'zp'=2,'zq'=2] {'x','y','zq'}, dimensions={0} | all-to-all | bytes 2097152 | tf_op jit(solution)/shard_map/all_to_all | solution.py:183
  43.6 0.1 sum_parts.2
  43.7 4.7 %collective-permute-start.6 = (bf16[8,2048]{1,0:T(8,128)(2,1)S(1)}, bf16[8,2048]{1,0:T(8,128)(2,1)S(1)}, u32[]{:S(2)}, u32[]{:S(2)}) collective-permute-start(bf16[8,2048]{1,0:T(8,128)(2,1)S(1)} %sum_parts.2), channel_id=1, source_target_pairs={{0,34},{2,0},{32,2},{34,32},{1,35},{3,1},{33,3},{35,33},{4,38},{6,... | collective-permute-start | bytes 98312 | tf_op jit(solution)/shard_map/ppermute | solution.py:177
  48.5 2.6 %collective-permute-start.4 = (bf16[8,2048]{1,0:T(8,128)(2,1)S(1)}, bf16[8,2048]{1,0:T(8,128)(2,1)S(1)}, u32[]{:S(2)}, u32[]{:S(2)}) collective-permute-start(bf16[8,2048]{1,0:T(8,128)(2,1)S(1)} %sum_parts.2), channel_id=1, source_target_pairs={{0,32},{2,34},{32,0},{34,2},{1,33},{3,35},{33,1},{35,3},{4,36},{6,... | collective-permute-start | bytes 98312 | tf_op jit(solution)/shard_map/ppermute | solution.py:177
  51.1 3.2 %collective-permute-start.7 = (bf16[2048,768]{1,0:T(8,128)(2,1)S(1)}, bf16[2048,768]{1,0:T(8,128)(2,1)S(1)}, u32[]{:S(2)}, u32[]{:S(2)}) collective-permute-start(bf16[2048,768]{1,0:T(8,128)(2,1)S(1)} %copy-done.2), channel_id=1, source_target_pairs={{0,4},{4,0},{1,5},{5,1},{2,6},{6,2},{3,7},{7,3},{8,12},{12,8},{9,1... | collective-permute-start | bytes 9437192 | tf_op jit(solution)/shard_map/ppermute | solution.py:171
  54.3 0.8 collective-permute-done.4
  55.2 0.1 broadcast_in_dim.4
  55.3 19.7 %all_to_all.21 = bf16[32,8,2048]{2,1,0:T(8,128)(2,1)S(1)} all-to-all(bf16[32,8,2048]{2,1,0:T(8,128)(2,1)S(1)} %broadcast_in_dim.4), channel_id=1, replica_groups=mesh['x'=4,'zhi'=2,'y'=4,'core'=2,'zp'=2,'zq'=2] {'x','y','zq'}, dimensions={0} | all-to-all | bytes 2097152 | tf_op jit(solution)/shard_map/all_to_all | solution.py:183
  75.0 1.0 subtract_convert_fusion
  76.1 1.0 fusion.27
  77.1 1.0 fusion.7
  78.1 2.0 %fusion.2 = bf16[32,8,2048]{2,1,0:T(8,128)(2,1)} fusion(f32[256,2048]{1,0:T(8,128)S(1)} %fusion.27, bf16[256,768]{1,0:T(8,128)(2,1)S(1)} %fusion.7, bf16[2048,768]{1,0:T(8,128)(2,1)S(1)} %collective-permute-done.7), kind=kOutput, calls=%fused_computation.6 | convolution fusion | flops 806354944 | bytes 6684672 | tf_op jit(solution)/shard_map/dot_general | solution.py:222
  80.1 3.9 %all-to-all-start.2 = ((bf16[32,8,2048]{2,1,0:T(8,128)(2,1)}), bf16[32,8,2048]{2,1,0:T(8,128)(2,1)S(1)}, u32[]{:S(2)}, u32[]{:S(2)}) async-start(bf16[32,8,2048]{2,1,0:T(8,128)(2,1)} %fusion.2), calls=%async_computation.2 | async-start | bytes 2097152 | tf_op jit(solution)/shard_map/all_to_all | solution.py:183
  84.1 2.9 %collective-permute-start.8 = (bf16[256,2048]{1,0:T(8,128)(2,1)S(1)}, bf16[256,2048]{1,0:T(8,128)(2,1)S(1)}, u32[]{:S(2)}, u32[]{:S(2)}) collective-permute-start(bf16[256,2048]{1,0:T(8,128)(2,1)S(1)} %bitcast.32), channel_id=1, source_target_pairs={{0,4},{4,0},{1,5},{5,1},{2,6},{6,2},{3,7},{7,3},{8,12},{12,8},{9,1... | collective-permute-start | bytes 3145736 | tf_op jit(solution)/shard_map/ppermute | solution.py:171
  87.0 0.1 collective-permute-start.9
  87.1 0.4 collective-permute-start.10
  87.5 2.9 %collective-permute-done.9 = bf16[256,768]{1,0:T(8,128)(2,1)S(1)} collective-permute-done((bf16[256,768]{1,0:T(8,128)(2,1)S(1)}, bf16[256,768]{1,0:T(8,128)(2,1)S(1)}, u32[]{:S(2)}, u32[]{:S(2)}) %collective-permute-start.9) | collective-permute-done | bytes 393248 | tf_op jit(solution)/shard_map/ppermute | solution.py:171
  90.4 4.5 %convolution_convert_fusion = bf16[2048,768]{1,0:T(8,128)(2,1)} fusion(bf16[256,2048]{1,0:T(8,128)(2,1)S(1)} %collective-permute-done.8, bf16[256,2048]{1,0:T(8,128)(2,1)S(1)} %bitcast.33, bf16[256,768]{1,0:T(8,128)(2,1)S(1)} %collective-permute-done.9, bf16[256,768]{1,0:T(8,128)(2,1)} %copy-done.3), kind=kOutput, calls=%fused_computation.1 | convolution fusion | flops 1617952768 | bytes 6029312 | tf_op jit(solution)/shard_map/dot_general | solution.py:227
  94.9 4.9 %all-to-all-done.2.parts_ref = bf16[32,8,2048]{2,1,0:T(8,128)(2,1)S(1)} async-done(((bf16[32,8,2048]{2,1,0:T(8,128)(2,1)}), bf16[32,8,2048]{2,1,0:T(8,128)(2,1)S(1)}, u32[]{:S(2)}, u32[]{:S(2)}) %all-to-all-start.2) | async-done | bytes 1048608 | tf_op jit(solution)/shard_map/all_to_all | solution.py:183
  99.8 0.1 sum_parts.3
  100.0 3.1 %collective-permute-start.13 = (bf16[8,2048]{1,0:T(8,128)(2,1)S(1)}, bf16[8,2048]{1,0:T(8,128)(2,1)S(1)}, u32[]{:S(2)}, u32[]{:S(2)}) collective-permute-start(bf16[8,2048]{1,0:T(8,128)(2,1)S(1)} %sum_parts.3), channel_id=1, source_target_pairs={{0,34},{2,0},{32,2},{34,32},{1,35},{3,1},{33,3},{35,33},{4,38},{6,... | collective-permute-start | bytes 98312 | tf_op jit(solution)/shard_map/ppermute | solution.py:177
  103.1 2.2 %collective-permute-start.11 = (bf16[8,2048]{1,0:T(8,128)(2,1)S(1)}, bf16[8,2048]{1,0:T(8,128)(2,1)S(1)}, u32[]{:S(2)}, u32[]{:S(2)}) collective-permute-start(bf16[8,2048]{1,0:T(8,128)(2,1)S(1)} %sum_parts.3), channel_id=1, source_target_pairs={{0,32},{2,34},{32,0},{34,2},{1,33},{3,35},{33,1},{35,3},{4,36},{6,... | collective-permute-start | bytes 98312 | tf_op jit(solution)/shard_map/ppermute | solution.py:177
  105.2 2.7 %collective-permute-done.12 = bf16[8,2048]{1,0:T(8,128)(2,1)S(1)} collective-permute-done((bf16[8,2048]{1,0:T(8,128)(2,1)S(1)}, bf16[8,2048]{1,0:T(8,128)(2,1)S(1)}, u32[]{:S(2)}, u32[]{:S(2)}) %collective-permute-start.12) | collective-permute-done | bytes 32800 | tf_op jit(solution)/shard_map/ppermute | solution.py:177
  107.9 1.8 %collective-permute-done.11 = bf16[8,2048]{1,0:T(8,128)(2,1)S(1)} collective-permute-done((bf16[8,2048]{1,0:T(8,128)(2,1)S(1)}, bf16[8,2048]{1,0:T(8,128)(2,1)S(1)}, u32[]{:S(2)}, u32[]{:S(2)}) %collective-permute-start.11) | collective-permute-done | bytes 32800 | tf_op jit(solution)/shard_map/ppermute | solution.py:177
  109.7 0.1 fusion.17
  109.8 0.1 broadcast_in_dim.5
  109.9 17.2 %all_to_all.22 = bf16[32,8,2048]{2,1,0:T(8,128)(2,1)S(1)} all-to-all(bf16[32,8,2048]{2,1,0:T(8,128)(2,1)S(1)} %broadcast_in_dim.5), channel_id=1, replica_groups=mesh['x'=4,'zhi'=2,'y'=4,'core'=2,'zp'=2,'zq'=2] {'x','y','zq'}, dimensions={0} | all-to-all | bytes 2097152 | tf_op jit(solution)/shard_map/all_to_all | solution.py:183
  127.1 4.7 %collective-permute-start.14 = (bf16[256,2048]{1,0:T(8,128)(2,1)S(1)}, bf16[256,2048]{1,0:T(8,128)(2,1)S(1)}, u32[]{:S(2)}, u32[]{:S(2)}) collective-permute-start(bf16[256,2048]{1,0:T(8,128)(2,1)S(1)} %bitcast.31), channel_id=1, source_target_pairs={{0,4},{4,0},{1,5},{5,1},{2,6},{6,2},{3,7},{7,3},{8,12},{12,8},{9,1... | collective-permute-start | bytes 3145736 | tf_op jit(solution)/shard_map/ppermute | solution.py:171
  131.8 1.0 fusion.19
  132.9 1.3 collective-permute-done.14
  134.1 3.7 %add_convert_fusion = bf16[768,2048]{1,0:T(8,128)(2,1)} fusion(f32[768,2048]{1,0:T(8,128)S(1)} %fusion.19, bf16[256,768]{1,0:T(8,128)(2,1)} %collective-permute-done.10, bf16[256,2048]{1,0:T(8,128)(2,1)S(1)} %collective-permute-done.14), kind=kOutput, calls=%fused_computation | convolution fusion | flops 808452096 | bytes 10878976 | tf_op jit(solution)/shard_map/dot_general | solution.py:227
  (18 shorter events, 0.1 us)
Async XLA Ops:
  0.6 14.8 %collective-permute-start.3 = (bf16[768,2048]{1,0:T(8,128)(2,1)}, bf16[768,2048]{1,0:T(8,128)(2,1)}, u32[]{:S(2)}, u32[]{:S(2)}) collective-permute-start(bf16[768,2048]{1,0:T(8,128)(2,1)} %param.7), channel_id=1, source_target_pairs={{0,4},{4,0},{1,5},{5,1},{2,6},{6,2},{3,7},{7,3},{8,12},{12,8},{9,1... | collective-permute-start | bytes 9437192 | tf_op jit(solution)/shard_map/ppermute | solution.py:171
  5.4 5.8 %collective-permute-start.2 = (bf16[64,384]{1,0:T(8,128)(2,1)}, bf16[64,384]{1,0:T(8,128)(2,1)S(1)}, u32[]{:S(2)}, u32[]{:S(2)}) collective-permute-start(bf16[64,384]{1,0:T(8,128)(2,1)} %pack_peaks.1.packed_ref), channel_id=1, source_target_pairs={{0,1},{1,2},{2,3},{3,0},{4,5},{5,6},{6,7},{7,4},{8,9},{9,10},{10,1... | collective-permute-start | bytes 147464 | tf_op jit(solution)/shard_map/ppermute | solution.py:177
  5.4 7.2 %collective-permute-start.1 = (bf16[64,384]{1,0:T(8,128)(2,1)}, bf16[64,384]{1,0:T(8,128)(2,1)S(1)}, u32[]{:S(2)}, u32[]{:S(2)}) collective-permute-start(bf16[64,384]{1,0:T(8,128)(2,1)} %pack_peaks.1.packed_ref), channel_id=1, source_target_pairs={{0,2},{1,3},{2,0},{3,1},{4,6},{5,7},{6,4},{7,5},{8,10},{9,11},{10,... | collective-permute-start | bytes 147464 | tf_op jit(solution)/shard_map/ppermute | solution.py:177
  8.3 5.7 %collective-permute-start = (bf16[64,384]{1,0:T(8,128)(2,1)}, bf16[64,384]{1,0:T(8,128)(2,1)S(1)}, u32[]{:S(2)}, u32[]{:S(2)}) collective-permute-start(bf16[64,384]{1,0:T(8,128)(2,1)} %pack_peaks.1.packed_ref), channel_id=1, source_target_pairs={{0,3},{1,0},{2,1},{3,2},{4,7},{5,4},{6,5},{7,6},{8,11},{9,8},{10,9... | collective-permute-start | bytes 147464 | tf_op jit(solution)/shard_map/ppermute | solution.py:177
  9.1 0.8 copy-start
  15.4 3.0 %copy-start.1 = (bf16[768,2048]{1,0:T(8,128)(2,1)S(1)}, bf16[768,2048]{1,0:T(8,128)(2,1)}, u32[]{:S(2)}) copy-start(bf16[768,2048]{1,0:T(8,128)(2,1)} %param.7) | copy-start | bytes 9437188
  19.5 31.6 %copy-start.2 = (bf16[2048,768]{1,0:T(8,128)(2,1)S(1)}, bf16[2048,768]{1,0:T(8,128)(2,1)}, u32[]{:S(2)}) copy-start(bf16[2048,768]{1,0:T(8,128)(2,1)} %param.9) | copy-start | bytes 9437188
  19.5 35.6 %copy-start.4 = (f32[2048]{0:T(1024)S(1)}, f32[2048]{0:T(1024)}, u32[]{:S(2)}) copy-start(f32[2048]{0:T(1024)} %param.8) | copy-start | bytes 24580
  43.7 10.6 %collective-permute-start.6 = (bf16[8,2048]{1,0:T(8,128)(2,1)S(1)}, bf16[8,2048]{1,0:T(8,128)(2,1)S(1)}, u32[]{:S(2)}, u32[]{:S(2)}) collective-permute-start(bf16[8,2048]{1,0:T(8,128)(2,1)S(1)} %sum_parts.2), channel_id=1, source_target_pairs={{0,34},{2,0},{32,2},{34,32},{1,35},{3,1},{33,3},{35,33},{4,38},{6,... | collective-permute-start | bytes 98312 | tf_op jit(solution)/shard_map/ppermute | solution.py:177
  48.4 5.9 %collective-permute-start.5 = (bf16[8,2048]{1,0:T(8,128)(2,1)S(1)}, bf16[8,2048]{1,0:T(8,128)(2,1)S(1)}, u32[]{:S(2)}, u32[]{:S(2)}) collective-permute-start(bf16[8,2048]{1,0:T(8,128)(2,1)S(1)} %sum_parts.2), channel_id=1, source_target_pairs={{0,2},{2,32},{32,34},{34,0},{1,3},{3,33},{33,35},{35,1},{4,6},{6,3... | collective-permute-start | bytes 98312 | tf_op jit(solution)/shard_map/ppermute | solution.py:177
  48.5 6.7 %collective-permute-start.4 = (bf16[8,2048]{1,0:T(8,128)(2,1)S(1)}, bf16[8,2048]{1,0:T(8,128)(2,1)S(1)}, u32[]{:S(2)}, u32[]{:S(2)}) collective-permute-start(bf16[8,2048]{1,0:T(8,128)(2,1)S(1)} %sum_parts.2), channel_id=1, source_target_pairs={{0,32},{2,34},{32,0},{34,2},{1,33},{3,35},{33,1},{35,3},{4,36},{6,... | collective-permute-start | bytes 98312 | tf_op jit(solution)/shard_map/ppermute | solution.py:177
  51.1 26.0 %collective-permute-start.7 = (bf16[2048,768]{1,0:T(8,128)(2,1)S(1)}, bf16[2048,768]{1,0:T(8,128)(2,1)S(1)}, u32[]{:S(2)}, u32[]{:S(2)}) collective-permute-start(bf16[2048,768]{1,0:T(8,128)(2,1)S(1)} %copy-done.2), channel_id=1, source_target_pairs={{0,4},{4,0},{1,5},{5,1},{2,6},{6,2},{3,7},{7,3},{8,12},{12,8},{9,1... | collective-permute-start | bytes 9437192 | tf_op jit(solution)/shard_map/ppermute | solution.py:171
  76.0 2.0 %copy-start.3 = (bf16[256,768]{1,0:T(8,128)(2,1)}, bf16[256,768]{1,0:T(8,128)(2,1)S(1)}, u32[]{:S(2)}) copy-start(bf16[256,768]{1,0:T(8,128)(2,1)S(1)} %subtract_convert_fusion) | copy-start | bytes 1179652
  80.1 19.7 %all-to-all-start.2 = ((bf16[32,8,2048]{2,1,0:T(8,128)(2,1)}), bf16[32,8,2048]{2,1,0:T(8,128)(2,1)S(1)}, u32[]{:S(2)}, u32[]{:S(2)}) async-start(bf16[32,8,2048]{2,1,0:T(8,128)(2,1)} %fusion.2), calls=%async_computation.2 | async-start | bytes 2097152 | tf_op jit(solution)/shard_map/all_to_all | solution.py:183
  84.1 6.3 %collective-permute-start.8 = (bf16[256,2048]{1,0:T(8,128)(2,1)S(1)}, bf16[256,2048]{1,0:T(8,128)(2,1)S(1)}, u32[]{:S(2)}, u32[]{:S(2)}) collective-permute-start(bf16[256,2048]{1,0:T(8,128)(2,1)S(1)} %bitcast.32), channel_id=1, source_target_pairs={{0,4},{4,0},{1,5},{5,1},{2,6},{6,2},{3,7},{7,3},{8,12},{12,8},{9,1... | collective-permute-start | bytes 3145736 | tf_op jit(solution)/shard_map/ppermute | solution.py:171
  87.0 3.4 %collective-permute-start.9 = (bf16[256,768]{1,0:T(8,128)(2,1)S(1)}, bf16[256,768]{1,0:T(8,128)(2,1)S(1)}, u32[]{:S(2)}, u32[]{:S(2)}) collective-permute-start(bf16[256,768]{1,0:T(8,128)(2,1)S(1)} %fusion.7), channel_id=1, source_target_pairs={{0,4},{4,0},{1,5},{5,1},{2,6},{6,2},{3,7},{7,3},{8,12},{12,8},{9,1... | collective-permute-start | bytes 1179656 | tf_op jit(solution)/shard_map/ppermute | solution.py:171
  87.1 7.8 %collective-permute-start.10 = (bf16[256,768]{1,0:T(8,128)(2,1)S(1)}, bf16[256,768]{1,0:T(8,128)(2,1)}, u32[]{:S(2)}, u32[]{:S(2)}) collective-permute-start(bf16[256,768]{1,0:T(8,128)(2,1)S(1)} %get-tuple-element.20), channel_id=1, source_target_pairs={{0,4},{4,0},{1,5},{5,1},{2,6},{6,2},{3,7},{7,3},{8,12},{12,8},{9,1... | collective-permute-start | bytes 1179656 | tf_op jit(solution)/shard_map/ppermute | solution.py:171
  100.0 5.3 %collective-permute-start.13 = (bf16[8,2048]{1,0:T(8,128)(2,1)S(1)}, bf16[8,2048]{1,0:T(8,128)(2,1)S(1)}, u32[]{:S(2)}, u32[]{:S(2)}) collective-permute-start(bf16[8,2048]{1,0:T(8,128)(2,1)S(1)} %sum_parts.3), channel_id=1, source_target_pairs={{0,34},{2,0},{32,2},{34,32},{1,35},{3,1},{33,3},{35,33},{4,38},{6,... | collective-permute-start | bytes 98312 | tf_op jit(solution)/shard_map/ppermute | solution.py:177
  103.1 4.9 %collective-permute-start.12 = (bf16[8,2048]{1,0:T(8,128)(2,1)S(1)}, bf16[8,2048]{1,0:T(8,128)(2,1)S(1)}, u32[]{:S(2)}, u32[]{:S(2)}) collective-permute-start(bf16[8,2048]{1,0:T(8,128)(2,1)S(1)} %sum_parts.3), channel_id=1, source_target_pairs={{0,2},{2,32},{32,34},{34,0},{1,3},{3,33},{33,35},{35,1},{4,6},{6,3... | collective-permute-start | bytes 98312 | tf_op jit(solution)/shard_map/ppermute | solution.py:177
  103.1 6.7 %collective-permute-start.11 = (bf16[8,2048]{1,0:T(8,128)(2,1)S(1)}, bf16[8,2048]{1,0:T(8,128)(2,1)S(1)}, u32[]{:S(2)}, u32[]{:S(2)}) collective-permute-start(bf16[8,2048]{1,0:T(8,128)(2,1)S(1)} %sum_parts.3), channel_id=1, source_target_pairs={{0,32},{2,34},{32,0},{34,2},{1,33},{3,35},{33,1},{35,3},{4,36},{6,... | collective-permute-start | bytes 98312 | tf_op jit(solution)/shard_map/ppermute | solution.py:177
  127.1 7.0 %collective-permute-start.14 = (bf16[256,2048]{1,0:T(8,128)(2,1)S(1)}, bf16[256,2048]{1,0:T(8,128)(2,1)S(1)}, u32[]{:S(2)}, u32[]{:S(2)}) collective-permute-start(bf16[256,2048]{1,0:T(8,128)(2,1)S(1)} %bitcast.31), channel_id=1, source_target_pairs={{0,4},{4,0},{1,5},{5,1},{2,6},{6,2},{3,7},{7,3},{8,12},{12,8},{9,1... | collective-permute-start | bytes 3145736 | tf_op jit(solution)/shard_map/ppermute | solution.py:171

commit v8 on v7

--- a/solution.py
+++ b/solution.py
@@ -117,13 +117,14 @@
     lax.fori_loop(0, rows // 16, step, 0, unroll=True)
 
 
-def build_dense(place, blocks, width):
+def build_dense(place, blocks, weights, width):
     groups = len(blocks)
     part = blocks[0].shape
     rows = part[0] * groups
     vmem = pl.BlockSpec(memory_space=pltpu.VMEM)
     dense = ()
     for back, block in enumerate(blocks):
+        early = {groups - 2: weights[:1], groups - 1: weights[1:]}.get(back, ())
         dense = pl.pallas_call(
             functools.partial(dense_kernel, back=back, groups=groups),
             out_shape=(jax.ShapeDtypeStruct((rows, width), BF16),) * 2,
@@ -132,7 +133,8 @@
                 pl.BlockSpec(memory_space=pltpu.SMEM),
                 pl.BlockSpec(part, lambda i: (0, 0)),
             ]
-            + [vmem] * len(dense),
+            + [vmem] * len(dense)
+            + [vmem] * len(early),
             out_specs=(vmem, vmem),
             input_output_aliases={2 + k: k for k in range(len(dense))},
             compiler_params=pltpu.CompilerParams(vmem_limit_bytes=DENSE_VMEM),
@@ -140,7 +142,7 @@
                 flops=1_000_000_000, bytes_accessed=3_000_000, transcendentals=0
             ),
             name="build_dense",
-        )(place, block, *dense)
+        )(place, block, *dense, *early)
     return dense
 
 
@@ -206,10 +208,9 @@
     enc_weights = (enc_weight, swap(enc_weight))
     dec_weights = (dec_weight, swap(dec_weight))
     dense_own, dense_pair = build_dense(
-        place, [packed] + from_others(packed, SPECTRA_AXES), width
+        place, [packed] + from_others(packed, SPECTRA_AXES), enc_weights, width
     )
     dense = (dense_own, dense_pair)
-    dense_other = swap(dense_pair)
 
     def encode(block, weight):
         return jnp.dot(block, weight, preferred_element_type=F32)
@@ -242,8 +243,8 @@
     grad_dec = rows_dot(
         jnp.concatenate([hidden, swap(hidden)]), jnp.concatenate([resid[0], swap(resid[1])])
     ).astype(BF16)
-    parts, grad_dec, dense_other = lax.optimization_barrier((parts, grad_dec, dense_other))
-    back = far_sum(sum_parts(parts))
+    parts, grad_dec, dense_sent = lax.optimization_barrier((parts, grad_dec, dense_pair))
+    back, dense_other = lax.optimization_barrier((far_sum(sum_parts(parts)), swap(dense_sent)))
     dpre = near_gather(slope_times(pre, back))
     grad_own = lax.optimization_barrier(rows_dot(dense_own, dpre))
     grad_enc = (rows_dot(dense_other, swap(dpre)) + grad_own).astype(BF16)

time: 138 us -> 137 us (level)
  matrix products: 18.3 us -> 15.4 us
  waiting for transfers between devices: 14.4 us -> 11.7 us
  starting transfers between devices: 34.9 us -> 36.6 us
  blocking collectives: 60.9 us -> 62.5 us
    ppermute x9, waiting for transfers between devices: 5.33 us -> 1.33 us  [from_others(): lax.ppermute(values, axes, [(i, (i + step) % count) for i in range(count)])]
    dot_general x2, matrix products: 4.07 us -> 2.08 us  [encode(): return jnp.dot(block, weight, preferred_element_type=F32)]
    ppermute x6, starting transfers between devices: 14.7 us -> 16.6 us  [swap(): return lax.ppermute(values, 'core', [(0, 1), (1, 0)])]
    all_to_all x3, blocking collectives: 60.9 us -> 62.5 us  [near_exchange(): return lax.all_to_all(values, NEAR, 0, 0, tiled=True)]
  transfers between devices with their start and end apart: 16 -> 16, of which waited for: 6 -> 6; matrix products, arithmetic and copies ran while one was open for 6% -> 6% of each run, Pallas kernels for 5% -> 4%
where the time goes in v8:
time: 137 us; the launch traced here: 136 us
  blocking collectives  62.5 us (46%)
  starting transfers between devices  36.6 us (27%)
  matrix products  15.4 us (11%)
  waiting for transfers between devices  11.7 us (9%)
  Pallas kernels  7.95 us (6%)
    all_to_all x3, blocking collectives, near_exchange(): return lax.all_to_all(values, NEAR, 0, 0, tiled=True)  62.5 us
    ppermute x6, starting transfers between devices, swap(): return lax.ppermute(values, 'core', [(0, 1), (1, 0)])  16.6 us
    ppermute x9, starting transfers between devices, from_others(): lax.ppermute(values, axes, [(i, (i + step) % count) for i in range(count)])  16.1 us
    dot_general x3, matrix products, rows_dot(): lax.dot_general(left, right, (((0,), (0,)), ((), ())), preferred_element_...  8.19 us
    pallas_call x4, Pallas kernels, build_dense(): pl.pallas_call(functools.partial(dense_kernel, back=back, groups=groups),...  6.18 us
    all_to_all x1, waiting for transfers between devices, near_exchange(): return lax.all_to_all(values, NEAR, 0, 0, tiled=True)  5.48 us
    ppermute x6, waiting for transfers between devices, swap(): return lax.ppermute(values, 'core', [(0, 1), (1, 0)])  4.85 us
    all_to_all x1, starting transfers between devices, near_exchange(): return lax.all_to_all(values, NEAR, 0, 0, tiled=True)  3.93 us
  transfers between devices with their start and end apart: 16, of which 6 were waited for; matrix products, arithmetic and copies ran while one was open for 6% of the time, Pallas kernels for 4%

profile of v8, /device:TPU:1, one launch (start us, length us, event | category | flops | bytes accessed | tf_op | source)
XLA Modules:
  0.0 136.2 jit_solution(12699327290640743178)
XLA Ops:
  0.6 3.3 %collective-permute-start.3 = (bf16[768,2048]{1,0:T(8,128)(2,1)}, bf16[768,2048]{1,0:T(8,128)(2,1)S(1)}, u32[]{:S(2)}, u32[]{:S(2)}) collective-permute-start(bf16[768,2048]{1,0:T(8,128)(2,1)} %refs_2_.1), channel_id=1, source_target_pairs={{0,4},{4,0},{1,5},{5,1},{2,6},{6,2},{3,7},{7,3},{8,12},{12,8},{9,1... | collective-permute-start | bytes 9437192 | tf_op jit(solution)/shard_map/ppermute | solution.py:173
  4.0 1.5 %pack_peaks.1.packed_ref = bf16[64,384]{1,0:T(8,128)(2,1)} custom-call(s32[1]{0:T(128)} %bitcast.3.core_ref, s32[128,128]{1,0:T(8,128)} %bins_ref.1, bf16[128,128]{1,0:T(8,128)(2,1)} %values_ref.1), custom_call_target="tpu_custom_call" | custom-call | tf_op jit(solution)/shard_map/pack_peaks/pallas_call | solution.py:47
  5.4 0.0 collective-permute-start.2
  5.4 2.9 %collective-permute-start.1 = (bf16[64,384]{1,0:T(8,128)(2,1)}, bf16[64,384]{1,0:T(8,128)(2,1)}, u32[]{:S(2)}, u32[]{:S(2)}) collective-permute-start(bf16[64,384]{1,0:T(8,128)(2,1)} %pack_peaks.1.packed_ref), channel_id=1, source_target_pairs={{0,2},{1,3},{2,0},{3,1},{4,6},{5,7},{6,4},{7,5},{8,10},{9,11},{10,... | collective-permute-start | bytes 147464 | tf_op jit(solution)/shard_map/ppermute | solution.py:179
  8.3 0.7 collective-permute-start
  9.1 0.1 pad_add_fusion.place_ref
  9.1 0.8 copy-done.3
  9.9 1.3 build_dense.4
  11.3 1.6 %build_dense.5 = (bf16[256,768]{1,0:T(8,128)(2,1)S(1)}, bf16[256,768]{1,0:T(8,128)(2,1)S(1)}) custom-call(s32[3]{0:T(128)S(1)} %pad_add_fusion.place_ref, bf16[64,384]{1,0:T(8,128)(2,1)} %collective-permute-done.2.packed_ref, bf16[256,768]{1,0:T(8,128)(2,1)S(1)} %get-tuple-element.15.refs_0_, ...), custom_call_target="tpu_custom_call", output_to_operand_aliasing={{0}: (2, {}), {1}: (3, {})} | custom-call | flops 1000000000 | bytes 3000000 | tf_op jit(solution)/shard_map/build_dense/pallas_call | solution.py:128
  12.9 1.6 %build_dense.6 = (bf16[256,768]{1,0:T(8,128)(2,1)S(1)}, bf16[256,768]{1,0:T(8,128)(2,1)S(1)}) custom-call(s32[3]{0:T(128)S(1)} %pad_add_fusion.place_ref, bf16[64,384]{1,0:T(8,128)(2,1)} %collective-permute-done.1.packed_ref, bf16[256,768]{1,0:T(8,128)(2,1)S(1)} %get-tuple-element.17.refs_0_, ...), custom_call_target="tpu_custom_call", output_to_operand_aliasing={{0}: (2, {}), {1}: (3, {})} | custom-call | flops 1000000000 | bytes 3000000 | tf_op jit(solution)/shard_map/build_dense/pallas_call | solution.py:128
  14.5 0.0 collective-permute-done.packed_ref
  14.6 1.6 %build_dense.7 = (bf16[256,768]{1,0:T(8,128)(2,1)S(1)}, bf16[256,768]{1,0:T(8,128)(2,1)S(1)}) custom-call(s32[3]{0:T(128)S(1)} %pad_add_fusion.place_ref, bf16[64,384]{1,0:T(8,128)(2,1)} %collective-permute-done.packed_ref, bf16[256,768]{1,0:T(8,128)(2,1)S(1)} %get-tuple-element.19.refs_0_, ...), custom_call_target="tpu_custom_call", output_to_operand_aliasing={{0}: (2, {}), {1}: (3, {})} | custom-call | flops 1000000000 | bytes 3000000 | tf_op jit(solution)/shard_map/build_dense/pallas_call | solution.py:128
  16.2 1.0 fusion.26
  17.2 1.1 fusion.3
  18.3 0.0 copy-start.4
  18.3 0.0 copy-start.6
  18.3 24.0 %all_to_all.20.parts_ref = bf16[32,8,2048]{2,1,0:T(8,128)(2,1)S(1)} all-to-all(bf16[32,8,2048]{2,1,0:T(8,128)(2,1)S(1)} %fusion.3), channel_id=1, replica_groups=mesh['x'=4,'zhi'=2,'y'=4,'core'=2,'zp'=2,'zq'=2] {'x','y','zq'}, dimensions={0} | all-to-all | bytes 2097152 | tf_op jit(solution)/shard_map/all_to_all | solution.py:185
  42.4 0.1 sum_parts.2
  42.5 4.6 %collective-permute-start.6 = (bf16[8,2048]{1,0:T(8,128)(2,1)S(1)}, bf16[8,2048]{1,0:T(8,128)(2,1)S(1)}, u32[]{:S(2)}, u32[]{:S(2)}) collective-permute-start(bf16[8,2048]{1,0:T(8,128)(2,1)S(1)} %sum_parts.2), channel_id=1, source_target_pairs={{0,34},{2,0},{32,2},{34,32},{1,35},{3,1},{33,3},{35,33},{4,38},{6,... | collective-permute-start | bytes 98312 | tf_op jit(solution)/shard_map/ppermute | solution.py:179
  47.1 2.6 %collective-permute-start.4 = (bf16[8,2048]{1,0:T(8,128)(2,1)S(1)}, bf16[8,2048]{1,0:T(8,128)(2,1)S(1)}, u32[]{:S(2)}, u32[]{:S(2)}) collective-permute-start(bf16[8,2048]{1,0:T(8,128)(2,1)S(1)} %sum_parts.2), channel_id=1, source_target_pairs={{0,32},{2,34},{32,0},{34,2},{1,33},{3,35},{33,1},{35,3},{4,36},{6,... | collective-permute-start | bytes 98312 | tf_op jit(solution)/shard_map/ppermute | solution.py:179
  49.7 3.2 %collective-permute-start.7 = (bf16[2048,768]{1,0:T(8,128)(2,1)S(1)}, bf16[2048,768]{1,0:T(8,128)(2,1)S(1)}, u32[]{:S(2)}, u32[]{:S(2)}) collective-permute-start(bf16[2048,768]{1,0:T(8,128)(2,1)S(1)} %copy-done.4), channel_id=1, source_target_pairs={{0,4},{4,0},{1,5},{5,1},{2,6},{6,2},{3,7},{7,3},{8,12},{12,8},{9,1... | collective-permute-start | bytes 9437192 | tf_op jit(solution)/shard_map/ppermute | solution.py:173
  53.0 0.8 collective-permute-done.4
  53.8 0.1 broadcast_in_dim.4
  54.0 19.7 %all_to_all.21 = bf16[32,8,2048]{2,1,0:T(8,128)(2,1)S(1)} all-to-all(bf16[32,8,2048]{2,1,0:T(8,128)(2,1)S(1)} %broadcast_in_dim.4), channel_id=1, replica_groups=mesh['x'=4,'zhi'=2,'y'=4,'core'=2,'zp'=2,'zq'=2] {'x','y','zq'}, dimensions={0} | all-to-all | bytes 2097152 | tf_op jit(solution)/shard_map/all_to_all | solution.py:185
  73.7 1.0 subtract_convert_fusion
  74.7 1.0 fusion.27
  75.7 0.0 collective-permute-done.7
  75.7 1.0 fusion.7
  76.8 2.0 %fusion.2 = bf16[32,8,2048]{2,1,0:T(8,128)(2,1)} fusion(f32[256,2048]{1,0:T(8,128)S(1)} %fusion.27, bf16[256,768]{1,0:T(8,128)(2,1)S(1)} %fusion.7, bf16[2048,768]{1,0:T(8,128)(2,1)S(1)} %collective-permute-done.7), kind=kOutput, calls=%fused_computation.6 | convolution fusion | flops 806354944 | bytes 6684672 | tf_op jit(solution)/shard_map/dot_general | solution.py:223
  78.8 3.9 %all-to-all-start.2 = ((bf16[32,8,2048]{2,1,0:T(8,128)(2,1)}), bf16[32,8,2048]{2,1,0:T(8,128)(2,1)S(1)}, u32[]{:S(2)}, u32[]{:S(2)}) async-start(bf16[32,8,2048]{2,1,0:T(8,128)(2,1)} %fusion.2), calls=%async_computation.2 | async-start | bytes 2097152 | tf_op jit(solution)/shard_map/all_to_all | solution.py:185
  82.8 2.9 %collective-permute-start.8 = (bf16[256,2048]{1,0:T(8,128)(2,1)S(1)}, bf16[256,2048]{1,0:T(8,128)(2,1)S(1)}, u32[]{:S(2)}, u32[]{:S(2)}) collective-permute-start(bf16[256,2048]{1,0:T(8,128)(2,1)S(1)} %bitcast.32), channel_id=1, source_target_pairs={{0,4},{4,0},{1,5},{5,1},{2,6},{6,2},{3,7},{7,3},{8,12},{12,8},{9,1... | collective-permute-start | bytes 3145736 | tf_op jit(solution)/shard_map/ppermute | solution.py:173
  85.7 0.1 collective-permute-start.9
  85.8 2.7 %collective-permute-done.9 = bf16[256,768]{1,0:T(8,128)(2,1)S(1)} collective-permute-done((bf16[256,768]{1,0:T(8,128)(2,1)S(1)}, bf16[256,768]{1,0:T(8,128)(2,1)S(1)}, u32[]{:S(2)}, u32[]{:S(2)}) %collective-permute-start.9) | collective-permute-done | bytes 393248 | tf_op jit(solution)/shard_map/ppermute | solution.py:173
  88.5 4.5 %convolution_convert_fusion = bf16[2048,768]{1,0:T(8,128)(2,1)} fusion(bf16[256,2048]{1,0:T(8,128)(2,1)S(1)} %collective-permute-done.8, bf16[256,2048]{1,0:T(8,128)(2,1)S(1)} %bitcast.33, bf16[256,768]{1,0:T(8,128)(2,1)S(1)} %collective-permute-done.9, bf16[256,768]{1,0:T(8,128)(2,1)} %copy-done.5), kind=kOutput, calls=%fused_computation.1 | convolution fusion | flops 1617952768 | bytes 6029312 | tf_op jit(solution)/shard_map/dot_general | solution.py:228
  93.0 5.5 %all-to-all-done.2.parts_ref = bf16[32,8,2048]{2,1,0:T(8,128)(2,1)S(1)} async-done(((bf16[32,8,2048]{2,1,0:T(8,128)(2,1)}), bf16[32,8,2048]{2,1,0:T(8,128)(2,1)S(1)}, u32[]{:S(2)}, u32[]{:S(2)}) %all-to-all-start.2) | async-done | bytes 1048608 | tf_op jit(solution)/shard_map/all_to_all | solution.py:185
  98.5 0.1 sum_parts.3
  98.6 3.1 %collective-permute-start.12 = (bf16[8,2048]{1,0:T(8,128)(2,1)S(1)}, bf16[8,2048]{1,0:T(8,128)(2,1)S(1)}, u32[]{:S(2)}, u32[]{:S(2)}) collective-permute-start(bf16[8,2048]{1,0:T(8,128)(2,1)S(1)} %sum_parts.3), channel_id=1, source_target_pairs={{0,34},{2,0},{32,2},{34,32},{1,35},{3,1},{33,3},{35,33},{4,38},{6,... | collective-permute-start | bytes 98312 | tf_op jit(solution)/shard_map/ppermute | solution.py:179
  101.8 2.2 %collective-permute-start.10 = (bf16[8,2048]{1,0:T(8,128)(2,1)S(1)}, bf16[8,2048]{1,0:T(8,128)(2,1)S(1)}, u32[]{:S(2)}, u32[]{:S(2)}) collective-permute-start(bf16[8,2048]{1,0:T(8,128)(2,1)S(1)} %sum_parts.3), channel_id=1, source_target_pairs={{0,32},{2,34},{32,0},{34,2},{1,33},{3,35},{33,1},{35,3},{4,36},{6,... | collective-permute-start | bytes 98312 | tf_op jit(solution)/shard_map/ppermute | solution.py:179
  103.9 4.0 %collective-permute-start.13 = (bf16[256,768]{1,0:T(8,128)(2,1)S(1)}, bf16[256,768]{1,0:T(8,128)(2,1)S(1)}, u32[]{:S(2)}, u32[]{:S(2)}) collective-permute-start(bf16[256,768]{1,0:T(8,128)(2,1)S(1)} %copy-done.2), channel_id=1, source_target_pairs={{0,4},{4,0},{1,5},{5,1},{2,6},{6,2},{3,7},{7,3},{8,12},{12,8},{9,1... | collective-permute-start | bytes 1179656 | tf_op jit(solution)/shard_map/ppermute | solution.py:173
  107.9 0.5 collective-permute-done.10
  108.5 0.8 collective-permute-done.13
  109.3 0.1 fusion.17
  109.4 0.1 broadcast_in_dim.5
  109.5 18.8 %all_to_all.22 = bf16[32,8,2048]{2,1,0:T(8,128)(2,1)S(1)} all-to-all(bf16[32,8,2048]{2,1,0:T(8,128)(2,1)S(1)} %broadcast_in_dim.5), channel_id=1, replica_groups=mesh['x'=4,'zhi'=2,'y'=4,'core'=2,'zp'=2,'zq'=2] {'x','y','zq'}, dimensions={0} | all-to-all | bytes 2097152 | tf_op jit(solution)/shard_map/all_to_all | solution.py:185
  128.3 3.0 %collective-permute-start.14 = (bf16[256,2048]{1,0:T(8,128)(2,1)S(1)}, bf16[256,2048]{1,0:T(8,128)(2,1)S(1)}, u32[]{:S(2)}, u32[]{:S(2)}) collective-permute-start(bf16[256,2048]{1,0:T(8,128)(2,1)S(1)} %bitcast.31), channel_id=1, source_target_pairs={{0,4},{4,0},{1,5},{5,1},{2,6},{6,2},{3,7},{7,3},{8,12},{12,8},{9,1... | collective-permute-start | bytes 3145736 | tf_op jit(solution)/shard_map/ppermute | solution.py:173
  131.3 1.0 fusion.19
  132.3 1.3 collective-permute-done.14
  133.6 2.7 %add_convert_fusion = bf16[768,2048]{1,0:T(8,128)(2,1)} fusion(f32[768,2048]{1,0:T(8,128)S(1)} %fusion.19, bf16[256,768]{1,0:T(8,128)(2,1)S(1)} %collective-permute-done.13, bf16[256,2048]{1,0:T(8,128)(2,1)S(1)} %collective-permute-done.14), kind=kOutput, calls=%fused_computation | convolution fusion | flops 808452096 | bytes 10878976 | tf_op jit(solution)/shard_map/dot_general | solution.py:228
  (23 shorter events, 0.1 us)
Async XLA Ops:
  0.6 13.9 %collective-permute-start.3 = (bf16[768,2048]{1,0:T(8,128)(2,1)}, bf16[768,2048]{1,0:T(8,128)(2,1)S(1)}, u32[]{:S(2)}, u32[]{:S(2)}) collective-permute-start(bf16[768,2048]{1,0:T(8,128)(2,1)} %refs_2_.1), channel_id=1, source_target_pairs={{0,4},{4,0},{1,5},{5,1},{2,6},{6,2},{3,7},{7,3},{8,12},{12,8},{9,1... | collective-permute-start | bytes 9437192 | tf_op jit(solution)/shard_map/ppermute | solution.py:173
  5.4 5.8 %collective-permute-start.2 = (bf16[64,384]{1,0:T(8,128)(2,1)}, bf16[64,384]{1,0:T(8,128)(2,1)}, u32[]{:S(2)}, u32[]{:S(2)}) collective-permute-start(bf16[64,384]{1,0:T(8,128)(2,1)} %pack_peaks.1.packed_ref), channel_id=1, source_target_pairs={{0,1},{1,2},{2,3},{3,0},{4,5},{5,6},{6,7},{7,4},{8,9},{9,10},{10,1... | collective-permute-start | bytes 147464 | tf_op jit(solution)/shard_map/ppermute | solution.py:179
  5.4 7.5 %collective-permute-start.1 = (bf16[64,384]{1,0:T(8,128)(2,1)}, bf16[64,384]{1,0:T(8,128)(2,1)}, u32[]{:S(2)}, u32[]{:S(2)}) collective-permute-start(bf16[64,384]{1,0:T(8,128)(2,1)} %pack_peaks.1.packed_ref), channel_id=1, source_target_pairs={{0,2},{1,3},{2,0},{3,1},{4,6},{5,7},{6,4},{7,5},{8,10},{9,11},{10,... | collective-permute-start | bytes 147464 | tf_op jit(solution)/shard_map/ppermute | solution.py:179
  8.3 6.2 %collective-permute-start = (bf16[64,384]{1,0:T(8,128)(2,1)}, bf16[64,384]{1,0:T(8,128)(2,1)}, u32[]{:S(2)}, u32[]{:S(2)}) collective-permute-start(bf16[64,384]{1,0:T(8,128)(2,1)} %pack_peaks.1.packed_ref), channel_id=1, source_target_pairs={{0,3},{1,0},{2,1},{3,2},{4,7},{5,4},{6,5},{7,6},{8,11},{9,8},{10,9... | collective-permute-start | bytes 147464 | tf_op jit(solution)/shard_map/ppermute | solution.py:179
  9.1 0.8 copy-start.3
  9.9 3.0 %copy-start = (bf16[768,2048]{1,0:T(8,128)(2,1)S(1)}, bf16[768,2048]{1,0:T(8,128)(2,1)}, u32[]{:S(2)}) copy-start(bf16[768,2048]{1,0:T(8,128)(2,1)} %refs_2_.1) | copy-start | bytes 9437188
  16.2 59.5 %copy-start.1 = (bf16[256,768]{1,0:T(8,128)(2,1)}, bf16[256,768]{1,0:T(8,128)(2,1)S(1)}, u32[]{:S(2)}) copy-start(bf16[256,768]{1,0:T(8,128)(2,1)S(1)} %get-tuple-element.24) | copy-start | bytes 1179652
  18.3 31.4 %copy-start.4 = (bf16[2048,768]{1,0:T(8,128)(2,1)S(1)}, bf16[2048,768]{1,0:T(8,128)(2,1)}, u32[]{:S(2)}) copy-start(bf16[2048,768]{1,0:T(8,128)(2,1)} %param.9) | copy-start | bytes 9437188
  18.3 35.5 %copy-start.6 = (f32[2048]{0:T(1024)S(1)}, f32[2048]{0:T(1024)}, u32[]{:S(2)}) copy-start(f32[2048]{0:T(1024)} %param.8) | copy-start | bytes 24580
  42.5 10.5 %collective-permute-start.6 = (bf16[8,2048]{1,0:T(8,128)(2,1)S(1)}, bf16[8,2048]{1,0:T(8,128)(2,1)S(1)}, u32[]{:S(2)}, u32[]{:S(2)}) collective-permute-start(bf16[8,2048]{1,0:T(8,128)(2,1)S(1)} %sum_parts.2), channel_id=1, source_target_pairs={{0,34},{2,0},{32,2},{34,32},{1,35},{3,1},{33,3},{35,33},{4,38},{6,... | collective-permute-start | bytes 98312 | tf_op jit(solution)/shard_map/ppermute | solution.py:179
  47.1 5.9 %collective-permute-start.5 = (bf16[8,2048]{1,0:T(8,128)(2,1)S(1)}, bf16[8,2048]{1,0:T(8,128)(2,1)S(1)}, u32[]{:S(2)}, u32[]{:S(2)}) collective-permute-start(bf16[8,2048]{1,0:T(8,128)(2,1)S(1)} %sum_parts.2), channel_id=1, source_target_pairs={{0,2},{2,32},{32,34},{34,0},{1,3},{3,33},{33,35},{35,1},{4,6},{6,3... | collective-permute-start | bytes 98312 | tf_op jit(solution)/shard_map/ppermute | solution.py:179
  47.1 6.7 %collective-permute-start.4 = (bf16[8,2048]{1,0:T(8,128)(2,1)S(1)}, bf16[8,2048]{1,0:T(8,128)(2,1)S(1)}, u32[]{:S(2)}, u32[]{:S(2)}) collective-permute-start(bf16[8,2048]{1,0:T(8,128)(2,1)S(1)} %sum_parts.2), channel_id=1, source_target_pairs={{0,32},{2,34},{32,0},{34,2},{1,33},{3,35},{33,1},{35,3},{4,36},{6,... | collective-permute-start | bytes 98312 | tf_op jit(solution)/shard_map/ppermute | solution.py:179
  49.7 26.0 %collective-permute-start.7 = (bf16[2048,768]{1,0:T(8,128)(2,1)S(1)}, bf16[2048,768]{1,0:T(8,128)(2,1)S(1)}, u32[]{:S(2)}, u32[]{:S(2)}) collective-permute-start(bf16[2048,768]{1,0:T(8,128)(2,1)S(1)} %copy-done.4), channel_id=1, source_target_pairs={{0,4},{4,0},{1,5},{5,1},{2,6},{6,2},{3,7},{7,3},{8,12},{12,8},{9,1... | collective-permute-start | bytes 9437192 | tf_op jit(solution)/shard_map/ppermute | solution.py:173
  74.7 2.1 %copy-start.5 = (bf16[256,768]{1,0:T(8,128)(2,1)}, bf16[256,768]{1,0:T(8,128)(2,1)S(1)}, u32[]{:S(2)}) copy-start(bf16[256,768]{1,0:T(8,128)(2,1)S(1)} %subtract_convert_fusion) | copy-start | bytes 1179652
  78.8 19.7 %all-to-all-start.2 = ((bf16[32,8,2048]{2,1,0:T(8,128)(2,1)}), bf16[32,8,2048]{2,1,0:T(8,128)(2,1)S(1)}, u32[]{:S(2)}, u32[]{:S(2)}) async-start(bf16[32,8,2048]{2,1,0:T(8,128)(2,1)} %fusion.2), calls=%async_computation.2 | async-start | bytes 2097152 | tf_op jit(solution)/shard_map/all_to_all | solution.py:185
  82.8 21.2 %copy-start.2 = (bf16[256,768]{1,0:T(8,128)(2,1)S(1)}, bf16[256,768]{1,0:T(8,128)(2,1)}, u32[]{:S(2)}) copy-start(bf16[256,768]{1,0:T(8,128)(2,1)} %copy-done.1) | copy-start | bytes 1179652
  82.8 5.7 %collective-permute-start.8 = (bf16[256,2048]{1,0:T(8,128)(2,1)S(1)}, bf16[256,2048]{1,0:T(8,128)(2,1)S(1)}, u32[]{:S(2)}, u32[]{:S(2)}) collective-permute-start(bf16[256,2048]{1,0:T(8,128)(2,1)S(1)} %bitcast.32), channel_id=1, source_target_pairs={{0,4},{4,0},{1,5},{5,1},{2,6},{6,2},{3,7},{7,3},{8,12},{12,8},{9,1... | collective-permute-start | bytes 3145736 | tf_op jit(solution)/shard_map/ppermute | solution.py:173
  85.7 2.8 %collective-permute-start.9 = (bf16[256,768]{1,0:T(8,128)(2,1)S(1)}, bf16[256,768]{1,0:T(8,128)(2,1)S(1)}, u32[]{:S(2)}, u32[]{:S(2)}) collective-permute-start(bf16[256,768]{1,0:T(8,128)(2,1)S(1)} %fusion.7), channel_id=1, source_target_pairs={{0,4},{4,0},{1,5},{5,1},{2,6},{6,2},{3,7},{7,3},{8,12},{12,8},{9,1... | collective-permute-start | bytes 1179656 | tf_op jit(solution)/shard_map/ppermute | solution.py:173
  98.6 9.3 %collective-permute-start.12 = (bf16[8,2048]{1,0:T(8,128)(2,1)S(1)}, bf16[8,2048]{1,0:T(8,128)(2,1)S(1)}, u32[]{:S(2)}, u32[]{:S(2)}) collective-permute-start(bf16[8,2048]{1,0:T(8,128)(2,1)S(1)} %sum_parts.3), channel_id=1, source_target_pairs={{0,34},{2,0},{32,2},{34,32},{1,35},{3,1},{33,3},{35,33},{4,38},{6,... | collective-permute-start | bytes 98312 | tf_op jit(solution)/shard_map/ppermute | solution.py:179
  101.8 6.2 %collective-permute-start.11 = (bf16[8,2048]{1,0:T(8,128)(2,1)S(1)}, bf16[8,2048]{1,0:T(8,128)(2,1)S(1)}, u32[]{:S(2)}, u32[]{:S(2)}) collective-permute-start(bf16[8,2048]{1,0:T(8,128)(2,1)S(1)} %sum_parts.3), channel_id=1, source_target_pairs={{0,2},{2,32},{32,34},{34,0},{1,3},{3,33},{33,35},{35,1},{4,6},{6,3... | collective-permute-start | bytes 98312 | tf_op jit(solution)/shard_map/ppermute | solution.py:179
  101.8 6.7 %collective-permute-start.10 = (bf16[8,2048]{1,0:T(8,128)(2,1)S(1)}, bf16[8,2048]{1,0:T(8,128)(2,1)S(1)}, u32[]{:S(2)}, u32[]{:S(2)}) collective-permute-start(bf16[8,2048]{1,0:T(8,128)(2,1)S(1)} %sum_parts.3), channel_id=1, source_target_pairs={{0,32},{2,34},{32,0},{34,2},{1,33},{3,35},{33,1},{35,3},{4,36},{6,... | collective-permute-start | bytes 98312 | tf_op jit(solution)/shard_map/ppermute | solution.py:179
  103.9 5.3 %collective-permute-start.13 = (bf16[256,768]{1,0:T(8,128)(2,1)S(1)}, bf16[256,768]{1,0:T(8,128)(2,1)S(1)}, u32[]{:S(2)}, u32[]{:S(2)}) collective-permute-start(bf16[256,768]{1,0:T(8,128)(2,1)S(1)} %copy-done.2), channel_id=1, source_target_pairs={{0,4},{4,0},{1,5},{5,1},{2,6},{6,2},{3,7},{7,3},{8,12},{12,8},{9,1... | collective-permute-start | bytes 1179656 | tf_op jit(solution)/shard_map/ppermute | solution.py:173
  128.3 5.3 %collective-permute-start.14 = (bf16[256,2048]{1,0:T(8,128)(2,1)S(1)}, bf16[256,2048]{1,0:T(8,128)(2,1)S(1)}, u32[]{:S(2)}, u32[]{:S(2)}) collective-permute-start(bf16[256,2048]{1,0:T(8,128)(2,1)S(1)} %bitcast.31), channel_id=1, source_target_pairs={{0,4},{4,0},{1,5},{5,1},{2,6},{6,2},{3,7},{7,3},{8,12},{12,8},{9,1... | collective-permute-start | bytes 3145736 | tf_op jit(solution)/shard_map/ppermute | solution.py:173

commit v9 on v8

--- a/solution.py
+++ b/solution.py
@@ -187,7 +187,7 @@
 
 def far_sum(sent):
     one, two, three = [block.astype(F32) for block in from_others(sent, FAR)]
-    return (sent.astype(F32) + two) + (one + three)
+    return (one + three) + (sent.astype(F32) + two)
 
 
 def near_gather(values):

time: 137 us -> 138 us (level)
  starting transfers between devices: 36.6 us -> 39.3 us
    ppermute x9, starting transfers between devices: 16.1 us -> 18.4 us  [from_others(): lax.ppermute(values, axes, [(i, (i + step) % count) for i in range(count)])]
  transfers between devices with their start and end apart: 16 -> 16, of which waited for: 6 -> 4; matrix products, arithmetic and copies ran while one was open for 6% -> 6% of each run, Pallas kernels for 4% -> 4%
where the time goes in v9:
time: 138 us; the launch traced here: 137 us
  blocking collectives  61.8 us (45%)
  starting transfers between devices  39.3 us (28%)
  matrix products  15.4 us (11%)
  waiting for transfers between devices  10.8 us (8%)
  Pallas kernels  7.95 us (6%)
    all_to_all x3, blocking collectives, near_exchange(): return lax.all_to_all(values, NEAR, 0, 0, tiled=True)  61.8 us
    ppermute x9, starting transfers between devices, from_others(): lax.ppermute(values, axes, [(i, (i + step) % count) for i in range(count)])  18.4 us
    ppermute x6, starting transfers between devices, swap(): return lax.ppermute(values, 'core', [(0, 1), (1, 0)])  17 us
    dot_general x3, matrix products, rows_dot(): lax.dot_general(left, right, (((0,), (0,)), ((), ())), preferred_element_...  8.18 us
    pallas_call x4, Pallas kernels, build_dense(): pl.pallas_call(functools.partial(dense_kernel, back=back, groups=groups),...  6.18 us
    all_to_all x1, waiting for transfers between devices, near_exchange(): return lax.all_to_all(values, NEAR, 0, 0, tiled=True)  5.45 us
    ppermute x6, waiting for transfers between devices, swap(): return lax.ppermute(values, 'core', [(0, 1), (1, 0)])  5.35 us
    all_to_all x1, starting transfers between devices, near_exchange(): return lax.all_to_all(values, NEAR, 0, 0, tiled=True)  3.93 us
  transfers between devices with their start and end apart: 16, of which 4 were waited for; matrix products, arithmetic and copies ran while one was open for 6% of the time, Pallas kernels for 4%

profile of v9, /device:TPU:1, one launch (start us, length us, event | category | flops | bytes accessed | tf_op | source)
XLA Modules:
  0.0 137.4 jit_solution(4570875427570323640)
XLA Ops:
  0.6 3.3 %collective-permute-start.3 = (bf16[768,2048]{1,0:T(8,128)(2,1)}, bf16[768,2048]{1,0:T(8,128)(2,1)S(1)}, u32[]{:S(2)}, u32[]{:S(2)}) collective-permute-start(bf16[768,2048]{1,0:T(8,128)(2,1)} %refs_2_.1), channel_id=1, source_target_pairs={{0,4},{4,0},{1,5},{5,1},{2,6},{6,2},{3,7},{7,3},{8,12},{12,8},{9,1... | collective-permute-start | bytes 9437192 | tf_op jit(solution)/shard_map/ppermute | solution.py:173
  4.0 1.5 %pack_peaks.1.packed_ref = bf16[64,384]{1,0:T(8,128)(2,1)} custom-call(s32[1]{0:T(128)} %bitcast.3.core_ref, s32[128,128]{1,0:T(8,128)} %bins_ref.1, bf16[128,128]{1,0:T(8,128)(2,1)} %values_ref.1), custom_call_target="tpu_custom_call" | custom-call | tf_op jit(solution)/shard_map/pack_peaks/pallas_call | solution.py:47
  5.4 0.0 collective-permute-start.2
  5.4 2.9 %collective-permute-start.1 = (bf16[64,384]{1,0:T(8,128)(2,1)}, bf16[64,384]{1,0:T(8,128)(2,1)}, u32[]{:S(2)}, u32[]{:S(2)}) collective-permute-start(bf16[64,384]{1,0:T(8,128)(2,1)} %pack_peaks.1.packed_ref), channel_id=1, source_target_pairs={{0,2},{1,3},{2,0},{3,1},{4,6},{5,7},{6,4},{7,5},{8,10},{9,11},{10,... | collective-permute-start | bytes 147464 | tf_op jit(solution)/shard_map/ppermute | solution.py:179
  8.3 0.7 collective-permute-start
  9.1 0.1 pad_add_fusion.place_ref
  9.1 0.8 copy-done.3
  9.9 1.3 build_dense.4
  11.3 1.6 %build_dense.5 = (bf16[256,768]{1,0:T(8,128)(2,1)S(1)}, bf16[256,768]{1,0:T(8,128)(2,1)S(1)}) custom-call(s32[3]{0:T(128)S(1)} %pad_add_fusion.place_ref, bf16[64,384]{1,0:T(8,128)(2,1)} %collective-permute-done.2.packed_ref, bf16[256,768]{1,0:T(8,128)(2,1)S(1)} %get-tuple-element.15.refs_0_, ...), custom_call_target="tpu_custom_call", output_to_operand_aliasing={{0}: (2, {}), {1}: (3, {})} | custom-call | flops 1000000000 | bytes 3000000 | tf_op jit(solution)/shard_map/build_dense/pallas_call | solution.py:128
  12.9 1.6 %build_dense.6 = (bf16[256,768]{1,0:T(8,128)(2,1)S(1)}, bf16[256,768]{1,0:T(8,128)(2,1)S(1)}) custom-call(s32[3]{0:T(128)S(1)} %pad_add_fusion.place_ref, bf16[64,384]{1,0:T(8,128)(2,1)} %collective-permute-done.1.packed_ref, bf16[256,768]{1,0:T(8,128)(2,1)S(1)} %get-tuple-element.17.refs_0_, ...), custom_call_target="tpu_custom_call", output_to_operand_aliasing={{0}: (2, {}), {1}: (3, {})} | custom-call | flops 1000000000 | bytes 3000000 | tf_op jit(solution)/shard_map/build_dense/pallas_call | solution.py:128
  14.5 0.0 collective-permute-done.packed_ref
  14.6 1.6 %build_dense.7 = (bf16[256,768]{1,0:T(8,128)(2,1)S(1)}, bf16[256,768]{1,0:T(8,128)(2,1)S(1)}) custom-call(s32[3]{0:T(128)S(1)} %pad_add_fusion.place_ref, bf16[64,384]{1,0:T(8,128)(2,1)} %collective-permute-done.packed_ref, bf16[256,768]{1,0:T(8,128)(2,1)S(1)} %get-tuple-element.19.refs_0_, ...), custom_call_target="tpu_custom_call", output_to_operand_aliasing={{0}: (2, {}), {1}: (3, {})} | custom-call | flops 1000000000 | bytes 3000000 | tf_op jit(solution)/shard_map/build_dense/pallas_call | solution.py:128
  16.2 1.0 fusion.26
  17.2 1.1 fusion.3
  18.3 0.0 copy-start.4
  18.3 0.0 copy-start.6
  18.3 24.0 %all_to_all.20.parts_ref = bf16[32,8,2048]{2,1,0:T(8,128)(2,1)S(1)} all-to-all(bf16[32,8,2048]{2,1,0:T(8,128)(2,1)S(1)} %fusion.3), channel_id=1, replica_groups=mesh['x'=4,'zhi'=2,'y'=4,'core'=2,'zp'=2,'zq'=2] {'x','y','zq'}, dimensions={0} | all-to-all | bytes 2097152 | tf_op jit(solution)/shard_map/all_to_all | solution.py:185
  42.4 0.1 sum_parts.2
  42.5 4.9 %collective-permute-start.6 = (bf16[8,2048]{1,0:T(8,128)(2,1)S(1)}, bf16[8,2048]{1,0:T(8,128)(2,1)S(1)}, u32[]{:S(2)}, u32[]{:S(2)}) collective-permute-start(bf16[8,2048]{1,0:T(8,128)(2,1)S(1)} %sum_parts.2), channel_id=1, source_target_pairs={{0,32},{2,34},{32,0},{34,2},{1,33},{3,35},{33,1},{35,3},{4,36},{6,... | collective-permute-start | bytes 98312 | tf_op jit(solution)/shard_map/ppermute | solution.py:179
  47.4 2.4 %collective-permute-start.4 = (bf16[8,2048]{1,0:T(8,128)(2,1)S(1)}, bf16[8,2048]{1,0:T(8,128)(2,1)S(1)}, u32[]{:S(2)}, u32[]{:S(2)}) collective-permute-start(bf16[8,2048]{1,0:T(8,128)(2,1)S(1)} %sum_parts.2), channel_id=1, source_target_pairs={{0,2},{2,32},{32,34},{34,0},{1,3},{3,33},{33,35},{35,1},{4,6},{6,3... | collective-permute-start | bytes 98312 | tf_op jit(solution)/shard_map/ppermute | solution.py:179
  49.7 3.2 %collective-permute-start.7 = (bf16[2048,768]{1,0:T(8,128)(2,1)S(1)}, bf16[2048,768]{1,0:T(8,128)(2,1)S(1)}, u32[]{:S(2)}, u32[]{:S(2)}) collective-permute-start(bf16[2048,768]{1,0:T(8,128)(2,1)S(1)} %copy-done.4), channel_id=1, source_target_pairs={{0,4},{4,0},{1,5},{5,1},{2,6},{6,2},{3,7},{7,3},{8,12},{12,8},{9,1... | collective-permute-start | bytes 9437192 | tf_op jit(solution)/shard_map/ppermute | solution.py:173
  53.0 0.0 collective-permute-done.6
  53.0 0.1 multiply_convert_fusion
  53.1 0.1 broadcast_in_dim.4
  53.2 19.1 %all_to_all.21 = bf16[32,8,2048]{2,1,0:T(8,128)(2,1)S(1)} all-to-all(bf16[32,8,2048]{2,1,0:T(8,128)(2,1)S(1)} %broadcast_in_dim.4), channel_id=1, replica_groups=mesh['x'=4,'zhi'=2,'y'=4,'core'=2,'zp'=2,'zq'=2] {'x','y','zq'}, dimensions={0} | all-to-all | bytes 2097152 | tf_op jit(solution)/shard_map/all_to_all | solution.py:185
  72.3 1.0 subtract_convert_fusion
  73.3 1.0 fusion.27
  74.4 1.0 fusion.7
  75.4 2.0 %fusion.2 = bf16[32,8,2048]{2,1,0:T(8,128)(2,1)} fusion(f32[256,2048]{1,0:T(8,128)S(1)} %fusion.27, bf16[256,768]{1,0:T(8,128)(2,1)S(1)} %fusion.7, bf16[2048,768]{1,0:T(8,128)(2,1)S(1)} %collective-permute-done.7), kind=kOutput, calls=%fused_computation.6 | convolution fusion | flops 806354944 | bytes 6684672 | tf_op jit(solution)/shard_map/dot_general | solution.py:223
  77.5 3.9 %all-to-all-start.2 = ((bf16[32,8,2048]{2,1,0:T(8,128)(2,1)}), bf16[32,8,2048]{2,1,0:T(8,128)(2,1)S(1)}, u32[]{:S(2)}, u32[]{:S(2)}) async-start(bf16[32,8,2048]{2,1,0:T(8,128)(2,1)} %fusion.2), calls=%async_computation.2 | async-start | bytes 2097152 | tf_op jit(solution)/shard_map/all_to_all | solution.py:185
  81.4 2.9 %collective-permute-start.8 = (bf16[256,2048]{1,0:T(8,128)(2,1)S(1)}, bf16[256,2048]{1,0:T(8,128)(2,1)S(1)}, u32[]{:S(2)}, u32[]{:S(2)}) collective-permute-start(bf16[256,2048]{1,0:T(8,128)(2,1)S(1)} %bitcast.32), channel_id=1, source_target_pairs={{0,4},{4,0},{1,5},{5,1},{2,6},{6,2},{3,7},{7,3},{8,12},{12,8},{9,1... | collective-permute-start | bytes 3145736 | tf_op jit(solution)/shard_map/ppermute | solution.py:173
  84.3 0.1 collective-permute-start.9
  84.4 2.7 %collective-permute-done.9 = bf16[256,768]{1,0:T(8,128)(2,1)S(1)} collective-permute-done((bf16[256,768]{1,0:T(8,128)(2,1)S(1)}, bf16[256,768]{1,0:T(8,128)(2,1)S(1)}, u32[]{:S(2)}, u32[]{:S(2)}) %collective-permute-start.9) | collective-permute-done | bytes 393248 | tf_op jit(solution)/shard_map/ppermute | solution.py:173
  87.1 4.5 %convolution_convert_fusion = bf16[2048,768]{1,0:T(8,128)(2,1)} fusion(bf16[256,2048]{1,0:T(8,128)(2,1)S(1)} %collective-permute-done.8, bf16[256,2048]{1,0:T(8,128)(2,1)S(1)} %bitcast.33, bf16[256,768]{1,0:T(8,128)(2,1)S(1)} %collective-permute-done.9, bf16[256,768]{1,0:T(8,128)(2,1)} %copy-done.5), kind=kOutput, calls=%fused_computation.1 | convolution fusion | flops 1617952768 | bytes 6029312 | tf_op jit(solution)/shard_map/dot_general | solution.py:228
  91.6 5.5 %all-to-all-done.2.parts_ref = bf16[32,8,2048]{2,1,0:T(8,128)(2,1)S(1)} async-done(((bf16[32,8,2048]{2,1,0:T(8,128)(2,1)}), bf16[32,8,2048]{2,1,0:T(8,128)(2,1)S(1)}, u32[]{:S(2)}, u32[]{:S(2)}) %all-to-all-start.2) | async-done | bytes 1048608 | tf_op jit(solution)/shard_map/all_to_all | solution.py:185
  97.1 0.1 sum_parts.3
  97.2 5.2 %collective-permute-start.12 = (bf16[8,2048]{1,0:T(8,128)(2,1)S(1)}, bf16[8,2048]{1,0:T(8,128)(2,1)S(1)}, u32[]{:S(2)}, u32[]{:S(2)}) collective-permute-start(bf16[8,2048]{1,0:T(8,128)(2,1)S(1)} %sum_parts.3), channel_id=1, source_target_pairs={{0,32},{2,34},{32,0},{34,2},{1,33},{3,35},{33,1},{35,3},{4,36},{6,... | collective-permute-start | bytes 98312 | tf_op jit(solution)/shard_map/ppermute | solution.py:179
  102.4 0.9 collective-permute-start.11
  103.3 1.5 %collective-permute-start.10 = (bf16[8,2048]{1,0:T(8,128)(2,1)S(1)}, bf16[8,2048]{1,0:T(8,128)(2,1)S(1)}, u32[]{:S(2)}, u32[]{:S(2)}) collective-permute-start(bf16[8,2048]{1,0:T(8,128)(2,1)S(1)} %sum_parts.3), channel_id=1, source_target_pairs={{0,2},{2,32},{32,34},{34,0},{1,3},{3,33},{33,35},{35,1},{4,6},{6,3... | collective-permute-start | bytes 98312 | tf_op jit(solution)/shard_map/ppermute | solution.py:179
  104.8 4.3 %collective-permute-start.13 = (bf16[256,768]{1,0:T(8,128)(2,1)S(1)}, bf16[256,768]{1,0:T(8,128)(2,1)S(1)}, u32[]{:S(2)}, u32[]{:S(2)}) collective-permute-start(bf16[256,768]{1,0:T(8,128)(2,1)S(1)} %copy-done.2), channel_id=1, source_target_pairs={{0,4},{4,0},{1,5},{5,1},{2,6},{6,2},{3,7},{7,3},{8,12},{12,8},{9,1... | collective-permute-start | bytes 1179656 | tf_op jit(solution)/shard_map/ppermute | solution.py:173
  109.1 1.3 collective-permute-done.13
  110.4 0.1 fusion.17
  110.5 0.1 broadcast_in_dim.5
  110.6 18.6 %all_to_all.22 = bf16[32,8,2048]{2,1,0:T(8,128)(2,1)S(1)} all-to-all(bf16[32,8,2048]{2,1,0:T(8,128)(2,1)S(1)} %broadcast_in_dim.5), channel_id=1, replica_groups=mesh['x'=4,'zhi'=2,'y'=4,'core'=2,'zp'=2,'zq'=2] {'x','y','zq'}, dimensions={0} | all-to-all | bytes 2097152 | tf_op jit(solution)/shard_map/all_to_all | solution.py:185
  129.2 3.2 %collective-permute-start.14 = (bf16[256,2048]{1,0:T(8,128)(2,1)S(1)}, bf16[256,2048]{1,0:T(8,128)(2,1)S(1)}, u32[]{:S(2)}, u32[]{:S(2)}) collective-permute-start(bf16[256,2048]{1,0:T(8,128)(2,1)S(1)} %bitcast.31), channel_id=1, source_target_pairs={{0,4},{4,0},{1,5},{5,1},{2,6},{6,2},{3,7},{7,3},{8,12},{12,8},{9,1... | collective-permute-start | bytes 3145736 | tf_op jit(solution)/shard_map/ppermute | solution.py:173
  132.4 1.0 fusion.19
  133.4 1.3 collective-permute-done.14
  134.7 2.7 %add_convert_fusion = bf16[768,2048]{1,0:T(8,128)(2,1)} fusion(f32[768,2048]{1,0:T(8,128)S(1)} %fusion.19, bf16[256,768]{1,0:T(8,128)(2,1)S(1)} %collective-permute-done.13, bf16[256,2048]{1,0:T(8,128)(2,1)S(1)} %collective-permute-done.14), kind=kOutput, calls=%fused_computation | convolution fusion | flops 808452096 | bytes 10878976 | tf_op jit(solution)/shard_map/dot_general | solution.py:228
  (23 shorter events, 0.1 us)
Async XLA Ops:
  0.6 13.9 %collective-permute-start.3 = (bf16[768,2048]{1,0:T(8,128)(2,1)}, bf16[768,2048]{1,0:T(8,128)(2,1)S(1)}, u32[]{:S(2)}, u32[]{:S(2)}) collective-permute-start(bf16[768,2048]{1,0:T(8,128)(2,1)} %refs_2_.1), channel_id=1, source_target_pairs={{0,4},{4,0},{1,5},{5,1},{2,6},{6,2},{3,7},{7,3},{8,12},{12,8},{9,1... | collective-permute-start | bytes 9437192 | tf_op jit(solution)/shard_map/ppermute | solution.py:173
  5.4 5.8 %collective-permute-start.2 = (bf16[64,384]{1,0:T(8,128)(2,1)}, bf16[64,384]{1,0:T(8,128)(2,1)}, u32[]{:S(2)}, u32[]{:S(2)}) collective-permute-start(bf16[64,384]{1,0:T(8,128)(2,1)} %pack_peaks.1.packed_ref), channel_id=1, source_target_pairs={{0,1},{1,2},{2,3},{3,0},{4,5},{5,6},{6,7},{7,4},{8,9},{9,10},{10,1... | collective-permute-start | bytes 147464 | tf_op jit(solution)/shard_map/ppermute | solution.py:179
  5.4 7.5 %collective-permute-start.1 = (bf16[64,384]{1,0:T(8,128)(2,1)}, bf16[64,384]{1,0:T(8,128)(2,1)}, u32[]{:S(2)}, u32[]{:S(2)}) collective-permute-start(bf16[64,384]{1,0:T(8,128)(2,1)} %pack_peaks.1.packed_ref), channel_id=1, source_target_pairs={{0,2},{1,3},{2,0},{3,1},{4,6},{5,7},{6,4},{7,5},{8,10},{9,11},{10,... | collective-permute-start | bytes 147464 | tf_op jit(solution)/shard_map/ppermute | solution.py:179
  8.3 6.2 %collective-permute-start = (bf16[64,384]{1,0:T(8,128)(2,1)}, bf16[64,384]{1,0:T(8,128)(2,1)}, u32[]{:S(2)}, u32[]{:S(2)}) collective-permute-start(bf16[64,384]{1,0:T(8,128)(2,1)} %pack_peaks.1.packed_ref), channel_id=1, source_target_pairs={{0,3},{1,0},{2,1},{3,2},{4,7},{5,4},{6,5},{7,6},{8,11},{9,8},{10,9... | collective-permute-start | bytes 147464 | tf_op jit(solution)/shard_map/ppermute | solution.py:179
  9.1 0.8 copy-start.3
  9.9 3.0 %copy-start = (bf16[768,2048]{1,0:T(8,128)(2,1)S(1)}, bf16[768,2048]{1,0:T(8,128)(2,1)}, u32[]{:S(2)}) copy-start(bf16[768,2048]{1,0:T(8,128)(2,1)} %refs_2_.1) | copy-start | bytes 9437188
  16.2 58.2 %copy-start.1 = (bf16[256,768]{1,0:T(8,128)(2,1)}, bf16[256,768]{1,0:T(8,128)(2,1)S(1)}, u32[]{:S(2)}) copy-start(bf16[256,768]{1,0:T(8,128)(2,1)S(1)} %get-tuple-element.24) | copy-start | bytes 1179652
  18.3 31.4 %copy-start.4 = (bf16[2048,768]{1,0:T(8,128)(2,1)S(1)}, bf16[2048,768]{1,0:T(8,128)(2,1)}, u32[]{:S(2)}) copy-start(bf16[2048,768]{1,0:T(8,128)(2,1)} %param.9) | copy-start | bytes 9437188
  18.3 34.7 %copy-start.6 = (f32[2048]{0:T(1024)S(1)}, f32[2048]{0:T(1024)}, u32[]{:S(2)}) copy-start(f32[2048]{0:T(1024)} %param.8) | copy-start | bytes 24580
  42.5 10.5 %collective-permute-start.6 = (bf16[8,2048]{1,0:T(8,128)(2,1)S(1)}, bf16[8,2048]{1,0:T(8,128)(2,1)S(1)}, u32[]{:S(2)}, u32[]{:S(2)}) collective-permute-start(bf16[8,2048]{1,0:T(8,128)(2,1)S(1)} %sum_parts.2), channel_id=1, source_target_pairs={{0,32},{2,34},{32,0},{34,2},{1,33},{3,35},{33,1},{35,3},{4,36},{6,... | collective-permute-start | bytes 98312 | tf_op jit(solution)/shard_map/ppermute | solution.py:179
  47.4 5.6 %collective-permute-start.5 = (bf16[8,2048]{1,0:T(8,128)(2,1)S(1)}, bf16[8,2048]{1,0:T(8,128)(2,1)S(1)}, u32[]{:S(2)}, u32[]{:S(2)}) collective-permute-start(bf16[8,2048]{1,0:T(8,128)(2,1)S(1)} %sum_parts.2), channel_id=1, source_target_pairs={{0,34},{2,0},{32,2},{34,32},{1,35},{3,1},{33,3},{35,33},{4,38},{6,... | collective-permute-start | bytes 98312 | tf_op jit(solution)/shard_map/ppermute | solution.py:179
  47.4 5.6 %collective-permute-start.4 = (bf16[8,2048]{1,0:T(8,128)(2,1)S(1)}, bf16[8,2048]{1,0:T(8,128)(2,1)S(1)}, u32[]{:S(2)}, u32[]{:S(2)}) collective-permute-start(bf16[8,2048]{1,0:T(8,128)(2,1)S(1)} %sum_parts.2), channel_id=1, source_target_pairs={{0,2},{2,32},{32,34},{34,0},{1,3},{3,33},{33,35},{35,1},{4,6},{6,3... | collective-permute-start | bytes 98312 | tf_op jit(solution)/shard_map/ppermute | solution.py:179
  49.7 24.6 %collective-permute-start.7 = (bf16[2048,768]{1,0:T(8,128)(2,1)S(1)}, bf16[2048,768]{1,0:T(8,128)(2,1)S(1)}, u32[]{:S(2)}, u32[]{:S(2)}) collective-permute-start(bf16[2048,768]{1,0:T(8,128)(2,1)S(1)} %copy-done.4), channel_id=1, source_target_pairs={{0,4},{4,0},{1,5},{5,1},{2,6},{6,2},{3,7},{7,3},{8,12},{12,8},{9,1... | collective-permute-start | bytes 9437192 | tf_op jit(solution)/shard_map/ppermute | solution.py:173
  73.3 2.1 %copy-start.5 = (bf16[256,768]{1,0:T(8,128)(2,1)}, bf16[256,768]{1,0:T(8,128)(2,1)S(1)}, u32[]{:S(2)}) copy-start(bf16[256,768]{1,0:T(8,128)(2,1)S(1)} %subtract_convert_fusion) | copy-start | bytes 1179652
  77.5 19.6 %all-to-all-start.2 = ((bf16[32,8,2048]{2,1,0:T(8,128)(2,1)}), bf16[32,8,2048]{2,1,0:T(8,128)(2,1)S(1)}, u32[]{:S(2)}, u32[]{:S(2)}) async-start(bf16[32,8,2048]{2,1,0:T(8,128)(2,1)} %fusion.2), calls=%async_computation.2 | async-start | bytes 2097152 | tf_op jit(solution)/shard_map/all_to_all | solution.py:185
  81.4 23.4 %copy-start.2 = (bf16[256,768]{1,0:T(8,128)(2,1)S(1)}, bf16[256,768]{1,0:T(8,128)(2,1)}, u32[]{:S(2)}) copy-start(bf16[256,768]{1,0:T(8,128)(2,1)} %copy-done.1) | copy-start | bytes 1179652
  81.4 5.7 %collective-permute-start.8 = (bf16[256,2048]{1,0:T(8,128)(2,1)S(1)}, bf16[256,2048]{1,0:T(8,128)(2,1)S(1)}, u32[]{:S(2)}, u32[]{:S(2)}) collective-permute-start(bf16[256,2048]{1,0:T(8,128)(2,1)S(1)} %bitcast.32), channel_id=1, source_target_pairs={{0,4},{4,0},{1,5},{5,1},{2,6},{6,2},{3,7},{7,3},{8,12},{12,8},{9,1... | collective-permute-start | bytes 3145736 | tf_op jit(solution)/shard_map/ppermute | solution.py:173
  84.3 2.8 %collective-permute-start.9 = (bf16[256,768]{1,0:T(8,128)(2,1)S(1)}, bf16[256,768]{1,0:T(8,128)(2,1)S(1)}, u32[]{:S(2)}, u32[]{:S(2)}) collective-permute-start(bf16[256,768]{1,0:T(8,128)(2,1)S(1)} %fusion.7), channel_id=1, source_target_pairs={{0,4},{4,0},{1,5},{5,1},{2,6},{6,2},{3,7},{7,3},{8,12},{12,8},{9,1... | collective-permute-start | bytes 1179656 | tf_op jit(solution)/shard_map/ppermute | solution.py:173
  97.2 11.8 %collective-permute-start.12 = (bf16[8,2048]{1,0:T(8,128)(2,1)S(1)}, bf16[8,2048]{1,0:T(8,128)(2,1)S(1)}, u32[]{:S(2)}, u32[]{:S(2)}) collective-permute-start(bf16[8,2048]{1,0:T(8,128)(2,1)S(1)} %sum_parts.3), channel_id=1, source_target_pairs={{0,32},{2,34},{32,0},{34,2},{1,33},{3,35},{33,1},{35,3},{4,36},{6,... | collective-permute-start | bytes 98312 | tf_op jit(solution)/shard_map/ppermute | solution.py:179
  102.4 6.6 %collective-permute-start.11 = (bf16[8,2048]{1,0:T(8,128)(2,1)S(1)}, bf16[8,2048]{1,0:T(8,128)(2,1)S(1)}, u32[]{:S(2)}, u32[]{:S(2)}) collective-permute-start(bf16[8,2048]{1,0:T(8,128)(2,1)S(1)} %sum_parts.3), channel_id=1, source_target_pairs={{0,34},{2,0},{32,2},{34,32},{1,35},{3,1},{33,3},{35,33},{4,38},{6,... | collective-permute-start | bytes 98312 | tf_op jit(solution)/shard_map/ppermute | solution.py:179
  103.3 5.8 %collective-permute-start.10 = (bf16[8,2048]{1,0:T(8,128)(2,1)S(1)}, bf16[8,2048]{1,0:T(8,128)(2,1)S(1)}, u32[]{:S(2)}, u32[]{:S(2)}) collective-permute-start(bf16[8,2048]{1,0:T(8,128)(2,1)S(1)} %sum_parts.3), channel_id=1, source_target_pairs={{0,2},{2,32},{32,34},{34,0},{1,3},{3,33},{33,35},{35,1},{4,6},{6,3... | collective-permute-start | bytes 98312 | tf_op jit(solution)/shard_map/ppermute | solution.py:179
  104.8 5.6 %collective-permute-start.13 = (bf16[256,768]{1,0:T(8,128)(2,1)S(1)}, bf16[256,768]{1,0:T(8,128)(2,1)S(1)}, u32[]{:S(2)}, u32[]{:S(2)}) collective-permute-start(bf16[256,768]{1,0:T(8,128)(2,1)S(1)} %copy-done.2), channel_id=1, source_target_pairs={{0,4},{4,0},{1,5},{5,1},{2,6},{6,2},{3,7},{7,3},{8,12},{12,8},{9,1... | collective-permute-start | bytes 1179656 | tf_op jit(solution)/shard_map/ppermute | solution.py:173
  129.2 5.4 %collective-permute-start.14 = (bf16[256,2048]{1,0:T(8,128)(2,1)S(1)}, bf16[256,2048]{1,0:T(8,128)(2,1)S(1)}, u32[]{:S(2)}, u32[]{:S(2)}) collective-permute-start(bf16[256,2048]{1,0:T(8,128)(2,1)S(1)} %bitcast.31), channel_id=1, source_target_pairs={{0,4},{4,0},{1,5},{5,1},{2,6},{6,2},{3,7},{7,3},{8,12},{12,8},{9,1... | collective-permute-start | bytes 3145736 | tf_op jit(solution)/shard_map/ppermute | solution.py:173
